TPU v7x, 32 devices: a whole 2x2x4 slice. The times are simulated.
32 devices in a mesh: shard: 4 (over y, x), replica: 8 (over z, core).
Axes of the slice: x: 2, y: 2, z: 4, core: 2. Of those that a mesh axis runs over, the one named last changes fastest.
Arguments:
- tokens: bfloat16 [8192, 768], P(('shard', 'replica')), may hold values from -6 to 6
- cond: bfloat16 [32, 768], P(('shard', 'replica')), may hold values from -6 to 6
- cot: bfloat16 [8192, 768], P(('shard', 'replica')), may hold values from -6 to 6
- w_mod: bfloat16 [768, 4608], P('shard'), may hold values from -0.21875 to 0.21875
- b_mod: bfloat16 [4608], P('shard'), may hold values from -2.5 to 2.5
- w_qkv: bfloat16 [768, 2304], P('shard'), may hold values from -0.21875 to 0.21875
- b_qv: bfloat16 [1536], P('shard'), may hold values from -2.5 to 2.5
- w_out: bfloat16 [768, 768], P('shard'), may hold values from -0.875 to 0.875
- b_out: bfloat16 [768], P('shard'), may hold values from -2.5 to 2.5
- w_fc1: bfloat16 [768, 3072], P('shard'), may hold values from -0.21875 to 0.21875
- b_fc1: bfloat16 [3072], P('shard'), may hold values from -2.5 to 2.5
- w_fc2: bfloat16 [3072, 768], P('shard'), may hold values from -0.109375 to 0.109375
- b_fc2: bfloat16 [768], P('shard'), may hold values from -2.5 to 2.5
Outputs:
- mixed: bfloat16 [8192, 768], P(('shard', 'replica'))
- grad_tokens: float32 [8192, 768], P(('shard', 'replica'))
- grad_cond: float32 [32, 768], P(('shard', 'replica'))
- grad_w_mod: float32 [768, 4608], P('shard')
- grad_b_mod: float32 [4608], P('shard')
- grad_w_qkv: float32 [768, 2304], P('shard')
- grad_b_qv: float32 [1536], P('shard')
- grad_w_out: float32 [768, 768], P('shard')
- grad_b_out: float32 [768], P('shard')
- grad_w_fc1: float32 [768, 3072], P('shard')
- grad_b_fc1: float32 [3072], P('shard')
- grad_w_fc2: float32 [3072, 768], P('shard')
- grad_b_fc2: float32 [768], P('shard')
All inputs are finite; a program needn't handle non-finite values.
Results may differ from a plain program's by a relative error of at most 0.015.
The roundings to bfloat16 on the way count: a program that leaves them out, or rounds other values in their place, can miss the bound.
Values may be sent and summed in bfloat16 or wider, within the bound.
No kernel may reach another device: no remote copies, remote signals or barrier semaphores. Data moves between devices by JAX's collectives and lax.ppermute only.
A program may use at most 192 MiB of HBM per device.

v0:
```python
import functools

import jax
import jax.numpy as jnp
from jax import lax
from jax.experimental import pallas as pl
from jax.experimental.pallas import tpu as pltpu
from jax.sharding import PartitionSpec as P

F32 = jnp.float32
BF16 = jnp.bfloat16
HEAD = 64
CHUNK = 512


def dot_nn(left, right):
    return lax.dot_general(left, right, (((1,), (0,)), ((), ())), preferred_element_type=F32)


def dot_tn(left, right):
    return lax.dot_general(left, right, (((0,), (0,)), ((), ())), preferred_element_type=F32)


def dot_nt(left, right):
    return lax.dot_general(left, right, (((1,), (1,)), ((), ())), preferred_element_type=F32)


def layer_norm(values):
    center = values - jnp.mean(values, -1, keepdims=True)
    rstd_val = lax.rsqrt(jnp.mean(center * center, -1, keepdims=True) + 1e-06)
    return (center * rstd_val, rstd_val)


def norm_back(grad_norm, normed, rstd_val):
    return rstd_val * (
        grad_norm
        - jnp.mean(grad_norm, -1, keepdims=True)
        - normed * jnp.mean(grad_norm * normed, -1, keepdims=True)
    )


def hop(value, axis, size, flip):
    return lax.ppermute(value, axis, [(at, at ^ flip) for at in range(size)])


def bits_of(number):
    return [1 << at for at in range(number.bit_length()) if number >> at & 1]


def by_weight(count):
    return sorted(range(1, count), key=lambda number: (bin(number).count("1"), number))


def xor_rows(rows, place):
    count = rows.shape[0]
    flip = 1
    while flip < count:
        swapped = rows.reshape(count // (2 * flip), 2, flip, -1)[:, ::-1].reshape(rows.shape)
        rows = jnp.where((place & flip) != 0, swapped, rows)
        flip *= 2
    return rows


def piece_layout(shards, width):
    layout = []
    for number in by_weight(shards):
        ways = len(bits_of(number))
        part = width // ways
        layout += [(number, at * part, part) for at in range(ways)]
    return layout


def gather_weight(half, shards, replicas, first):
    width = half.shape[1]
    mine = {0: half}
    pieces = []
    for number in by_weight(shards):
        ways = bits_of(number)
        part = width // len(ways)
        got = []
        for at, flip in enumerate(ways):
            source = mine[number ^ flip]
            if len(ways) > 1:
                source = source[:, at * part : (at + 1) * part]
            got.append(hop(source, "shard", shards, flip))
        mine[number] = got[0] if len(got) == 1 else jnp.concatenate(got, 1)
        pieces += got
        if len(ways) == 1:
            first.append(got[0])
    return pieces + [hop(piece, "replica", replicas, 1) for piece in pieces]


def reduce_grad(keep, send, shards, replicas):
    came = [hop(piece, "replica", replicas, 1) for piece in send]
    parts = [mine.astype(F32) + other.astype(F32) for mine, other in zip(keep, came)]
    width = parts[0].shape[1]
    for number in reversed(by_weight(shards)):
        ways = bits_of(number)
        part = width // len(ways)
        for at, flip in enumerate(ways):
            target = number ^ flip
            if len(ways) == 1:
                sent = parts[number].astype(BF16)
                parts[target] = parts[target] + hop(sent, "shard", shards, flip).astype(F32)
            else:
                low, high = at * part, (at + 1) * part
                sent = parts[number][:, low:high].astype(BF16)
                got = hop(sent, "shard", shards, flip).astype(F32)
                old = parts[target]
                parts[target] = jnp.concatenate(
                    [old[:, :low], old[:, low:high] + got, old[:, high:]], 1
                )
    value = parts[0]
    chips = replicas // 2
    chip = lax.axis_index("replica") // 2
    span = width // chips
    total = lax.dynamic_slice_in_dim(value, chip * span, span, 1)
    for flip in range(1, chips):
        sent = lax.dynamic_slice_in_dim(value, (chip ^ flip) * span, span, 1).astype(BF16)
        total = total + hop(sent, "replica", replicas, 2 * flip).astype(F32)
    total = total.astype(BF16)
    cols = [total] + [hop(total, "replica", replicas, 2 * flip) for flip in range(1, chips)]
    stack = jnp.stack(cols, 0)
    whole = xor_blocks(stack, chip)
    whole = whole.transpose(1, 0, 2).reshape(value.shape)
    other = hop(whole, "replica", replicas, 1)
    core = lax.axis_index("replica") % 2
    both = jnp.where(
        core == 1, jnp.concatenate([other, whole], 0), jnp.concatenate([whole, other], 0)
    )
    return both.astype(F32)


def xor_blocks(stack, place):
    count = stack.shape[0]
    flip = 1
    while flip < count:
        swapped = stack.reshape((count // (2 * flip), 2, flip) + stack.shape[1:])[:, ::-1]
        stack = jnp.where((place & flip) != 0, swapped.reshape(stack.shape), stack)
        flip *= 2
    return stack


def start_fetch(own, pieces, whole, sems, shards):
    place = lax.axis_index("shard")
    core = lax.axis_index("replica") % 2
    total_rows, width = whole.shape
    block = total_rows // shards
    half = block // 2
    copies = []

    def add(source, row, low, cols):
        rows = source.shape[0]
        there = whole.at[pl.ds(pl.multiple_of(row, 16), rows), pl.ds(low, cols)]
        copy = pltpu.make_async_copy(source, there, sems.at[len(copies)])
        copy.start()
        copies.append(copy)

    low = 0
    for part in own:
        cols = part.shape[1]
        add(part, place * block, low, cols)
        low += cols
    layout = piece_layout(shards, width)
    for at, (number, first, cols) in enumerate(layout):
        for side, source in ((core, pieces[at]), (1 - core, pieces[len(layout) + at])):
            add(source, (place ^ number) * block + side * half, first, cols)
    return copies


def fetch_count(shards, own):
    return own + 2 * len(piece_layout(shards, 1 << 20))


def start_emit(grad, keep, send, sems, shards):
    place = lax.axis_index("shard")
    core = lax.axis_index("replica") % 2
    block = grad.shape[0] // shards
    half = block // 2
    copies = []
    for number in range(shards):
        for side, target in ((core, keep[number]), (1 - core, send[number])):
            row = pl.multiple_of((place ^ number) * block + side * half, 16)
            copy = pltpu.make_async_copy(
                grad.at[pl.ds(row, half), :], target, sems.at[len(copies)]
            )
            copy.start()
            copies.append(copy)
    return copies


def wait_all(copies):
    for copy in copies:
        copy.wait()


def mod_piece(mod, at, width):
    return mod[:, at * width : (at + 1) * width]


def take(refs, count):
    head = refs[:count]
    del refs[:count]
    return head


def gelu_parts(pre):
    scale = 0.7978845608028654
    square = pre * pre
    inner = jnp.tanh(scale * (pre + 0.044715 * (square * pre)))
    value = 0.5 * pre * (1.0 + inner)
    slope = 0.5 * (1.0 + inner) + 0.5 * pre * (1.0 - inner * inner) * (
        scale * (1.0 + 0.134145 * square)
    )
    return value, slope


def attend_kernel(shards, *refs):
    refs = list(refs)
    tokens, mod, bias_qv, bias_out = take(refs, 4)
    own = take(refs, 2)
    pieces = take(refs, 2 * len(piece_layout(shards, 1 << 20)))
    modul_a, qkv, attended, lse, branch_a, middle, modul_b = take(refs, 7)
    weight, sems = refs
    rows, width = tokens.shape
    copies = start_fetch(own, pieces, weight, sems, shards)
    inputs = tokens[...].astype(F32)
    norm_a, _ = layer_norm(inputs)
    mod_val = mod[...]
    modul = (norm_a * (1.0 + mod_piece(mod_val, 1, width)) + mod_piece(mod_val, 0, width)).astype(
        BF16
    )
    modul_a[...] = modul
    wait_all(copies)
    for at in range(3):
        projected = dot_nn(modul, weight[:, at * width : (at + 1) * width])
        if at != 1:
            low = 0 if at == 0 else width
            projected = projected + bias_qv[:, low : low + width]
        qkv[:, at * width : (at + 1) * width] = projected.astype(BF16)
    lane = lax.broadcasted_iota(jnp.int32, (rows, 2 * HEAD), 1)

    def pair(at, lse_all):
        col = pl.multiple_of(at * 2 * HEAD, 2 * HEAD)
        query = qkv[:, pl.ds(col, 2 * HEAD)]
        key = qkv[:, pl.ds(width + col, 2 * HEAD)]
        value = qkv[:, pl.ds(2 * width + col, 2 * HEAD)]
        out = jnp.zeros((rows, 2 * HEAD), F32)
        for side in range(2):
            mask = (lane < HEAD) if side == 0 else (lane >= HEAD)
            scores = dot_nt(jnp.where(mask, query, 0), key) * 0.125
            top = jnp.max(scores, -1, keepdims=True)
            exps = jnp.exp(scores - top)
            total = jnp.sum(exps, -1, keepdims=True)
            probs = (exps / total).astype(BF16)
            out = out + dot_nn(probs, jnp.where(mask, value, 0))
            lse_all = jnp.where(lane == 2 * at + side, top + jnp.log(total), lse_all)
        attended[:, pl.ds(col, 2 * HEAD)] = out.astype(BF16)
        return lse_all

    lse[...] = lax.fori_loop(
        0, width // (2 * HEAD), pair, jnp.zeros((rows, 2 * HEAD), F32)
    )
    branch = dot_nn(attended[...], weight[:, 3 * width :]) + bias_out[...]
    branch_a[...] = branch
    mid = inputs + mod_piece(mod_val, 2, width) * branch
    middle[...] = mid
    norm_b, _ = layer_norm(mid)
    modul_b[...] = (
        norm_b * (1.0 + mod_piece(mod_val, 4, width)) + mod_piece(mod_val, 3, width)
    ).astype(BF16)


def hidden_kernel(shards, *refs):
    refs = list(refs)
    modul_b, cot, mod, bias_fc1 = take(refs, 4)
    own = take(refs, 1)
    pieces = take(refs, 2 * len(piece_layout(shards, 1 << 20)))
    hidden, slope = take(refs, 2)
    keep = take(refs, shards)
    send = take(refs, shards)
    weight, grad, sems, out_sems = refs
    rows, width = modul_b.shape
    copies = start_fetch(own, pieces, weight, sems, shards)
    low_branch = (cot[...].astype(F32) * mod_piece(mod[...], 5, width)).astype(BF16)
    modul = modul_b[...]
    wait_all(copies)

    def chunk(at, carry):
        col = pl.multiple_of(at * CHUNK, CHUNK)
        pre = dot_nn(modul, weight[:, pl.ds(col, CHUNK)]) + bias_fc1[:, pl.ds(col, CHUNK)]
        value, rate = gelu_parts(pre)
        value = value.astype(BF16)
        hidden[:, pl.ds(col, CHUNK)] = value
        slope[:, pl.ds(col, CHUNK)] = rate
        grad[pl.ds(col, CHUNK), :] = dot_tn(value, low_branch).astype(BF16)
        return carry

    lax.fori_loop(0, weight.shape[1] // CHUNK, chunk, 0)
    wait_all(start_emit(grad, keep, send, out_sems, shards))


def pre_kernel(shards, *refs):
    refs = list(refs)
    modul_b, cot, mod, slope = take(refs, 4)
    own = take(refs, 1)
    pieces = take(refs, 2 * len(piece_layout(shards, 1 << 20)))
    low_pre, sum_pre = take(refs, 2)
    keep = take(refs, shards)
    send = take(refs, shards)
    weight, grad, turned, sems, out_sems = refs
    rows, width = modul_b.shape
    copies = start_fetch(own, pieces, weight, sems, shards)
    low_branch = (cot[...].astype(F32) * mod_piece(mod[...], 5, width)).astype(BF16)
    turned[...] = modul_b[...].T
    wait_all(copies)

    def chunk(at, carry):
        col = pl.multiple_of(at * CHUNK, CHUNK)
        grad_pre = dot_nt(low_branch, weight[pl.ds(col, CHUNK), :]) * slope[:, pl.ds(col, CHUNK)]
        sum_pre[:, pl.ds(col, CHUNK)] = jnp.sum(grad_pre, 0, keepdims=True)
        low = grad_pre.astype(BF16)
        low_pre[:, pl.ds(col, CHUNK)] = low
        grad[:, pl.ds(col, CHUNK)] = dot_nn(turned[...], low).astype(BF16)
        return carry

    lax.fori_loop(0, weight.shape[0] // CHUNK, chunk, 0)
    wait_all(start_emit(grad, keep, send, out_sems, shards))


def back_kernel(shards, *refs):
    refs = list(refs)
    low_pre, cot, mod, middle, branch_a, modul_a, qkv, attended, lse = take(refs, 9)
    own_fc1 = take(refs, 1)
    pieces_fc1 = take(refs, 2 * len(piece_layout(shards, 1 << 20)))
    own_qkvo = take(refs, 2)
    pieces_qkvo = take(refs, 2 * len(piece_layout(shards, 1 << 20)))
    grad_middle, low_proj, sum_proj, sum_out, grad_mods = take(refs, 5)
    keep = take(refs, shards)
    send = take(refs, shards)
    w_fc1, w_qkvo, grad, grad_att, turned, sems_fc1, sems_qkvo, out_sems = refs
    rows, width = middle.shape
    copies_fc1 = start_fetch(own_fc1, pieces_fc1, w_fc1, sems_fc1, shards)
    copies_qkvo = start_fetch(own_qkvo, pieces_qkvo, w_qkvo, sems_qkvo, shards)
    mod_val = mod[...]
    norm_b, rstd_b = layer_norm(middle[...])
    wait_all(copies_fc1)
    grad_modul = dot_nt(low_pre[...], w_fc1[...])
    grad_mods[0:1, :] = jnp.sum(grad_modul, 0, keepdims=True)
    grad_mods[1:2, :] = jnp.sum(grad_modul * norm_b, 0, keepdims=True)
    grad_mid = cot[...].astype(F32) + norm_back(
        grad_modul * (1.0 + mod_piece(mod_val, 4, width)), norm_b, rstd_b
    )
    grad_middle[...] = grad_mid
    grad_mods[2:3, :] = jnp.sum(grad_mid * branch_a[...], 0, keepdims=True)
    grad_branch = grad_mid * mod_piece(mod_val, 2, width)
    sum_out[...] = jnp.sum(grad_branch, 0, keepdims=True)
    low_branch = grad_branch.astype(BF16)
    wait_all(copies_qkvo)
    grad_att[...] = dot_nt(low_branch, w_qkvo[:, 3 * width :]).astype(BF16)
    turned[...] = attended[...].T
    grad[:, 3 * width :] = dot_nn(turned[...], low_branch).astype(BF16)
    turned[...] = modul_a[...].T
    lane = lax.broadcasted_iota(jnp.int32, (rows, 2 * HEAD), 1)
    lse_val = lse[...]

    def pair(at, carry):
        col = pl.multiple_of(at * 2 * HEAD, 2 * HEAD)
        query = qkv[:, pl.ds(col, 2 * HEAD)]
        key = qkv[:, pl.ds(width + col, 2 * HEAD)]
        value = qkv[:, pl.ds(2 * width + col, 2 * HEAD)]
        grad_out = grad_att[:, pl.ds(col, 2 * HEAD)]
        product = grad_out.astype(F32) * attended[:, pl.ds(col, 2 * HEAD)].astype(F32)
        grad_q = jnp.zeros((rows, 2 * HEAD), F32)
        grad_k = jnp.zeros((rows, 2 * HEAD), F32)
        grad_v = jnp.zeros((rows, 2 * HEAD), F32)
        for side in range(2):
            mask = (lane < HEAD) if side == 0 else (lane >= HEAD)
            query_m = jnp.where(mask, query, 0)
            grad_m = jnp.where(mask, grad_out, 0)
            scores = dot_nt(query_m, key) * 0.125
            log_total = jnp.sum(
                jnp.where(lane == 2 * at + side, lse_val, 0.0), -1, keepdims=True
            )
            probs = jnp.exp(scores - log_total)
            delta = jnp.sum(jnp.where(mask, product, 0.0), -1, keepdims=True)
            grad_scores = (probs * (dot_nt(grad_m, value) - delta) * 0.125).astype(BF16)
            grad_v = grad_v + dot_tn(probs.astype(BF16), grad_m)
            grad_q = grad_q + dot_nn(grad_scores, jnp.where(mask, key, 0))
            grad_k = grad_k + dot_tn(grad_scores, query_m)
        for part, piece in enumerate((grad_q, grad_k, grad_v)):
            there = pl.multiple_of(part * width + col, 2 * HEAD)
            sum_proj[:, pl.ds(there, 2 * HEAD)] = jnp.sum(piece, 0, keepdims=True)
            low = piece.astype(BF16)
            low_proj[:, pl.ds(there, 2 * HEAD)] = low
        return carry

    lax.fori_loop(0, width // (2 * HEAD), pair, 0)

    def chunk(at, carry):
        col = pl.multiple_of(at * width, width)
        grad[:, pl.ds(col, width)] = dot_nn(turned[...], low_proj[:, pl.ds(col, width)]).astype(
            BF16
        )
        return carry

    lax.fori_loop(0, 3, chunk, 0)
    wait_all(start_emit(grad, keep, send, out_sems, shards))


def last_kernel(shards, *refs):
    refs = list(refs)
    low_proj, tokens, mod, grad_middle, hidden, middle, cot, bias_fc2 = take(refs, 8)
    own_qkvo = take(refs, 2)
    pieces_qkvo = take(refs, 2 * len(piece_layout(shards, 1 << 20)))
    own_fc2 = take(refs, 1)
    pieces_fc2 = take(refs, 2 * len(piece_layout(shards, 1 << 20)))
    grad_tokens, mixed, sum_fc2, grad_mods = take(refs, 4)
    w_qkvo, w_fc2, sems_qkvo, sems_fc2 = refs
    rows, width = tokens.shape
    copies_qkvo = start_fetch(own_qkvo, pieces_qkvo, w_qkvo, sems_qkvo, shards)
    copies_fc2 = start_fetch(own_fc2, pieces_fc2, w_fc2, sems_fc2, shards)
    mod_val = mod[...]
    norm_a, rstd_a = layer_norm(tokens[...].astype(F32))
    wait_all(copies_qkvo)
    grad_modul = dot_nt(low_proj[...], w_qkvo[:, : 3 * width])
    grad_mods[0:1, :] = jnp.sum(grad_modul, 0, keepdims=True)
    grad_mods[1:2, :] = jnp.sum(grad_modul * norm_a, 0, keepdims=True)
    grad_tokens[...] = grad_middle[...] + norm_back(
        grad_modul * (1.0 + mod_piece(mod_val, 1, width)), norm_a, rstd_a
    )
    wait_all(copies_fc2)
    branch_b = dot_nn(hidden[...], w_fc2[...]) + bias_fc2[...]
    gate_b = mod_piece(mod_val, 5, width)
    grad_out = cot[...].astype(F32)
    mixed[...] = (middle[...] + gate_b * branch_b).astype(BF16)
    grad_mods[2:3, :] = jnp.sum(grad_out * branch_b, 0, keepdims=True)
    sum_fc2[...] = jnp.sum(grad_out * gate_b, 0, keepdims=True)


def call(kernel, shards, inside, outside, outs, outside_outs, scratch, flops):
    vmem = pl.BlockSpec(memory_space=pltpu.VMEM)
    anywhere = pl.BlockSpec(memory_space=pl.ANY)
    moved = sum(value.size * value.dtype.itemsize for value in inside + outside)
    moved += sum(value.size * value.dtype.itemsize for value in outs + outside_outs)
    return pl.pallas_call(
        functools.partial(kernel, shards),
        out_shape=outs + outside_outs,
        in_specs=[vmem] * len(inside) + [anywhere] * len(outside),
        out_specs=[vmem] * len(outs) + [anywhere] * len(outside_outs),
        scratch_shapes=scratch,
        cost_estimate=pl.CostEstimate(flops=flops, bytes_accessed=moved, transcendentals=0),
        compiler_params=pltpu.CompilerParams(vmem_limit_bytes=56 << 20),
    )(*inside, *outside)


def shape(dims, dtype):
    return jax.ShapeDtypeStruct(dims, dtype)


def body(
    shards,
    replicas,
    tokens,
    cond,
    cot,
    w_mod,
    b_mod,
    w_qkv,
    b_qv,
    w_out,
    b_out,
    w_fc1,
    b_fc1,
    w_fc2,
    b_fc2,
):
    place = lax.axis_index("shard")
    core = lax.axis_index("replica") % 2
    rows, width = tokens.shape
    mod_rows = w_mod.shape[0]
    inner = w_fc1.shape[1]

    cond_f = cond.astype(F32)
    cond_act = jax.nn.silu(cond_f).astype(BF16)
    biases = [b_qv, b_out, b_fc1, b_fc2]
    note = jnp.concatenate([cond_act[0]] + biases)[None]
    notes = jnp.concatenate(
        [note] + [hop(note, "shard", shards, number) for number in range(1, shards)], 0
    )
    group_cols = lax.dynamic_slice_in_dim(notes[:, :width], place * mod_rows, mod_rows, 1)
    bias_rows = xor_rows(notes[:, width:].astype(F32), place)
    full_bias = []
    start = 0
    for piece in biases:
        full_bias.append(bias_rows[:, start : start + piece.shape[0]].reshape(1, -1))
        start += piece.shape[0]
    bias_qv, bias_out, bias_fc1, bias_fc2 = full_bias

    partial = dot_nn(group_cols, w_mod)
    own_bias = lax.dynamic_update_slice(
        jnp.zeros((6 * width,), F32), b_mod.astype(F32), (place * b_mod.shape[0],)
    )
    partial = partial + own_bias
    mod = partial[0:1]
    for number in range(1, shards):
        mod = mod + hop(partial[number : number + 1], "shard", shards, number)

    def halved(weight):
        half = weight.shape[0] // 2
        return lax.dynamic_slice_in_dim(weight, core * half, half, 0)

    first = []
    half_qkvo = jnp.concatenate([halved(w_qkv), halved(w_out)], 1)
    pieces_qkvo = gather_weight(half_qkvo, shards, replicas, first)
    tied = lax.optimization_barrier((w_fc1, *first))
    first = []
    pieces_fc1 = gather_weight(halved(tied[0]), shards, replicas, first)
    tied = lax.optimization_barrier((w_fc2, *first))
    pieces_fc2 = gather_weight(halved(tied[0]), shards, replicas, [])

    pieces = len(piece_layout(shards, 1 << 20)) * 2
    sems = pltpu.SemaphoreType.DMA
    qkvo_scratch = [pltpu.VMEM((width, 4 * width), BF16)]
    fc1_scratch = [pltpu.VMEM((width, inner), BF16)]
    fc2_scratch = [pltpu.VMEM((inner, width), BF16)]
    out_sems = [sems((2 * shards,))]
    half = mod_rows // 2
    half_inner = w_fc2.shape[0] // 2

    modul_a, qkv, attended, lse, branch_a, middle, modul_b = call(
        attend_kernel,
        shards,
        [tokens, mod, bias_qv, bias_out],
        [w_qkv, w_out] + pieces_qkvo,
        [
            shape((rows, width), BF16),
            shape((rows, 3 * width), BF16),
            shape((rows, width), BF16),
            shape((rows, 2 * HEAD), F32),
            shape((rows, width), F32),
            shape((rows, width), F32),
            shape((rows, width), BF16),
        ],
        [],
        qkvo_scratch + [sems((pieces + 2,))],
        10**10,
    )
    hidden, slope, *parts = call(
        hidden_kernel,
        shards,
        [modul_b, cot, mod, bias_fc1],
        [w_fc1] + pieces_fc1,
        [shape((rows, inner), BF16), shape((rows, inner), F32)],
        [shape((half_inner, width), BF16)] * (2 * shards),
        fc1_scratch + fc2_scratch + [sems((pieces + 1,))] + out_sems,
        10**10,
    )
    total_fc2 = reduce_grad(parts[:shards], parts[shards:], shards, replicas)
    low_pre, sum_pre, *parts = call(
        pre_kernel,
        shards,
        [modul_b, cot, mod, slope],
        [w_fc2] + pieces_fc2,
        [shape((rows, inner), BF16), shape((1, inner), F32)],
        [shape((half, inner), BF16)] * (2 * shards),
        fc2_scratch + fc1_scratch + [pltpu.VMEM((width, rows), BF16), sems((pieces + 1,))]
        + out_sems,
        10**10,
    )
    total_fc1 = reduce_grad(parts[:shards], parts[shards:], shards, replicas)
    grad_middle, low_proj, sum_proj, sum_out, mods_b, *parts = call(
        back_kernel,
        shards,
        [low_pre, cot, mod, middle, branch_a, modul_a, qkv, attended, lse],
        [w_fc1] + pieces_fc1 + [w_qkv, w_out] + pieces_qkvo,
        [
            shape((rows, width), F32),
            shape((rows, 3 * width), BF16),
            shape((1, 3 * width), F32),
            shape((1, width), F32),
            shape((3, width), F32),
        ],
        [shape((half, 4 * width), BF16)] * (2 * shards),
        fc1_scratch
        + qkvo_scratch
        + qkvo_scratch
        + [pltpu.VMEM((rows, width), BF16), pltpu.VMEM((width, rows), BF16)]
        + [sems((pieces + 1,)), sems((pieces + 2,))]
        + out_sems,
        10**10,
    )
    total_qkvo = reduce_grad(parts[:shards], parts[shards:], shards, replicas)
    grad_tokens, mixed, sum_fc2, mods_a = call(
        last_kernel,
        shards,
        [low_proj, tokens, mod, grad_middle, hidden, middle, cot, bias_fc2],
        [w_qkv, w_out] + pieces_qkvo + [w_fc2] + pieces_fc2,
        [
            shape((rows, width), F32),
            shape((rows, width), BF16),
            shape((1, width), F32),
            shape((3, width), F32),
        ],
        [],
        qkvo_scratch + fc2_scratch + [sems((pieces + 2,)), sems((pieces + 1,))],
        10**10,
    )
    grad_modulation = jnp.concatenate(
        [mods_a[0], mods_a[1], mods_b[2], mods_b[0], mods_b[1], mods_a[2]]
    )

    bias_grads = [
        jnp.concatenate([sum_proj[0, :width], sum_proj[0, 2 * width :]]),
        sum_out[0],
        sum_pre[0],
        sum_fc2[0],
    ]
    owned = jnp.concatenate([piece.reshape(shards, -1) for piece in bias_grads], 1).astype(BF16)
    own_span = owned.shape[1]
    mod_span = 6 * width
    news = jnp.concatenate([grad_modulation.astype(BF16), owned.reshape(-1)])[None]
    group_news = jnp.concatenate(
        [news] + [hop(news, "shard", shards, number) for number in range(1, shards)], 0
    )
    group_mod = group_news[:, :mod_span]
    own_bias_part = jnp.sum(
        lax.dynamic_slice_in_dim(group_news, mod_span + place * own_span, own_span, 1).astype(F32),
        0,
    )
    back_rows = dot_nt(group_mod, w_mod)
    came_rows = [back_rows[0:1]]
    for number in range(1, shards):
        came_rows.append(hop(back_rows[number : number + 1], "shard", shards, number))
    grad_cond_act = xor_rows(jnp.concatenate(came_rows, 0), place).reshape(1, width)
    _, silu_back = jax.vjp(jax.nn.silu, cond_f)
    grad_cond = silu_back(grad_cond_act)[0]

    share = jnp.concatenate(
        [
            jnp.concatenate([group_mod, group_cols], 1).reshape(1, -1),
            own_bias_part.astype(BF16)[None],
        ],
        1,
    )
    flip = 1
    while flip < replicas:
        share = jnp.concatenate([share, hop(share, "replica", replicas, flip)], 0)
        flip *= 2
    mod_part = share[:, : shards * (mod_span + mod_rows)].reshape(-1, mod_span + mod_rows)
    all_mod = mod_part[:, :mod_span]
    all_cols = mod_part[:, mod_span:]
    total_mod = dot_tn(all_cols, all_mod)
    own_mod = lax.dynamic_slice_in_dim(all_mod, place * b_mod.shape[0], b_mod.shape[0], 1)
    total_b_mod = jnp.sum(own_mod.astype(F32), 0)
    bias_sum = jnp.sum(share[:, shards * (mod_span + mod_rows) :].astype(F32), 0)
    bias_totals = []
    start = 0
    for piece in biases:
        bias_totals.append(bias_sum[start : start + piece.shape[0]])
        start += piece.shape[0]
    return (
        mixed,
        grad_tokens,
        grad_cond,
        total_mod,
        total_b_mod,
        total_qkvo[:, : 3 * width],
        bias_totals[0],
        total_qkvo[:, 3 * width :],
        bias_totals[1],
        total_fc1,
        bias_totals[2],
        total_fc2,
        bias_totals[3],
    )


def solution(mesh):
    shards = mesh.shape["shard"]
    replicas = mesh.shape["replica"]
    both = P(("shard", "replica"), None)
    pairs = (P("shard", None), P("shard")) * 5

    def run(*args):
        return body(shards, replicas, *args)

    return jax.shard_map(
        run,
        mesh=mesh,
        in_specs=(both, both, both) + pairs,
        out_specs=(both, both, both) + pairs,
        check_vma=False,
    )
```

profile of v0, /device:TPU:0, one launch (start us, length us, event | category | flops | bytes accessed | tf_op | source)
XLA Modules:
  0.0 374.5 jit_solution(16334359705679054253)
XLA Ops:
  2.9 3.0 collective-permute-start.7
  8.8 2.9 collective-permute-start.2
  11.9 9.1 %collective-permute-done = bf16[1,2304]{1,0:T(2,128)(2,1)S(1)} collective-permute-done((bf16[1,2304]{1,0:T(2,128)(2,1)S(1)}, bf16[1,2304]{1,0:T(2,128)(2,1)S(1)}, u32[]{:S(2)}, u32[]{:S(2)}) %collective-permute-start) | collective-permute-done | bytes 4640 | tf_op jit(solution)/shard_map/ppermute | solution.py:43
  30.1 10.1 %collective-permute-done.15.refs_6_.refs_11_ = bf16[96,3072]{1,0:T(8,128)(2,1)} collective-permute-done((bf16[96,3072]{1,0:T(8,128)(2,1)S(1)}, bf16[96,3072]{1,0:T(8,128)(2,1)}, u32[]{:S(2)}, u32[]{:S(2)}) %collective-permute-start.15) | collective-permute-done | bytes 589856 | tf_op jit(solution)/shard_map/ppermute | solution.py:43
  55.4 6.0 %collective-permute-done.9.refs_9_.refs_23_.refs_13_ = bf16[96,1536]{1,0:T(8,128)(2,1)} collective-permute-done((bf16[96,1536]{1,0:T(8,128)(2,1)S(1)}, bf16[96,1536]{1,0:T(8,128)(2,1)}, u32[]{:S(2)}, u32[]{:S(2)}) %collective-permute-start.9) | collective-permute-done | bytes 294944 | tf_op jit(solution)/shard_map/ppermute | solution.py:43
  61.9 4.4 %collective-permute-done.16.refs_7_.refs_12_ = bf16[96,1536]{1,0:T(8,128)(2,1)} collective-permute-done((bf16[96,1536]{1,0:T(8,128)(2,1)S(1)}, bf16[96,1536]{1,0:T(8,128)(2,1)}, u32[]{:S(2)}, u32[]{:S(2)}) %collective-permute-start.16) | collective-permute-done | bytes 294944 | tf_op jit(solution)/shard_map/ppermute | solution.py:43
  70.8 5.0 %collective-permute-done.17.refs_8_.refs_13_ = bf16[96,1536]{1,0:T(8,128)(2,1)S(1)} collective-permute-done((bf16[96,1536]{1,0:T(8,128)(2,1)S(1)}, bf16[96,1536]{1,0:T(8,128)(2,1)S(1)}, u32[]{:S(2)}, u32[]{:S(2)}) %collective-permute-start.17) | collective-permute-done | bytes 294944 | tf_op jit(solution)/shard_map/ppermute | solution.py:43
  78.1 9.8 %shard_map.228 = (bf16[256,768]{1,0:T(8,128)(2,1)}, bf16[256,2304]{1,0:T(8,128)(2,1)}, bf16[256,768]{1,0:T(8,128)(2,1)}, f32[256,128]{1,0:T(8,128)}, f32[256,768...) custom-call(bf16[256,768]{1,0:T(8,128)(2,1)} %refs_1_.7, f32[1,4608]{1,0:T(1,128)} %fusion.13.refs_1_.refs_2_, ...), custom_call_target="tpu_custom_call" | custom-call | flops 10000000000 | bytes 9202688 | tf_op jit(solution)/shard_map/pallas_call | solution.py:446
  89.9 13.9 %shard_map.229 = (bf16[256,3072]{1,0:T(8,128)(2,1)}, f32[256,3072]{1,0:T(8,128)}, bf16[384,768]{1,0:T(8,128)(2,1)}, bf16[384,768]{1,0:T(8,128)(2,1)}, bf16[384,7...) custom-call(bf16[256,768]{1,0:T(8,128)(2,1)} %get-tuple-element.59.r, ...), custom_call_target="tpu_custom_call" | custom-call | flops 10000000000 | bytes 14972928 | tf_op jit(solution)/shard_map/pallas_call | solution.py:446
  105.8 12.3 %shard_map.230 = (bf16[256,3072]{1,0:T(8,128)(2,1)}, f32[1,3072]{1,0:T(1,128)}, bf16[96,3072]{1,0:T(8,128)(2,1)}, bf16[96,3072]{1,0:T(8,128)(2,1)}, bf16[96,3072...) custom-call(bf16[256,768]{1,0:T(8,128)(2,1)} %get-tuple-element.59.r, ...), custom_call_target="tpu_custom_call" | custom-call | flops 10000000000 | bytes 14972928 | tf_op jit(solution)/shard_map/pallas_call | solution.py:446
  118.1 19.6 %shard_map.231 = (f32[256,768]{1,0:T(8,128)}, bf16[256,2304]{1,0:T(8,128)(2,1)}, f32[1,2304]{1,0:T(1,128)}, f32[1,768]{1,0:T(1,128)}, f32[3,768]{1,0:T(4,128)}, ...) custom-call(bf16[256,3072]{1,0:T(8,128)(2,1)} %get-tuple-element.63., ...), custom_call_target="tpu_custom_call" | custom-call | flops 10000000000 | bytes 21797888 | tf_op jit(solution)/shard_map/pallas_call | solution.py:446
  138.5 10.5 %shard_map.232 = (f32[256,768]{1,0:T(8,128)}, bf16[256,768]{1,0:T(8,128)(2,1)}, f32[1,768]{1,0:T(1,128)}, f32[3,768]{1,0:T(4,128)}) custom-call(bf16[256,2304]{1,0:T(8,128)(2,1)} %get-tuple-element.70.refs_0_, bf16[256,768]{1,0:T(8,128)(2,1)} %refs_1_.7, f32[1,4608]{1,0:T(1,128)} %fusion.13.refs_1_.refs_2_, f32[256,768]{1,0:T(8,128)} %get-tuple-element.71.refs_3_, ...), custom_call_target="tpu_custom_call" | custom-call | flops 10000000000 | bytes 15762432 | tf_op jit(solution)/shard_map/pallas_call | solution.py:446
  195.2 2.6 collective-permute-start.38
  200.6 5.3 %collective-permute-done.38 = bf16[4,20736]{1,0:T(4,128)(2,1)S(1)} collective-permute-done((bf16[4,20736]{1,0:T(4,128)(2,1)S(1)}, bf16[4,20736]{1,0:T(4,128)(2,1)S(1)}, u32[]{:S(2)}, u32[]{:S(2)}) %collective-permute-start.38) | collective-permute-done | bytes 165920 | tf_op jit(solution)/shard_map/ppermute | solution.py:43
  218.9 11.8 %collective-permute-done.73 = bf16[384,768]{1,0:T(8,128)(2,1)S(1)} collective-permute-done((bf16[384,768]{1,0:T(8,128)(2,1)S(1)}, bf16[384,768]{1,0:T(8,128)(2,1)S(1)}, u32[]{:S(2)}, u32[]{:S(2)}) %collective-permute-start.73) | collective-permute-done | bytes 589856 | tf_op jit(solution)/shard_map/ppermute | solution.py:43
  234.9 3.9 %collective-permute-done.57 = bf16[96,1536]{1,0:T(8,128)(2,1)S(1)} collective-permute-done((bf16[96,1536]{1,0:T(8,128)(2,1)S(1)}, bf16[96,1536]{1,0:T(8,128)(2,1)S(1)}, u32[]{:S(2)}, u32[]{:S(2)}) %collective-permute-start.57) | collective-permute-done | bytes 294944 | tf_op jit(solution)/shard_map/ppermute | solution.py:43
  246.2 3.2 collective-permute-start.79
  250.3 10.1 %collective-permute-done.78 = bf16[384,192]{1,0:T(8,128)(2,1)S(1)} collective-permute-done((bf16[384,192]{1,0:T(8,128)(2,1)S(1)}, bf16[384,192]{1,0:T(8,128)(2,1)S(1)}, u32[]{:S(2)}, u32[]{:S(2)}) %collective-permute-start.78) | collective-permute-done | bytes 147488 | tf_op jit(solution)/shard_map/ppermute | solution.py:43
  260.7 3.9 %collective-permute-start.80 = (bf16[384,192]{1,0:T(8,128)(2,1)S(1)}, bf16[384,192]{1,0:T(8,128)(2,1)S(1)}, u32[]{:S(2)}, u32[]{:S(2)}) collective-permute-start(bf16[384,192]{1,0:T(8,128)(2,1)S(1)} %add_convert_fusion.3), channel_id=1, source_target_pairs={{0,2},{1,3},{2,0},{3,1},{4,6},{5,7},{6,4},{7,5},{8,10},{9,11},{10,... | collective-permute-start | bytes 442376 | tf_op jit(solution)/shard_map/ppermute | solution.py:43
  267.8 3.9 %collective-permute-done.80 = bf16[384,192]{1,0:T(8,128)(2,1)S(1)} collective-permute-done((bf16[384,192]{1,0:T(8,128)(2,1)S(1)}, bf16[384,192]{1,0:T(8,128)(2,1)S(1)}, u32[]{:S(2)}, u32[]{:S(2)}) %collective-permute-start.80) | collective-permute-done | bytes 147488 | tf_op jit(solution)/shard_map/ppermute | solution.py:43
  272.4 9.2 %collective-permute-done.81 = bf16[384,192]{1,0:T(8,128)(2,1)S(1)} collective-permute-done((bf16[384,192]{1,0:T(8,128)(2,1)S(1)}, bf16[384,192]{1,0:T(8,128)(2,1)S(1)}, u32[]{:S(2)}, u32[]{:S(2)}) %collective-permute-start.81) | collective-permute-done | bytes 147488 | tf_op jit(solution)/shard_map/ppermute | solution.py:43
  289.8 7.9 %collective-permute-done.43 = bf16[96,3072]{1,0:T(8,128)(2,1)} collective-permute-done((bf16[96,3072]{1,0:T(8,128)(2,1)}, bf16[96,3072]{1,0:T(8,128)(2,1)}, u32[]{:S(2)}, u32[]{:S(2)}) %collective-permute-start.43) | collective-permute-done | bytes 589856 | tf_op jit(solution)/shard_map/ppermute | solution.py:43
  308.2 4.0 %collective-permute-start.62 = (bf16[96,768]{1,0:T(8,128)(2,1)S(1)}, bf16[96,768]{1,0:T(8,128)(2,1)S(1)}, u32[]{:S(2)}, u32[]{:S(2)}) collective-permute-start(bf16[96,768]{1,0:T(8,128)(2,1)S(1)} %get-tuple-element.144), channel_id=1, source_target_pairs={{0,2},{1,3},{2,0},{3,1},{4,6},{5,7},{6,4},{7,5},{8,10},{9,11},{10,... | collective-permute-start | bytes 442376 | tf_op jit(solution)/shard_map/ppermute | solution.py:43
  315.7 3.6 collective-permute-start.64
  319.4 7.3 %collective-permute-start.50 = (bf16[96,768]{1,0:T(8,128)(2,1)S(1)}, bf16[96,768]{1,0:T(8,128)(2,1)S(1)}, u32[]{:S(2)}, u32[]{:S(2)}) collective-permute-start(bf16[96,768]{1,0:T(8,128)(2,1)S(1)} %add_convert_fusion.5), channel_id=1, source_target_pairs={{0,2},{1,3},{2,0},{3,1},{4,6},{5,7},{6,4},{7,5},{8,10},{9,11},{10,... | collective-permute-start | bytes 442376 | tf_op jit(solution)/shard_map/ppermute | solution.py:43
  328.8 2.7 collective-permute-done.63
  333.5 4.0 %collective-permute-start.65 = (bf16[96,768]{1,0:T(8,128)(2,1)}, bf16[96,768]{1,0:T(8,128)(2,1)}, u32[]{:S(2)}, u32[]{:S(2)}) collective-permute-start(bf16[96,768]{1,0:T(8,128)(2,1)} %add_convert_fusion.4), channel_id=1, source_target_pairs={{0,2},{1,3},{2,0},{3,1},{4,6},{5,7},{6,4},{7,5},{8,10},{9,11},{10,... | collective-permute-start | bytes 442376 | tf_op jit(solution)/shard_map/ppermute | solution.py:43
  339.8 4.3 %collective-permute-done.51 = bf16[96,768]{1,0:T(8,128)(2,1)S(1)} collective-permute-done((bf16[96,768]{1,0:T(8,128)(2,1)S(1)}, bf16[96,768]{1,0:T(8,128)(2,1)S(1)}, u32[]{:S(2)}, u32[]{:S(2)}) %collective-permute-start.51) | collective-permute-done | bytes 147488 | tf_op jit(solution)/shard_map/ppermute | solution.py:43
  344.1 4.3 %collective-permute-start.67 = (bf16[96,768]{1,0:T(8,128)(2,1)}, bf16[96,768]{1,0:T(8,128)(2,1)}, u32[]{:S(2)}, u32[]{:S(2)}) collective-permute-start(bf16[96,768]{1,0:T(8,128)(2,1)} %add_convert_fusion.4), channel_id=1, source_target_pairs={{0,6},{1,7},{2,4},{3,5},{4,2},{5,3},{6,0},{7,1},{8,14},{9,15},{10,... | collective-permute-start | bytes 442376 | tf_op jit(solution)/shard_map/ppermute | solution.py:43
  350.6 3.1 collective-permute-done.66
  362.3 3.2 fusion.2
  365.5 3.0 copy.33
  (410 shorter events, 164.6 us)
Async XLA Ops:
  2.9 22.6 %collective-permute-start.7 = (bf16[96,3072]{1,0:T(8,128)(2,1)S(1)}, bf16[96,3072]{1,0:T(8,128)(2,1)S(1)}, u32[]{:S(2)}, u32[]{:S(2)}) collective-permute-start(bf16[96,3072]{1,0:T(8,128)(2,1)S(1)} %pad_maximum_fusion.1), channel_id=1, source_target_pairs={{0,16},{8,24},{16,0},{24,8},{1,17},{9,25},{17,1},{25,9},{2,18},{10... | collective-permute-start | bytes 1769480 | tf_op jit(solution)/shard_map/ppermute | solution.py:43
  5.9 19.6 %collective-permute-start.6 = (bf16[96,3072]{1,0:T(8,128)(2,1)S(1)}, bf16[96,3072]{1,0:T(8,128)(2,1)}, u32[]{:S(2)}, u32[]{:S(2)}) collective-permute-start(bf16[96,3072]{1,0:T(8,128)(2,1)S(1)} %pad_maximum_fusion.1), channel_id=1, source_target_pairs={{0,8},{8,0},{16,24},{24,16},{1,9},{9,1},{17,25},{25,17},{2,10},{10... | collective-permute-start | bytes 1769480 | tf_op jit(solution)/shard_map/ppermute | solution.py:43
  21.5 22.7 %collective-permute-start.3 = (f32[1,4608]{1,0:T(1,128)S(1)}, f32[1,4608]{1,0:T(1,128)S(1)}, u32[]{:S(2)}, u32[]{:S(2)}) collective-permute-start(f32[1,4608]{1,0:T(1,128)S(1)} %get-tuple-element.156), channel_id=1, source_target_pairs={{0,8},{8,0},{16,24},{24,16},{1,9},{9,1},{17,25},{25,17},{2,10},{10... | collective-permute-start | bytes 55304 | tf_op jit(solution)/shard_map/ppermute | solution.py:43
  23.1 24.2 %collective-permute-start.4 = (f32[1,4608]{1,0:T(1,128)S(1)}, f32[1,4608]{1,0:T(1,128)S(1)}, u32[]{:S(2)}, u32[]{:S(2)}) collective-permute-start(f32[1,4608]{1,0:T(1,128)S(1)} %get-tuple-element.158), channel_id=1, source_target_pairs={{0,16},{8,24},{16,0},{24,8},{1,17},{9,25},{17,1},{25,9},{2,18},{10... | collective-permute-start | bytes 55304 | tf_op jit(solution)/shard_map/ppermute | solution.py:43
  24.6 25.7 %collective-permute-start.5 = (f32[1,4608]{1,0:T(1,128)S(1)}, f32[1,4608]{1,0:T(1,128)S(1)}, u32[]{:S(2)}, u32[]{:S(2)}) collective-permute-start(f32[1,4608]{1,0:T(1,128)S(1)} %get-tuple-element.157), channel_id=1, source_target_pairs={{0,24},{8,16},{16,8},{24,0},{1,25},{9,17},{17,9},{25,1},{2,26},{10... | collective-permute-start | bytes 55304 | tf_op jit(solution)/shard_map/ppermute | solution.py:43
  43.1 23.2 %collective-permute-start.23 = (bf16[384,768]{1,0:T(8,128)(2,1)S(1)}, bf16[384,768]{1,0:T(8,128)(2,1)}, u32[]{:S(2)}, u32[]{:S(2)}) collective-permute-start(bf16[384,768]{1,0:T(8,128)(2,1)S(1)} %constant_dynamic-slice_fusion), channel_id=1, source_target_pairs={{0,16},{8,24},{16,0},{24,8},{1,17},{9,25},{17,1},{25,9},{2,18},{10... | collective-permute-start | bytes 1769480 | tf_op jit(solution)/shard_map/ppermute | solution.py:43
  44.2 23.1 %collective-permute-start.22 = (bf16[384,768]{1,0:T(8,128)(2,1)S(1)}, bf16[384,768]{1,0:T(8,128)(2,1)}, u32[]{:S(2)}, u32[]{:S(2)}) collective-permute-start(bf16[384,768]{1,0:T(8,128)(2,1)S(1)} %constant_dynamic-slice_fusion), channel_id=1, source_target_pairs={{0,8},{8,0},{16,24},{24,16},{1,9},{9,1},{17,25},{25,17},{2,10},{10... | collective-permute-start | bytes 1769480 | tf_op jit(solution)/shard_map/ppermute | solution.py:43
  70.2 17.8 %collective-permute-start.18 = (bf16[96,3072]{1,0:T(8,128)(2,1)}, bf16[96,3072]{1,0:T(8,128)(2,1)S(1)}, u32[]{:S(2)}, u32[]{:S(2)}) collective-permute-start(bf16[96,3072]{1,0:T(8,128)(2,1)} %collective-permute-done.14.refs_5_.refs_10_), channel_id=1, source_target_pairs={{0,1},{1,0},{2,3},{3,2},{4,5},{5,4},{6,7},{7,6},{8,9},{9,8},{10,11... | collective-permute-start | bytes 1769480 | tf_op jit(solution)/shard_map/ppermute | solution.py:43
  70.6 18.5 %collective-permute-start.19 = (bf16[96,3072]{1,0:T(8,128)(2,1)}, bf16[96,3072]{1,0:T(8,128)(2,1)S(1)}, u32[]{:S(2)}, u32[]{:S(2)}) collective-permute-start(bf16[96,3072]{1,0:T(8,128)(2,1)} %collective-permute-done.15.refs_6_.refs_11_), channel_id=1, source_target_pairs={{0,1},{1,0},{2,3},{3,2},{4,5},{5,4},{6,7},{7,6},{8,9},{9,8},{10,11... | collective-permute-start | bytes 1769480 | tf_op jit(solution)/shard_map/ppermute | solution.py:43
  88.0 16.9 %collective-permute-start.27 = (bf16[384,768]{1,0:T(8,128)(2,1)}, bf16[384,768]{1,0:T(8,128)(2,1)S(1)}, u32[]{:S(2)}, u32[]{:S(2)}) collective-permute-start(bf16[384,768]{1,0:T(8,128)(2,1)} %collective-permute-done.23.refs_6_.refs_20_), channel_id=1, source_target_pairs={{0,1},{1,0},{2,3},{3,2},{4,5},{5,4},{6,7},{7,6},{8,9},{9,8},{10,11... | collective-permute-start | bytes 1769480 | tf_op jit(solution)/shard_map/ppermute | solution.py:43
  103.8 67.5 %collective-permute-start.71 = (bf16[384,768]{1,0:T(8,128)(2,1)}, bf16[384,768]{1,0:T(8,128)(2,1)S(1)}, u32[]{:S(2)}, u32[]{:S(2)}) collective-permute-start(bf16[384,768]{1,0:T(8,128)(2,1)} %get-tuple-element.102), channel_id=1, source_target_pairs={{0,1},{1,0},{2,3},{3,2},{4,5},{5,4},{6,7},{7,6},{8,9},{9,8},{10,11... | collective-permute-start | bytes 1769480 | tf_op jit(solution)/shard_map/ppermute | solution.py:43
  104.0 69.4 %collective-permute-start.70 = (bf16[384,768]{1,0:T(8,128)(2,1)}, bf16[384,768]{1,0:T(8,128)(2,1)}, u32[]{:S(2)}, u32[]{:S(2)}) collective-permute-start(bf16[384,768]{1,0:T(8,128)(2,1)} %get-tuple-element.100), channel_id=1, source_target_pairs={{0,1},{1,0},{2,3},{3,2},{4,5},{5,4},{6,7},{7,6},{8,9},{9,8},{10,11... | collective-permute-start | bytes 1769480 | tf_op jit(solution)/shard_map/ppermute | solution.py:43
  104.4 71.9 %collective-permute-start.74 = (bf16[384,768]{1,0:T(8,128)(2,1)}, bf16[384,768]{1,0:T(8,128)(2,1)S(1)}, u32[]{:S(2)}, u32[]{:S(2)}) collective-permute-start(bf16[384,768]{1,0:T(8,128)(2,1)} %get-tuple-element.104), channel_id=1, source_target_pairs={{0,1},{1,0},{2,3},{3,2},{4,5},{5,4},{6,7},{7,6},{8,9},{9,8},{10,11... | collective-permute-start | bytes 1769480 | tf_op jit(solution)/shard_map/ppermute | solution.py:43
  104.5 113.0 %collective-permute-start.69 = (bf16[384,768]{1,0:T(8,128)(2,1)}, bf16[384,768]{1,0:T(8,128)(2,1)}, u32[]{:S(2)}, u32[]{:S(2)}) collective-permute-start(bf16[384,768]{1,0:T(8,128)(2,1)} %get-tuple-element.98), channel_id=1, source_target_pairs={{0,1},{1,0},{2,3},{3,2},{4,5},{5,4},{6,7},{7,6},{8,9},{9,8},{10,11... | collective-permute-start | bytes 1769480 | tf_op jit(solution)/shard_map/ppermute | solution.py:43
  176.4 17.2 %collective-permute-start.72 = (bf16[384,384]{1,0:T(8,128)(2,1)}, bf16[384,384]{1,0:T(8,128)(2,1)}, u32[]{:S(2)}, u32[]{:S(2)}) collective-permute-start(bf16[384,384]{1,0:T(8,128)(2,1)} %get-tuple-element.150), channel_id=1, source_target_pairs={{0,8},{8,0},{16,24},{24,16},{1,9},{9,1},{17,25},{25,17},{2,10},{10... | collective-permute-start | bytes 884744 | tf_op jit(solution)/shard_map/ppermute | solution.py:43
  186.4 26.8 %collective-permute-start.56 = (bf16[96,3072]{1,0:T(8,128)(2,1)}, bf16[96,3072]{1,0:T(8,128)(2,1)}, u32[]{:S(2)}, u32[]{:S(2)}) collective-permute-start(bf16[96,3072]{1,0:T(8,128)(2,1)} %get-tuple-element.94), channel_id=1, source_target_pairs={{0,1},{1,0},{2,3},{3,2},{4,5},{5,4},{6,7},{7,6},{8,9},{9,8},{10,11... | collective-permute-start | bytes 1769480 | tf_op jit(solution)/shard_map/ppermute | solution.py:43
  193.6 17.4 %collective-permute-start.59 = (bf16[96,3072]{1,0:T(8,128)(2,1)}, bf16[96,3072]{1,0:T(8,128)(2,1)}, u32[]{:S(2)}, u32[]{:S(2)}) collective-permute-start(bf16[96,3072]{1,0:T(8,128)(2,1)} %get-tuple-element.96), channel_id=1, source_target_pairs={{0,1},{1,0},{2,3},{3,2},{4,5},{5,4},{6,7},{7,6},{8,9},{9,8},{10,11... | collective-permute-start | bytes 1769480 | tf_op jit(solution)/shard_map/ppermute | solution.py:43
  205.9 96.9 %collective-permute-start.54 = (bf16[96,3072]{1,0:T(8,128)(2,1)}, bf16[96,3072]{1,0:T(8,128)(2,1)}, u32[]{:S(2)}, u32[]{:S(2)}) collective-permute-start(bf16[96,3072]{1,0:T(8,128)(2,1)} %get-tuple-element.90), channel_id=1, source_target_pairs={{0,1},{1,0},{2,3},{3,2},{4,5},{5,4},{6,7},{7,6},{8,9},{9,8},{10,11... | collective-permute-start | bytes 1769480 | tf_op jit(solution)/shard_map/ppermute | solution.py:43
  213.1 75.2 %collective-permute-start.39 = (bf16[96,3072]{1,0:T(8,128)(2,1)}, bf16[96,3072]{1,0:T(8,128)(2,1)}, u32[]{:S(2)}, u32[]{:S(2)}) collective-permute-start(bf16[96,3072]{1,0:T(8,128)(2,1)} %get-tuple-element.82), channel_id=1, source_target_pairs={{0,1},{1,0},{2,3},{3,2},{4,5},{5,4},{6,7},{7,6},{8,9},{9,8},{10,11... | collective-permute-start | bytes 1769480 | tf_op jit(solution)/shard_map/ppermute | solution.py:43
  217.5 21.3 %collective-permute-start.57 = (bf16[96,1536]{1,0:T(8,128)(2,1)S(1)}, bf16[96,1536]{1,0:T(8,128)(2,1)S(1)}, u32[]{:S(2)}, u32[]{:S(2)}) collective-permute-start(bf16[96,1536]{1,0:T(8,128)(2,1)S(1)} %get-tuple-element.152), channel_id=1, source_target_pairs={{0,8},{8,0},{16,24},{24,16},{1,9},{9,1},{17,25},{25,17},{2,10},{10... | collective-permute-start | bytes 884744 | tf_op jit(solution)/shard_map/ppermute | solution.py:43
  264.5 17.2 %collective-permute-start.81 = (bf16[384,192]{1,0:T(8,128)(2,1)S(1)}, bf16[384,192]{1,0:T(8,128)(2,1)S(1)}, u32[]{:S(2)}, u32[]{:S(2)}) collective-permute-start(bf16[384,192]{1,0:T(8,128)(2,1)S(1)} %add_convert_fusion.3), channel_id=1, source_target_pairs={{0,4},{1,5},{2,6},{3,7},{4,0},{5,1},{6,2},{7,3},{8,12},{9,13},{10,... | collective-permute-start | bytes 442376 | tf_op jit(solution)/shard_map/ppermute | solution.py:43
  264.7 17.7 %collective-permute-start.82 = (bf16[384,192]{1,0:T(8,128)(2,1)S(1)}, bf16[384,192]{1,0:T(8,128)(2,1)S(1)}, u32[]{:S(2)}, u32[]{:S(2)}) collective-permute-start(bf16[384,192]{1,0:T(8,128)(2,1)S(1)} %add_convert_fusion.3), channel_id=1, source_target_pairs={{0,6},{1,7},{2,4},{3,5},{4,2},{5,3},{6,0},{7,1},{8,14},{9,15},{10,... | collective-permute-start | bytes 442376 | tf_op jit(solution)/shard_map/ppermute | solution.py:43
  271.7 32.1 %collective-permute-start.58 = (bf16[96,3072]{1,0:T(8,128)(2,1)}, bf16[96,3072]{1,0:T(8,128)(2,1)}, u32[]{:S(2)}, u32[]{:S(2)}) collective-permute-start(bf16[96,3072]{1,0:T(8,128)(2,1)} %pad_maximum_fusion.5), channel_id=1, source_target_pairs={{0,16},{8,24},{16,0},{24,8},{1,17},{9,25},{17,1},{25,9},{2,18},{10... | collective-permute-start | bytes 1769480 | tf_op jit(solution)/shard_map/ppermute | solution.py:43
  288.3 18.3 %collective-permute-start.61 = (bf16[96,3072]{1,0:T(8,128)(2,1)}, bf16[96,3072]{1,0:T(8,128)(2,1)S(1)}, u32[]{:S(2)}, u32[]{:S(2)}) collective-permute-start(bf16[96,3072]{1,0:T(8,128)(2,1)} %pad_maximum_fusion.6), channel_id=1, source_target_pairs={{0,8},{8,0},{16,24},{24,16},{1,9},{9,1},{17,25},{25,17},{2,10},{10... | collective-permute-start | bytes 1769480 | tf_op jit(solution)/shard_map/ppermute | solution.py:43
  297.7 64.6 %collective-permute-start.83 = (bf16[384,768]{0,1:T(8,128)(2,1)}, bf16[384,768]{0,1:T(8,128)(2,1)}, u32[]{:S(2)}, u32[]{:S(2)}) collective-permute-start(bf16[384,768]{0,1:T(8,128)(2,1)} %bitcast.31), channel_id=1, source_target_pairs={{0,1},{1,0},{2,3},{3,2},{4,5},{5,4},{6,7},{7,6},{8,9},{9,8},{10,11... | collective-permute-start | bytes 1769480 | tf_op jit(solution)/shard_map/ppermute | solution.py:43
  308.2 18.4 %collective-permute-start.62 = (bf16[96,768]{1,0:T(8,128)(2,1)S(1)}, bf16[96,768]{1,0:T(8,128)(2,1)S(1)}, u32[]{:S(2)}, u32[]{:S(2)}) collective-permute-start(bf16[96,768]{1,0:T(8,128)(2,1)S(1)} %get-tuple-element.144), channel_id=1, source_target_pairs={{0,2},{1,3},{2,0},{3,1},{4,6},{5,7},{6,4},{7,5},{8,10},{9,11},{10,... | collective-permute-start | bytes 442376 | tf_op jit(solution)/shard_map/ppermute | solution.py:43
  312.2 19.2 %collective-permute-start.63 = (bf16[96,768]{1,0:T(8,128)(2,1)S(1)}, bf16[96,768]{1,0:T(8,128)(2,1)S(1)}, u32[]{:S(2)}, u32[]{:S(2)}) collective-permute-start(bf16[96,768]{1,0:T(8,128)(2,1)S(1)} %get-tuple-element.146), channel_id=1, source_target_pairs={{0,4},{1,5},{2,6},{3,7},{4,0},{5,1},{6,2},{7,3},{8,12},{9,13},{10,... | collective-permute-start | bytes 442376 | tf_op jit(solution)/shard_map/ppermute | solution.py:43
  315.7 17.1 %collective-permute-start.64 = (bf16[96,768]{1,0:T(8,128)(2,1)S(1)}, bf16[96,768]{1,0:T(8,128)(2,1)S(1)}, u32[]{:S(2)}, u32[]{:S(2)}) collective-permute-start(bf16[96,768]{1,0:T(8,128)(2,1)S(1)} %get-tuple-element.145), channel_id=1, source_target_pairs={{0,6},{1,7},{2,4},{3,5},{4,2},{5,3},{6,0},{7,1},{8,14},{9,15},{10,... | collective-permute-start | bytes 442376 | tf_op jit(solution)/shard_map/ppermute | solution.py:43
  319.4 18.1 %collective-permute-start.50 = (bf16[96,768]{1,0:T(8,128)(2,1)S(1)}, bf16[96,768]{1,0:T(8,128)(2,1)S(1)}, u32[]{:S(2)}, u32[]{:S(2)}) collective-permute-start(bf16[96,768]{1,0:T(8,128)(2,1)S(1)} %add_convert_fusion.5), channel_id=1, source_target_pairs={{0,2},{1,3},{2,0},{3,1},{4,6},{5,7},{6,4},{7,5},{8,10},{9,11},{10,... | collective-permute-start | bytes 442376 | tf_op jit(solution)/shard_map/ppermute | solution.py:43
  326.7 17.4 %collective-permute-start.51 = (bf16[96,768]{1,0:T(8,128)(2,1)S(1)}, bf16[96,768]{1,0:T(8,128)(2,1)S(1)}, u32[]{:S(2)}, u32[]{:S(2)}) collective-permute-start(bf16[96,768]{1,0:T(8,128)(2,1)S(1)} %add_convert_fusion.5), channel_id=1, source_target_pairs={{0,4},{1,5},{2,6},{3,7},{4,0},{5,1},{6,2},{7,3},{8,12},{9,13},{10,... | collective-permute-start | bytes 442376 | tf_op jit(solution)/shard_map/ppermute | solution.py:43
  331.5 17.0 %collective-permute-start.52 = (bf16[96,768]{1,0:T(8,128)(2,1)S(1)}, bf16[96,768]{1,0:T(8,128)(2,1)S(1)}, u32[]{:S(2)}, u32[]{:S(2)}) collective-permute-start(bf16[96,768]{1,0:T(8,128)(2,1)S(1)} %add_convert_fusion.5), channel_id=1, source_target_pairs={{0,6},{1,7},{2,4},{3,5},{4,2},{5,3},{6,0},{7,1},{8,14},{9,15},{10,... | collective-permute-start | bytes 442376 | tf_op jit(solution)/shard_map/ppermute | solution.py:43
  333.5 17.1 %collective-permute-start.65 = (bf16[96,768]{1,0:T(8,128)(2,1)}, bf16[96,768]{1,0:T(8,128)(2,1)}, u32[]{:S(2)}, u32[]{:S(2)}) collective-permute-start(bf16[96,768]{1,0:T(8,128)(2,1)} %add_convert_fusion.4), channel_id=1, source_target_pairs={{0,2},{1,3},{2,0},{3,1},{4,6},{5,7},{6,4},{7,5},{8,10},{9,11},{10,... | collective-permute-start | bytes 442376 | tf_op jit(solution)/shard_map/ppermute | solution.py:43
  (109 other events, 954.9 us)
where the time goes:
time: 376 us; the launch traced here: 375 us
  waiting for transfers between devices  112 us (30%)
  starting transfers between devices  100 us (27%)
  Pallas kernels  66 us (18%)
  local copies, waits for them, and re-layouts  49.8 us (13%)
  other arithmetic  41.4 us (11%)
    ppermute x84, waiting for transfers between devices, hop(): return lax.ppermute(value, axis, [(at, at ^ flip) for at in range(size)])  112 us
    ppermute x84, starting transfers between devices, hop(): return lax.ppermute(value, axis, [(at, at ^ flip) for at in range(size)])  100 us
    pallas_call x5, Pallas kernels, call(): pl.pallas_call(functools.partial(kernel, shards), out_shape=outs + outsid...  66 us
    unnamed x124, local copies, waits for them, and re-layouts  17 us
    another operation x15, other arithmetic  7.94 us
  transfers between devices with their start and end apart: 84, of which 26 were waited for; matrix products, arithmetic and copies ran while one was open for 23% of the time, Pallas kernels for 18%

commit v1 on v0

v1 whole, which is shorter than its diff:
```python
import functools

import jax
import jax.numpy as jnp
from jax import lax
from jax.experimental import pallas as pl
from jax.experimental.pallas import tpu as pltpu
from jax.sharding import PartitionSpec as P

F32 = jnp.float32
BF16 = jnp.bfloat16
HEAD = 64


def dot_nn(left, right):
    return lax.dot_general(left, right, (((1,), (0,)), ((), ())), preferred_element_type=F32)


def dot_tn(left, right):
    return lax.dot_general(left, right, (((0,), (0,)), ((), ())), preferred_element_type=F32)


def dot_nt(left, right):
    return lax.dot_general(left, right, (((1,), (1,)), ((), ())), preferred_element_type=F32)


def layer_norm(values):
    center = values - jnp.mean(values, -1, keepdims=True)
    rstd_val = lax.rsqrt(jnp.mean(center * center, -1, keepdims=True) + 1e-06)
    return (center * rstd_val, rstd_val)


def norm_back(grad_norm, normed, rstd_val):
    return rstd_val * (
        grad_norm
        - jnp.mean(grad_norm, -1, keepdims=True)
        - normed * jnp.mean(grad_norm * normed, -1, keepdims=True)
    )


def hop(value, axis, size, flip):
    return lax.ppermute(value, axis, [(at, at ^ flip) for at in range(size)])


def bits_of(number):
    return [1 << at for at in range(number.bit_length()) if number >> at & 1]


def by_weight(count):
    return sorted(range(1, count), key=lambda number: (bin(number).count("1"), number))


def xor_rows(rows, place):
    count = rows.shape[0]
    flip = 1
    while flip < count:
        swapped = rows.reshape(count // (2 * flip), 2, flip, -1)[:, ::-1].reshape(rows.shape)
        rows = jnp.where((place & flip) != 0, swapped, rows)
        flip *= 2
    return rows


def part_count(shards):
    return max(1, shards.bit_length() - 1)


def piece_layout(shards, width):
    layout = []
    for number in by_weight(shards):
        parts = 1 if len(bits_of(number)) == 1 else part_count(shards)
        span = width // parts
        layout += [(number, at * span, span) for at in range(parts)]
    return layout


def way(number, at):
    ways = bits_of(number)
    return ways[at % len(ways)]


def after(value, *others):
    return lax.optimization_barrier((value,) + others)[0]


def gate(values, *others):
    return list(lax.optimization_barrier(tuple(values) + others)[: len(values)])


class Gather:
    def __init__(self, half, shards, replicas):
        self.shards, self.replicas = shards, replicas
        self.half = half
        self.parts = part_count(shards)
        self.held = {}
        self.depths = shards.bit_length() - 1

    def operands(self, depth):
        span = self.half.shape[1] // self.parts
        if depth == 1:
            return [self.half]
        found = []
        for number in range(1, self.shards):
            if len(bits_of(number)) == depth:
                for at in range(self.parts):
                    source = self.held[number ^ way(number, at)]
                    if isinstance(source, list):
                        found.append(source[at])
                    else:
                        found.append(source[:, at * span : (at + 1) * span])
        return found

    def send(self, depth, operands):
        got = []
        operands = list(operands)
        for number in range(1, self.shards):
            if len(bits_of(number)) == depth:
                if depth == 1:
                    got.append(hop(operands[0], "shard", self.shards, number))
                else:
                    for at in range(self.parts):
                        flip = way(number, at)
                        got.append(hop(operands.pop(0), "shard", self.shards, flip))
        return got

    def hold(self, depth, got):
        got = list(got)
        for number in range(1, self.shards):
            if len(bits_of(number)) == depth:
                if depth == 1:
                    self.held[number] = got.pop(0)
                else:
                    self.held[number] = [got.pop(0) for _ in range(self.parts)]

    def pieces(self):
        flat = []
        for number in by_weight(self.shards):
            piece = self.held[number]
            flat += piece if isinstance(piece, list) else [piece]
        return flat + [hop(piece, "replica", self.replicas, 1) for piece in flat]


class Reduction:
    def __init__(self, keep, send, shards, replicas, chunks):
        self.keep, self.partner = keep, send
        self.shards, self.replicas, self.chunks = shards, replicas, chunks
        self.parts = part_count(shards)
        self.bits = [1 << at for at in range(shards.bit_length() - 1)]
        self.terms = {at: [] for at in range(self.parts)}

    def swap(self):
        self.came = hop(self.partner, "replica", self.replicas, 1)
        return self.came

    def order(self, at):
        return self.bits[at:] + self.bits[:at]

    def total(self, at, stage):
        order = self.order(at)
        span = self.keep.shape[2] // self.parts
        index = [slice(None)] * len(order)
        for bit in order[:stage]:
            index[len(order) - bit.bit_length()] = slice(0, 1)
        if stage < len(order):
            index[len(order) - order[stage].bit_length()] = slice(1, 2)
        index = tuple(index)
        value = None
        for array in (self.keep, self.came):
            cube = array.reshape((2,) * len(order) + array.shape[1:])
            cube = cube[index + (slice(None), slice(at * span, (at + 1) * span))].astype(F32)
            value = cube if value is None else value + cube
        for term in self.terms[at]:
            value = value + term[index].astype(F32)
        return value

    def ready(self, stage):
        self.sent = [self.total(at, stage).astype(BF16) for at in range(self.parts)]
        return self.sent

    def send(self, stage):
        self.flying = []
        for at in range(self.parts):
            piece = self.sent[at]
            got = hop(
                piece.reshape((-1,) + piece.shape[-2:]), "shard", self.shards, self.order(at)[stage]
            )
            self.flying.append(got.reshape(piece.shape))
        return self.flying

    def land(self, got):
        for at in range(self.parts):
            self.terms[at].append(got[at])

    def own(self):
        values = [self.total(at, len(self.bits)) for at in range(self.parts)]
        values = [value.reshape(value.shape[-2:]) for value in values]
        if self.chunks == 1:
            values = [jnp.concatenate(values, 1)]
        self.values = [value.astype(BF16) for value in values]
        return self.values

    def rounds(self):
        return self.replicas // 2 - 1

    def fold(self, at):
        chips = self.replicas // 2
        mid = chips // 2 - 1
        if at < mid:
            links = [(at, at + 1), (chips - 1 - at, chips - 2 - at)]
        elif at == mid:
            links = [(mid, mid + 1), (mid + 1, mid)]
        else:
            out = 2 * mid - at
            links = [(out + 1, out), (chips - 2 - out, chips - 1 - out)]
        pairs = [(2 * low + core, 2 * high + core) for low, high in links for core in range(2)]
        self.flying = [lax.ppermute(value, "replica", pairs) for value in self.values]
        return self.flying

    def folded(self, at, got):
        chips = self.replicas // 2
        mid = chips // 2 - 1
        chip = lax.axis_index("replica") // 2
        if at <= mid:
            self.values = [
                (value.astype(F32) + piece.astype(F32)).astype(BF16)
                for value, piece in zip(self.values, got)
            ]
        else:
            out = 2 * mid - at
            outer = (chip == out) | (chip == chips - 1 - out)
            self.values = [
                jnp.where(outer, piece, value) for value, piece in zip(self.values, got)
            ]
        return self.values

    def finish(self):
        core = lax.axis_index("replica") % 2
        cols = []
        for value in self.values:
            other = hop(value, "replica", self.replicas, 1)
            cols.append(
                jnp.where(
                    core == 1,
                    jnp.concatenate([other, value], 0),
                    jnp.concatenate([value, other], 0),
                )
            )
        whole = cols[0] if len(cols) == 1 else jnp.concatenate(cols, 1)
        return whole.astype(F32)


def together(*groups):
    flat = [value for group in groups for value in group]
    flat = list(lax.optimization_barrier(tuple(flat)))
    found = []
    for group in groups:
        found.append(flat[: len(group)])
        flat = flat[len(group) :]
    return found


def start_fetch(own, pieces, whole, sems, shards):
    place = lax.axis_index("shard")
    core = lax.axis_index("replica") % 2
    total_rows, width = whole.shape
    block = total_rows // shards
    half = block // 2
    copies = []

    def add(source, row, low, cols):
        rows = source.shape[0]
        there = whole.at[pl.ds(pl.multiple_of(row, 16), rows), pl.ds(low, cols)]
        copy = pltpu.make_async_copy(source, there, sems.at[len(copies)])
        copy.start()
        copies.append(copy)

    low = 0
    for part in own:
        cols = part.shape[1]
        add(part, place * block, low, cols)
        low += cols
    layout = piece_layout(shards, width)
    for at, (number, first, cols) in enumerate(layout):
        for side, source in ((core, pieces[at]), (1 - core, pieces[len(layout) + at])):
            add(source, (place ^ number) * block + side * half, first, cols)
    return copies


def start_emit(grad, low, cols, keep, send, sems, shards, copies):
    place = lax.axis_index("shard")
    core = lax.axis_index("replica") % 2
    block = grad.shape[0] // shards
    half = block // 2
    for number in range(shards):
        for side, target in ((core, keep), (1 - core, send)):
            row = pl.multiple_of((place ^ number) * block + side * half, 16)
            copy = pltpu.make_async_copy(
                grad.at[pl.ds(row, half), pl.ds(low, cols)],
                target.at[number, :, pl.ds(low, cols)],
                sems.at[len(copies)],
            )
            copy.start()
            copies.append(copy)


def wait_all(copies):
    for copy in copies:
        copy.wait()


def mod_piece(mod, at, width):
    return mod[:, at * width : (at + 1) * width]


def piece_total(shards):
    return 2 * len(piece_layout(shards, 1 << 20))


def take(refs, count):
    head = refs[:count]
    del refs[:count]
    return head


def gelu_parts(pre):
    scale = 0.7978845608028654
    square = pre * pre
    inner = jnp.tanh(scale * (pre + 0.044715 * (square * pre)))
    value = 0.5 * pre * (1.0 + inner)
    slope = 0.5 * (1.0 + inner) + 0.5 * pre * (1.0 - inner * inner) * (
        scale * (1.0 + 0.134145 * square)
    )
    return value, slope


def attend_kernel(shards, *refs):
    refs = list(refs)
    tokens, mod, bias_qv, bias_out = take(refs, 4)
    own = take(refs, 2)
    pieces = take(refs, piece_total(shards))
    modul_a, qkv, attended, lse, branch_a, middle, modul_b = take(refs, 7)
    weight, sems = refs
    rows, width = tokens.shape
    copies = start_fetch(own, pieces, weight, sems, shards)
    inputs = tokens[...].astype(F32)
    norm_a, _ = layer_norm(inputs)
    mod_val = mod[...]
    modul = (norm_a * (1.0 + mod_piece(mod_val, 1, width)) + mod_piece(mod_val, 0, width)).astype(
        BF16
    )
    modul_a[...] = modul
    wait_all(copies)
    for at in range(3):
        projected = dot_nn(modul, weight[:, at * width : (at + 1) * width])
        if at != 1:
            low = 0 if at == 0 else width
            projected = projected + bias_qv[:, low : low + width]
        qkv[:, at * width : (at + 1) * width] = projected.astype(BF16)
    lane = lax.broadcasted_iota(jnp.int32, (rows, 2 * HEAD), 1)

    def pair(at, lse_all):
        col = pl.multiple_of(at * 2 * HEAD, 2 * HEAD)
        query = qkv[:, pl.ds(col, 2 * HEAD)]
        key = qkv[:, pl.ds(width + col, 2 * HEAD)]
        value = qkv[:, pl.ds(2 * width + col, 2 * HEAD)]
        out = jnp.zeros((rows, 2 * HEAD), F32)
        for side in range(2):
            mask = (lane < HEAD) if side == 0 else (lane >= HEAD)
            scores = dot_nt(jnp.where(mask, query, 0), key) * 0.125
            top = jnp.max(scores, -1, keepdims=True)
            exps = jnp.exp(scores - top)
            total = jnp.sum(exps, -1, keepdims=True)
            probs = (exps / total).astype(BF16)
            out = out + dot_nn(probs, jnp.where(mask, value, 0))
            lse_all = jnp.where(lane == 2 * at + side, top + jnp.log(total), lse_all)
        attended[:, pl.ds(col, 2 * HEAD)] = out.astype(BF16)
        return lse_all

    lse[...] = lax.fori_loop(
        0, width // (2 * HEAD), pair, jnp.zeros((rows, 2 * HEAD), F32)
    )
    branch = dot_nn(attended[...], weight[:, 3 * width :]) + bias_out[...]
    branch_a[...] = branch
    mid = inputs + mod_piece(mod_val, 2, width) * branch
    middle[...] = mid
    norm_b, _ = layer_norm(mid)
    modul_b[...] = (
        norm_b * (1.0 + mod_piece(mod_val, 4, width)) + mod_piece(mod_val, 3, width)
    ).astype(BF16)


def hidden_kernel(shards, *refs):
    refs = list(refs)
    modul_b, cot, mod, bias_fc1 = take(refs, 4)
    own = take(refs, 1)
    pieces = take(refs, piece_total(shards))
    hidden, slope = take(refs, 2)
    keep, send = take(refs, 2)
    weight, grad, sems, out_sems = refs
    rows, width = modul_b.shape
    copies = start_fetch(own, pieces, weight, sems, shards)
    low_branch = (cot[...].astype(F32) * mod_piece(mod[...], 5, width)).astype(BF16)
    modul = modul_b[...]
    wait_all(copies)
    place = lax.axis_index("shard")
    core = lax.axis_index("replica") % 2
    span = weight.shape[1] // shards
    half = span // 2
    outs = []
    for number in range(shards - 1, -1, -1):
        col = pl.multiple_of((place ^ number) * span, 128)
        pre = dot_nn(modul, weight[:, pl.ds(col, span)]) + bias_fc1[:, pl.ds(col, span)]
        value, rate = gelu_parts(pre)
        value = value.astype(BF16)
        hidden[:, pl.ds(col, span)] = value
        slope[:, pl.ds(col, span)] = rate
        grad[number] = dot_tn(value, low_branch).astype(BF16)
        for side, target in ((core, keep), (1 - core, send)):
            row = pl.multiple_of(side * half, 16)
            copy = pltpu.make_async_copy(
                grad.at[number, pl.ds(row, half), :], target.at[number], out_sems.at[len(outs)]
            )
            copy.start()
            outs.append(copy)
    wait_all(outs)


def pre_kernel(shards, *refs):
    refs = list(refs)
    modul_b, cot, mod, slope = take(refs, 4)
    own = take(refs, 1)
    pieces = take(refs, piece_total(shards))
    low_pre, sum_pre = take(refs, 2)
    keep, send = take(refs, 2)
    weight, grad, turned, sems, out_sems = refs
    rows, width = modul_b.shape
    copies = start_fetch(own, pieces, weight, sems, shards)
    low_branch = (cot[...].astype(F32) * mod_piece(mod[...], 5, width)).astype(BF16)
    turned[...] = modul_b[...].T
    wait_all(copies)

    outs = []
    for col in range(0, weight.shape[0], width):
        cols = slice(col, col + width)
        grad_pre = dot_nt(low_branch, weight[cols, :]) * slope[:, cols]
        sum_pre[:, cols] = jnp.sum(grad_pre, 0, keepdims=True)
        low = grad_pre.astype(BF16)
        low_pre[:, cols] = low
        grad[:, cols] = dot_nn(turned[...], low).astype(BF16)
        start_emit(grad, col, width, keep, send, out_sems, shards, outs)
    wait_all(outs)


def middle_kernel(shards, *refs):
    refs = list(refs)
    low_pre, cot, mod, middle, branch_a = take(refs, 5)
    own = take(refs, 1)
    pieces = take(refs, piece_total(shards))
    grad_middle, low_branch_a, sum_out, grad_mods = take(refs, 4)
    weight, sems = refs
    rows, width = middle.shape
    copies = start_fetch(own, pieces, weight, sems, shards)
    mod_val = mod[...]
    norm_b, rstd_b = layer_norm(middle[...])
    wait_all(copies)
    grad_modul = dot_nt(low_pre[...], weight[...])
    grad_mods[0:1, :] = jnp.sum(grad_modul, 0, keepdims=True)
    grad_mods[1:2, :] = jnp.sum(grad_modul * norm_b, 0, keepdims=True)
    grad_mid = cot[...].astype(F32) + norm_back(
        grad_modul * (1.0 + mod_piece(mod_val, 4, width)), norm_b, rstd_b
    )
    grad_middle[...] = grad_mid
    grad_mods[2:3, :] = jnp.sum(grad_mid * branch_a[...], 0, keepdims=True)
    grad_branch = grad_mid * mod_piece(mod_val, 2, width)
    sum_out[...] = jnp.sum(grad_branch, 0, keepdims=True)
    low_branch_a[...] = grad_branch.astype(BF16)


def back_kernel(shards, *refs):
    refs = list(refs)
    low_branch_a, modul_a, qkv, attended, lse = take(refs, 5)
    own = take(refs, 2)
    pieces = take(refs, piece_total(shards))
    low_proj, sum_proj = take(refs, 2)
    keep, send = take(refs, 2)
    weight, grad, grad_att, turned, sems, out_sems = refs
    rows, width = modul_a.shape
    copies = start_fetch(own, pieces, weight, sems, shards)
    low_branch = low_branch_a[...]
    outs = []
    turned[...] = attended[...].T
    grad[:, 3 * width :] = dot_nn(turned[...], low_branch).astype(BF16)
    start_emit(grad, 3 * width, width, keep, send, out_sems, shards, outs)
    turned[...] = modul_a[...].T
    wait_all(copies)
    grad_att[...] = dot_nt(low_branch, weight[:, 3 * width :]).astype(BF16)
    lane = lax.broadcasted_iota(jnp.int32, (rows, 2 * HEAD), 1)
    lse_val = lse[...]

    def pair(at, carry):
        col = pl.multiple_of(at * 2 * HEAD, 2 * HEAD)
        query = qkv[:, pl.ds(col, 2 * HEAD)]
        key = qkv[:, pl.ds(width + col, 2 * HEAD)]
        value = qkv[:, pl.ds(2 * width + col, 2 * HEAD)]
        grad_out = grad_att[:, pl.ds(col, 2 * HEAD)]
        product = grad_out.astype(F32) * attended[:, pl.ds(col, 2 * HEAD)].astype(F32)
        grad_q = jnp.zeros((rows, 2 * HEAD), F32)
        grad_k = jnp.zeros((rows, 2 * HEAD), F32)
        grad_v = jnp.zeros((rows, 2 * HEAD), F32)
        for side in range(2):
            mask = (lane < HEAD) if side == 0 else (lane >= HEAD)
            query_m = jnp.where(mask, query, 0)
            grad_m = jnp.where(mask, grad_out, 0)
            scores = dot_nt(query_m, key) * 0.125
            log_total = jnp.sum(
                jnp.where(lane == 2 * at + side, lse_val, 0.0), -1, keepdims=True
            )
            probs = jnp.exp(scores - log_total)
            delta = jnp.sum(jnp.where(mask, product, 0.0), -1, keepdims=True)
            grad_scores = (probs * (dot_nt(grad_m, value) - delta) * 0.125).astype(BF16)
            grad_v = grad_v + dot_tn(probs.astype(BF16), grad_m)
            grad_q = grad_q + dot_nn(grad_scores, jnp.where(mask, key, 0))
            grad_k = grad_k + dot_tn(grad_scores, query_m)
        for part, piece in enumerate((grad_q, grad_k, grad_v)):
            there = pl.multiple_of(part * width + col, 2 * HEAD)
            sum_proj[:, pl.ds(there, 2 * HEAD)] = jnp.sum(piece, 0, keepdims=True)
            low_proj[:, pl.ds(there, 2 * HEAD)] = piece.astype(BF16)
        return carry

    lax.fori_loop(0, width // (2 * HEAD), pair, 0, unroll=2)
    for at in range(3):
        cols = slice(at * width, (at + 1) * width)
        grad[:, cols] = dot_nn(turned[...], low_proj[:, cols]).astype(BF16)
        start_emit(grad, at * width, width, keep, send, out_sems, shards, outs)
    wait_all(outs)


def last_kernel(shards, *refs):
    refs = list(refs)
    low_proj, tokens, mod, grad_middle, hidden, middle, cot, bias_fc2 = take(refs, 8)
    sum_proj, sum_out, sum_pre, mods_b = take(refs, 4)
    own_qkvo = take(refs, 2)
    pieces_qkvo = take(refs, piece_total(shards))
    own_fc2 = take(refs, 1)
    pieces_fc2 = take(refs, piece_total(shards))
    grad_tokens, mixed, news = take(refs, 3)
    w_qkvo, w_fc2, sems_qkvo, sems_fc2 = refs
    rows, width = tokens.shape
    copies_qkvo = start_fetch(own_qkvo, pieces_qkvo, w_qkvo, sems_qkvo, shards)
    copies_fc2 = start_fetch(own_fc2, pieces_fc2, w_fc2, sems_fc2, shards)
    mod_val = mod[...]
    norm_a, rstd_a = layer_norm(tokens[...].astype(F32))
    wait_all(copies_qkvo)
    grad_modul = dot_nt(low_proj[...], w_qkvo[:, : 3 * width])
    sums = [
        jnp.sum(grad_modul, 0, keepdims=True),
        jnp.sum(grad_modul * norm_a, 0, keepdims=True),
        mods_b[2:3, :],
        mods_b[0:1, :],
        mods_b[1:2, :],
    ]
    grad_tokens[...] = grad_middle[...] + norm_back(
        grad_modul * (1.0 + mod_piece(mod_val, 1, width)), norm_a, rstd_a
    )
    wait_all(copies_fc2)
    branch_b = dot_nn(hidden[...], w_fc2[...]) + bias_fc2[...]
    gate_b = mod_piece(mod_val, 5, width)
    grad_out = cot[...].astype(F32)
    mixed[...] = (middle[...] + gate_b * branch_b).astype(BF16)
    sums.append(jnp.sum(grad_out * branch_b, 0, keepdims=True))
    sums += [sum_proj[:, :width], sum_proj[:, 2 * width :], sum_out[...], sum_pre[...]]
    sums.append(jnp.sum(grad_out * gate_b, 0, keepdims=True))
    low = 0
    for piece in sums:
        news[:, low : low + piece.shape[1]] = piece.astype(BF16)
        low += piece.shape[1]


def share_kernel(shards, *refs):
    refs = list(refs)
    news = take(refs, shards)
    w_mod, group_cols = take(refs, 2)
    back = take(refs, shards)
    share, rows_ref = refs
    span = w_mod.shape[1]
    cols = w_mod.shape[0]
    rows_ref[...] = jnp.zeros_like(rows_ref)
    biases = jnp.zeros((1, news[0].shape[1] - span), F32)
    for at in range(shards):
        rows_ref[at : at + 1, :span] = news[at][:, :span].astype(F32)
        biases = biases + news[at][:, span:].astype(F32)
    low = rows_ref[:, :span].astype(BF16)
    rows_back = dot_nt(low, w_mod[...])
    for at in range(shards):
        for owner in range(shards):
            back[at][:, owner * cols : (owner + 1) * cols] = jnp.where(
                lax.axis_index("shard") == owner, rows_back[at : at + 1, :], 0.0
            )
    rows_ref[:shards, span : span + cols] = group_cols[...].astype(F32)
    part = biases.shape[1] // 2
    for at in range(2):
        rows_ref[shards + at : shards + at + 1, :part] = biases[:, at * part : (at + 1) * part]
    share[0] = rows_ref[...].astype(BF16)


def total_kernel(shards, *refs):
    share, total_mod, own_mod, own_qv, own_out, own_fc1, own_fc2 = refs
    cols, span = total_mod.shape
    groups, count, _ = share.shape
    row = lax.broadcasted_iota(jnp.int32, (count, 1), 0)
    total = jnp.zeros((count, share.shape[2]), F32)
    for at in range(groups):
        total = total + share[at].astype(F32)
    place = lax.axis_index("shard")

    def own(target, values):
        size = target.shape[1]
        found = jnp.zeros((1, size), F32)
        for at in range(shards):
            found = jnp.where(place == at, values[:, at * size : (at + 1) * size], found)
        target[...] = found

    own(own_mod, jnp.sum(jnp.where(row < shards, total[:, :span], 0.0), 0, keepdims=True))
    part = shards * (own_qv.shape[1] + own_out.shape[1] + own_fc1.shape[1] + own_fc2.shape[1]) // 2
    biases = jnp.concatenate(
        [total[shards : shards + 1, :part], total[shards + 1 : shards + 2, :part]], 1
    )
    low = 0
    for target in (own_qv, own_out, own_fc1, own_fc2):
        high = low + shards * target.shape[1]
        own(target, biases[:, low:high])
        low = high
    whole = share[...].reshape(groups * count, share.shape[2])
    left = whole[:, span : span + cols]
    total_mod[...] = dot_tn(left, whole[:, :span])


def call(kernel, shards, inside, outside, outs, outside_outs, scratch, flops):
    vmem = pl.BlockSpec(memory_space=pltpu.VMEM)
    anywhere = pl.BlockSpec(memory_space=pl.ANY)
    moved = sum(value.size * value.dtype.itemsize for value in inside + outside)
    moved += sum(value.size * value.dtype.itemsize for value in outs + outside_outs)
    return pl.pallas_call(
        functools.partial(kernel, shards),
        out_shape=outs + outside_outs,
        in_specs=[vmem] * len(inside) + [anywhere] * len(outside),
        out_specs=[vmem] * len(outs) + [anywhere] * len(outside_outs),
        scratch_shapes=scratch,
        cost_estimate=pl.CostEstimate(flops=flops, bytes_accessed=moved, transcendentals=0),
        compiler_params=pltpu.CompilerParams(vmem_limit_bytes=56 << 20),
    )(*inside, *outside)


def shape(dims, dtype):
    return jax.ShapeDtypeStruct(dims, dtype)


def body(
    shards,
    replicas,
    tokens,
    cond,
    cot,
    w_mod,
    b_mod,
    w_qkv,
    b_qv,
    w_out,
    b_out,
    w_fc1,
    b_fc1,
    w_fc2,
    b_fc2,
):
    place = lax.axis_index("shard")
    core = lax.axis_index("replica") % 2
    rows, width = tokens.shape
    mod_rows = w_mod.shape[0]
    inner = w_fc1.shape[1]

    def half_of(weight):
        half = weight.shape[0] // 2
        return lax.dynamic_slice_in_dim(weight, core * half, half, 0)

    all_qkvo = Gather(jnp.concatenate([half_of(w_qkv), half_of(w_out)], 1), shards, replicas)
    all_fc1 = Gather(half_of(w_fc1), shards, replicas)
    all_fc2 = Gather(half_of(w_fc2), shards, replicas)
    cond_f = cond.astype(F32)
    cond_act = jax.nn.silu(cond_f).astype(BF16)
    biases = [b_qv, b_out, b_fc1, b_fc2]
    note = jnp.concatenate([cond_act[0]] + biases)[None]
    got = all_qkvo.send(1, all_qkvo.operands(1))
    came = [hop(note, "shard", shards, number) for number in range(1, shards)]
    got = gate(got, *came)
    all_qkvo.hold(1, got)
    notes = jnp.concatenate([note] + gate(came, *got), 0)
    group_cols = lax.dynamic_slice_in_dim(notes[:, :width], place * mod_rows, mod_rows, 1)
    partial = dot_nn(group_cols, w_mod)
    own_bias = lax.dynamic_update_slice(
        jnp.zeros((6 * width,), F32), b_mod.astype(F32), (place * b_mod.shape[0],)
    )
    partial = partial + own_bias
    def rest(gather, behind):
        for depth in range(2, gather.depths + 1):
            got = gather.send(depth, behind if depth == 2 else gather.operands(depth))
            if depth < gather.depths:
                gather.hold(depth, got)
        return got

    came = [hop(partial[number : number + 1], "shard", shards, number) for number in range(1, shards)]
    came, got = together(came, rest(all_qkvo, all_qkvo.operands(2)))
    all_qkvo.hold(all_qkvo.depths, got)
    mod = partial[0:1]
    for row in came:
        mod = mod + row
    bias_rows = xor_rows(gate([notes], mod)[0][:, width:].astype(F32), place)
    full_bias = []
    start = 0
    for piece in biases:
        full_bias.append(bias_rows[:, start : start + piece.shape[0]].reshape(1, -1))
        start += piece.shape[0]
    bias_qv, bias_out, bias_fc1, bias_fc2 = full_bias

    pieces_qkvo = all_qkvo.pieces()
    ahead = gate(all_fc1.operands(1), *got)
    got_fc1 = all_fc1.send(1, ahead)
    tokens_in = after(tokens, *ahead)

    pieces = piece_total(shards)
    sems = pltpu.SemaphoreType.DMA
    qkvo_scratch = [pltpu.VMEM((width, 4 * width), BF16)]
    fc1_scratch = [pltpu.VMEM((width, inner), BF16)]
    fc2_scratch = [pltpu.VMEM((inner, width), BF16)]
    half = mod_rows // 2
    half_inner = w_fc2.shape[0] // 2
    chunks = inner // width

    modul_a, qkv, attended, lse, branch_a, middle, modul_b = call(
        attend_kernel,
        shards,
        [tokens_in, mod, bias_qv, bias_out],
        [w_qkv, w_out] + pieces_qkvo,
        [
            shape((rows, width), BF16),
            shape((rows, 3 * width), BF16),
            shape((rows, width), BF16),
            shape((rows, 2 * HEAD), F32),
            shape((rows, width), F32),
            shape((rows, width), F32),
            shape((rows, width), BF16),
        ],
        [],
        qkvo_scratch + [sems((pieces + 2,))],
        10**11,
    )
    got_fc1, [modul_b, middle] = together(got_fc1, [modul_b, middle])
    all_fc1.hold(1, got_fc1)
    got = rest(all_fc1, all_fc1.operands(2))
    ahead = gate(all_fc2.operands(1), *got)
    all_fc1.hold(all_fc1.depths, got)
    pieces_fc1 = all_fc1.pieces()
    got_fc2 = all_fc2.send(1, ahead)
    hidden, slope, *outs = call(
        hidden_kernel,
        shards,
        [after(modul_b, *ahead), cot, mod, bias_fc1],
        [w_fc1] + pieces_fc1,
        [shape((rows, inner), BF16), shape((rows, inner), F32)],
        [shape((shards, half_inner, width), BF16)] * 2,
        fc1_scratch
        + [pltpu.VMEM((shards, 2 * half_inner, width), BF16)]
        + [sems((pieces + 1,)), sems((2 * shards,))],
        10**11,
    )
    got_fc2, [slope, *outs] = together(got_fc2, [slope, *outs])
    all_fc2.hold(1, got_fc2)
    all_fc2.hold(all_fc2.depths, rest(all_fc2, all_fc2.operands(2)))
    pieces_fc2 = all_fc2.pieces()
    red_fc2 = Reduction(outs[0], outs[1], shards, replicas, 1)
    red_fc2.swap()
    low_pre, sum_pre, *outs = call(
        pre_kernel,
        shards,
        [modul_b, cot, mod, slope],
        [w_fc2] + pieces_fc2,
        [shape((rows, inner), BF16), shape((1, inner), F32)],
        [shape((shards, half, inner), BF16)] * 2,
        fc2_scratch
        + fc1_scratch
        + [pltpu.VMEM((width, rows), BF16), sems((pieces + 1,)), sems((2 * shards * chunks,))],
        10**11,
    )
    [red_fc2.came], [low_pre, *outs] = together([red_fc2.came], [low_pre, *outs])
    red_fc1 = Reduction(outs[0], outs[1], shards, replicas, 1)
    red_fc1.swap()
    low_pre = after(low_pre, *red_fc2.ready(0))
    red_fc2.send(0)
    grad_middle, low_branch_a, sum_out, mods_b = call(
        middle_kernel,
        shards,
        [low_pre, cot, mod, middle, branch_a],
        [w_fc1] + pieces_fc1,
        [
            shape((rows, width), F32),
            shape((rows, width), BF16),
            shape((1, width), F32),
            shape((3, width), F32),
        ],
        [],
        fc1_scratch + [sems((pieces + 1,))],
        10**11,
    )
    got, [red_fc1.came], [low_branch_a] = together(
        red_fc2.flying, [red_fc1.came], [low_branch_a]
    )
    red_fc2.land(got)
    stages = len(red_fc2.bits)
    for stage in range(1, stages - 1):
        red_fc2.ready(stage)
        red_fc2.land(red_fc2.send(stage))
    low_branch_a = after(low_branch_a, *red_fc2.ready(stages - 1), *red_fc1.ready(0))
    red_fc2.send(stages - 1)
    red_fc1.send(0)
    low_proj, sum_proj, *outs = call(
        back_kernel,
        shards,
        [low_branch_a, modul_a, qkv, attended, lse],
        [w_qkv, w_out] + pieces_qkvo,
        [shape((rows, 3 * width), BF16), shape((1, 3 * width), F32)],
        [shape((shards, half, 4 * width), BF16)] * 2,
        qkvo_scratch
        + qkvo_scratch
        + [pltpu.VMEM((rows, width), BF16), pltpu.VMEM((width, rows), BF16)]
        + [sems((pieces + 2,)), sems((8 * shards,))],
        10**11,
    )
    got_2, got_1, [low_proj, *outs] = together(
        red_fc2.flying, red_fc1.flying, [low_proj, *outs]
    )
    red_fc2.land(got_2)
    red_fc1.land(got_1)
    red_qkvo = Reduction(outs[0], outs[1], shards, replicas, part_count(shards))
    red_qkvo.swap()
    for stage in range(1, stages - 1):
        red_fc1.ready(stage)
        red_fc1.land(red_fc1.send(stage))
    low_proj = after(low_proj, *red_qkvo.ready(0), *red_fc1.ready(stages - 1), *red_fc2.own())
    red_qkvo.send(0)
    red_fc1.send(stages - 1)
    red_fc2.fold(0)
    grad_tokens, mixed, news = call(
        last_kernel,
        shards,
        [low_proj, tokens, mod, grad_middle, hidden, middle, cot, bias_fc2]
        + [sum_proj, sum_out, sum_pre, mods_b],
        [w_qkv, w_out] + pieces_qkvo + [w_fc2] + pieces_fc2,
        [
            shape((rows, width), F32),
            shape((rows, width), BF16),
            shape((1, 6 * width + 3 * width + inner + width), BF16),
        ],
        [],
        qkvo_scratch + fc2_scratch + [sems((pieces + 2,)), sems((pieces + 1,))],
        10**11,
    )
    got_q, got_1, got_2, [news] = together(
        red_qkvo.flying, red_fc1.flying, red_fc2.flying, [news]
    )
    red_qkvo.land(got_q)
    red_fc1.land(got_1)
    red_fc2.folded(0, got_2)
    for stage in range(1, stages - 1):
        red_qkvo.ready(stage)
        red_qkvo.land(red_qkvo.send(stage))
    steps = red_fc2.rounds()
    count = -(-(shards + 2) // 8) * 8
    mod_span = 6 * width
    share_span = mod_span + 2 * 128 * -(-mod_rows // 256)
    share_steps = replicas.bit_length() - 1

    def mod_chain():
        held = [news]
        flip = 1
        while flip < shards:
            got = yield [(value, "shard", flip) for value in held]
            held += got
            flip *= 2
        *back, share = call(
            share_kernel,
            shards,
            held + [w_mod, group_cols],
            [],
            [shape((1, width), F32)] * shards + [shape((1, count, share_span), BF16)],
            [],
            [pltpu.VMEM((count, share_span), F32)],
            10**8,
        )
        rows = dict(enumerate(back))
        step = 0
        while step < share_steps:
            moving = [(share, "replica", replicas >> (step + 1))]
            half = shards >> (step + 1)
            if half:
                moving += [(rows[half + at], "shard", half) for at in range(half)]
            got = yield moving
            share = jnp.concatenate([share, got[0]], 0)
            for at in range(half):
                rows[at] = rows[at] + got[1 + at]
            step += 1
        while shards >> (step + 1):
            half = shards >> (step + 1)
            got = yield [(rows[half + at], "shard", half) for at in range(half)]
            for at in range(half):
                rows[at] = rows[at] + got[at]
            step += 1
        mod_chain.result = (share, rows[0])

    def send_on(moves):
        return [
            hop(value, axis, shards if axis == "shard" else replicas, flip)
            for value, axis, flip in moves
        ]

    at_1, at_2 = 1, min(2, steps)
    sent_1 = red_fc1.own() + red_fc2.values
    flying_1 = red_fc1.fold(0)
    flying_2 = red_fc2.fold(1) if steps > 1 else []
    red_qkvo.keep = after(red_qkvo.keep, *sent_1)
    sent_q = red_qkvo.ready(stages - 1)
    flying_q = red_qkvo.send(stages - 1)
    [news], flying_1, flying_2, _ = together([news], flying_1, flying_2, sent_q)
    red_fc1.folded(0, flying_1)
    if steps > 1:
        red_fc2.folded(1, flying_2)
    chain = mod_chain()
    moves = next(chain)
    at_q = -1
    while True:
        moves = list(moves)
        values = [value for value, _, _ in moves]
        lanes = [[], []]
        if at_1 < steps:
            lanes[0] = red_fc1.fold(at_1)
        if at_2 < steps:
            lanes[1] = red_fc2.fold(at_2)
        flying_m = send_on(moves)
        sent_b = values + red_fc1.values + red_fc2.values
        if at_q < steps:
            got = gate(flying_q, *sent_b)
            if at_q < 0:
                red_qkvo.land(got)
                red_qkvo.own()
            else:
                red_qkvo.folded(at_q, got)
            at_q += 1
            if at_q < steps:
                flying_q = red_qkvo.fold(at_q)
        lanes[0], lanes[1], flying_m, _ = together(
            lanes[0], lanes[1], flying_m, red_qkvo.values
        )
        if at_1 < steps:
            red_fc1.folded(at_1, lanes[0])
            at_1 += 1
        if at_2 < steps:
            red_fc2.folded(at_2, lanes[1])
            at_2 += 1
        try:
            moves = chain.send(flying_m) if chain else []
        except StopIteration:
            chain = None
            moves = []
        if chain is None and at_1 >= steps and at_2 >= steps and at_q >= steps:
            break
    share, grad_row = mod_chain.result
    _, silu_back = jax.vjp(jax.nn.silu, cond_f)
    grad_cond = silu_back(grad_row)[0]
    total_mod, total_b_mod, *bias_totals = call(
        total_kernel,
        shards,
        [share],
        [],
        [shape((mod_rows, mod_span), F32), shape((1, b_mod.shape[0]), F32)]
        + [shape((1, piece.shape[0]), F32) for piece in biases],
        [],
        [],
        10**8,
    )
    total_b_mod = total_b_mod.reshape(-1)
    bias_totals = [piece.reshape(-1) for piece in bias_totals]

    total_fc2 = red_fc2.finish()
    total_fc1 = red_fc1.finish()
    total_qkvo = red_qkvo.finish()
    return (
        mixed,
        grad_tokens,
        grad_cond,
        total_mod,
        total_b_mod,
        total_qkvo[:, : 3 * width],
        bias_totals[0],
        total_qkvo[:, 3 * width :],
        bias_totals[1],
        total_fc1,
        bias_totals[2],
        total_fc2,
        bias_totals[3],
    )


def solution(mesh):
    shards = mesh.shape["shard"]
    replicas = mesh.shape["replica"]
    both = P(("shard", "replica"), None)
    pairs = (P("shard", None), P("shard")) * 5

    def run(*args):
        return body(shards, replicas, *args)

    return jax.shard_map(
        run,
        mesh=mesh,
        in_specs=(both, both, both) + pairs,
        out_specs=(both, both, both) + pairs,
        check_vma=False,
    )
```

time: 376 us -> 274 us (0.73)
  local copies, waits for them, and re-layouts: 49.8 us -> 12.9 us
  starting transfers between devices: 100 us -> 67.3 us
  waiting for transfers between devices: 112 us -> 89.7 us
  other arithmetic: 41.4 us -> 33 us
    ppermute x84 -> x58, starting transfers between devices: 100 us -> 42.5 us  [hop(): return lax.ppermute(value, axis, [(at, at ^ flip) for at in range(size)])]
    ppermute x84 -> x58, waiting for transfers between devices: 112 us -> 54.7 us  [hop(): return lax.ppermute(value, axis, [(at, at ^ flip) for at in range(size)])]
    ppermute x0 -> x12, waiting for transfers between devices: none -> 35 us  [fold(): lax.ppermute(value, 'replica', pairs)]
    ppermute x0 -> x12, starting transfers between devices: none -> 24.8 us  [fold(): lax.ppermute(value, 'replica', pairs)]
    convert_element_type x7 -> x22, other arithmetic: 8 us -> 20.4 us  [the longest x9 13.3 us: ready(): self.sent = [self.total(at, stage).astype(BF16) for at in range(self.parts)]]
    unnamed x124 -> x111, local copies, waits for them, and re-layouts: 17 us -> 4.88 us
    slice x28 -> x8, local copies, waits for them, and re-layouts: 11.8 us -> 1.97 us  [the longest x6 1.91 us: operands(): found.append(source[:, at * span:(at + 1) * span])]
    another operation x18 -> x0, other arithmetic: 9.41 us -> none
  transfers between devices with their start and end apart: 84 -> 70, of which waited for: 26 -> 28; matrix products, arithmetic and copies ran while one was open for 23% -> 9% of each run, Pallas kernels for 18% -> 24%
where the time goes in v1:
time: 274 us; the launch traced here: 273 us
  waiting for transfers between devices  89.7 us (33%)
  Pallas kernels  68 us (25%)
  starting transfers between devices  67.3 us (25%)
  other arithmetic  33 us (12%)
  local copies, waits for them, and re-layouts  12.9 us (5%)
    pallas_call x8, Pallas kernels, call(): pl.pallas_call(functools.partial(kernel, shards), out_shape=outs + outsid...  68 us
    ppermute x58, waiting for transfers between devices, hop(): return lax.ppermute(value, axis, [(at, at ^ flip) for at in range(size)])  54.7 us
    ppermute x58, starting transfers between devices, hop(): return lax.ppermute(value, axis, [(at, at ^ flip) for at in range(size)])  42.5 us
    ppermute x12, waiting for transfers between devices, fold(): lax.ppermute(value, 'replica', pairs)  35 us
    ppermute x12, starting transfers between devices, fold(): lax.ppermute(value, 'replica', pairs)  24.8 us
    convert_element_type x9, other arithmetic, ready(): self.sent = [self.total(at, stage).astype(BF16) for at in range(self.parts)]  13.3 us
  transfers between devices with their start and end apart: 70, of which 28 were waited for; matrix products, arithmetic and copies ran while one was open for 9% of the time, Pallas kernels for 24%

profile of v1, /device:TPU:0, one launch (start us, length us, event | category | flops | bytes accessed | tf_op | source)
XLA Modules:
  0.0 272.9 jit_solution(10183901430898674218)
XLA Ops:
  2.8 3.0 %collective-permute-start.4 = (bf16[96,3072]{1,0:T(8,128)(2,1)S(1)}, bf16[96,3072]{1,0:T(8,128)(2,1)}, u32[]{:S(2)}, u32[]{:S(2)}) collective-permute-start(bf16[96,3072]{1,0:T(8,128)(2,1)S(1)} %pad_maximum_fusion.1), channel_id=1, source_target_pairs={{0,16},{8,24},{16,0},{24,8},{1,17},{9,25},{17,1},{25,9},{2,18},{10... | collective-permute-start | bytes 1769480 | tf_op jit(solution)/shard_map/ppermute | solution.py:42
  8.2 1.9 collective-permute-start.1
  11.7 9.0 %collective-permute-done.2 = bf16[1,2304]{1,0:T(2,128)(2,1)S(1)} collective-permute-done((bf16[1,2304]{1,0:T(2,128)(2,1)S(1)}, bf16[1,2304]{1,0:T(2,128)(2,1)S(1)}, u32[]{:S(2)}, u32[]{:S(2)}) %collective-permute-start.2) | collective-permute-done | bytes 4640 | tf_op jit(solution)/shard_map/ppermute | solution.py:42
  24.2 2.4 collective-permute-start.7
  31.3 3.8 %collective-permute-done.8.refs_8_.refs_9_.refs_16_ = bf16[96,1536]{1,0:T(8,128)(2,1)S(1)} collective-permute-done((bf16[96,1536]{1,0:T(8,128)(2,1)}, bf16[96,1536]{1,0:T(8,128)(2,1)S(1)}, u32[]{:S(2)}, u32[]{:S(2)}) %collective-permute-start.8) | collective-permute-done | bytes 294944 | tf_op jit(solution)/shard_map/ppermute | solution.py:42
  42.0 9.9 %shard_map.228 = (bf16[256,768]{1,0:T(8,128)(2,1)}, bf16[256,2304]{1,0:T(8,128)(2,1)}, bf16[256,768]{1,0:T(8,128)(2,1)}, f32[256,128]{1,0:T(8,128)}, f32[256,768...) custom-call(bf16[256,768]{1,0:T(8,128)(2,1)} %refs_1_.7, f32[1,4608]{1,0:T(1,128)} %fusion.9.refs_1_.refs_2_, ...), custom_call_target="tpu_custom_call" | custom-call | flops 99999997952 | bytes 9202688 | tf_op jit(solution)/shard_map/pallas_call | solution.py:642
  53.3 3.0 %collective-permute-done.10.refs_5_.refs_6_ = bf16[96,3072]{1,0:T(8,128)(2,1)S(1)} collective-permute-done((bf16[96,3072]{1,0:T(8,128)(2,1)S(1)}, bf16[96,3072]{1,0:T(8,128)(2,1)S(1)}, u32[]{:S(2)}, u32[]{:S(2)}) %collective-permute-start.10) | collective-permute-done | bytes 589856 | tf_op jit(solution)/shard_map/ppermute | solution.py:42
  58.3 5.9 %collective-permute-done.17.refs_8_.refs_9_ = bf16[96,1536]{1,0:T(8,128)(2,1)S(1)} collective-permute-done((bf16[96,1536]{1,0:T(8,128)(2,1)S(1)}, bf16[96,1536]{1,0:T(8,128)(2,1)S(1)}, u32[]{:S(2)}, u32[]{:S(2)}) %collective-permute-start.17) | collective-permute-done | bytes 294944 | tf_op jit(solution)/shard_map/ppermute | solution.py:42
  68.2 11.3 %shard_map.229 = (bf16[256,3072]{1,0:T(8,128)(2,1)}, f32[256,3072]{1,0:T(8,128)}, bf16[4,384,768]{2,1,0:T(8,128)(2,1)}, bf16[4,384,768]{2,1,0:T(8,128)(2,1)}) custom-call(bf16[256,768]{1,0:T(8,128)(2,1)} %get-tuple-element.141.refs_0_, bf16[256,768]{1,0:T(8,128)(2,1)} %refs_6_.3, f32[1,4608]{1,0:T(1,128)} %fusion.9.refs_1_.refs_2_, f32[1,3072]{1,0:T(1,128)} %bitcast.119, ...), custom_call_target="tpu_custom_call" | custom-call | flops 99999997952 | bytes 14972928 | tf_op jit(solution)/shard_map/pallas_call | solution.py:642
  79.5 1.8 collective-permute-done.19.refs_6_.refs_24_
  84.4 6.4 %collective-permute-done.25.refs_7_.refs_25_ = bf16[384,384]{1,0:T(8,128)(2,1)S(1)} collective-permute-done((bf16[384,384]{1,0:T(8,128)(2,1)S(1)}, bf16[384,384]{1,0:T(8,128)(2,1)S(1)}, u32[]{:S(2)}, u32[]{:S(2)}) %collective-permute-start.25) | collective-permute-done | bytes 294944 | tf_op jit(solution)/shard_map/ppermute | solution.py:42
  94.6 9.8 %shard_map.230 = (bf16[256,3072]{1,0:T(8,128)(2,1)}, f32[1,3072]{1,0:T(1,128)}, bf16[4,96,3072]{2,1,0:T(8,128)(2,1)}, bf16[4,96,3072]{2,1,0:T(8,128)(2,1)}) custom-call(bf16[256,768]{1,0:T(8,128)(2,1)} %get-tuple-element.141.refs_0_, bf16[256,768]{1,0:T(8,128)(2,1)} %refs_6_.3, f32[1,4608]{1,0:T(1,128)} %fusion.9.refs_1_.refs_2_, ...), custom_call_target="tpu_custom_call" | custom-call | flops 99999997952 | bytes 14972928 | tf_op jit(solution)/shard_map/pallas_call | solution.py:642
  109.0 7.3 %shard_map.231 = (f32[256,768]{1,0:T(8,128)}, bf16[256,768]{1,0:T(8,128)(2,1)}, f32[1,768]{1,0:T(1,128)}, f32[3,768]{1,0:T(4,128)}) custom-call(bf16[256,3072]{1,0:T(8,128)(2,1)} %get-tuple-element.156.refs_0_, bf16[256,768]{1,0:T(8,128)(2,1)} %refs_6_.3, f32[1,4608]{1,0:T(1,128)} %fusion.9.refs_1_.refs_2_, f32[256,768]{1,0:T(8,128)} %get-tuple-element.157.refs_3_.refs_5_, ...), custom_call_target="tpu_custom_call" | custom-call | flops 99999997952 | bytes 9467904 | tf_op jit(solution)/shard_map/pallas_call | solution.py:642
  116.3 5.8 %collective-permute-done.31 = bf16[2,384,384]{2,1,0:T(8,128)(2,1)S(1)} collective-permute-done((bf16[2,384,384]{2,1,0:T(8,128)(2,1)}, bf16[2,384,384]{2,1,0:T(8,128)(2,1)S(1)}, u32[]{:S(2)}, u32[]{:S(2)}) %collective-permute-start.31) | collective-permute-done | bytes 589856 | tf_op jit(solution)/shard_map/ppermute | solution.py:42
  126.0 2.1 add_convert_fusion.24
  132.1 12.9 %shard_map.232 = (bf16[256,2304]{1,0:T(8,128)(2,1)}, f32[1,2304]{1,0:T(1,128)}, bf16[4,96,3072]{2,1,0:T(8,128)(2,1)}, bf16[4,96,3072]{2,1,0:T(8,128)(2,1)}) custom-call(bf16[256,768]{1,0:T(8,128)(2,1)} %get-tuple-element.165.refs_0_, bf16[256,768]{1,0:T(8,128)(2,1)} %get-tuple-element.166.refs_1_, bf16[256,2304]{1,0:T(8,128)(2,1)} %get-tuple-element.167.refs_2_, ...), custom_call_target="tpu_custom_call" | custom-call | flops 99999997952 | bytes 13116416 | tf_op jit(solution)/shard_map/pallas_call | solution.py:642
  145.0 4.2 %collective-permute-done.36 = bf16[2,96,1536]{2,1,0:T(8,128)(2,1)S(1)} collective-permute-done((bf16[2,96,1536]{2,1,0:T(8,128)(2,1)}, bf16[2,96,1536]{2,1,0:T(8,128)(2,1)S(1)}, u32[]{:S(2)}, u32[]{:S(2)}) %collective-permute-start.36) | collective-permute-done | bytes 589856 | tf_op jit(solution)/shard_map/ppermute | solution.py:42
  150.0 2.2 add_convert_fusion.22
  156.0 3.5 %collective-permute-start.43 = (bf16[384,768]{1,0:T(8,128)(2,1)S(1)}, bf16[384,768]{1,0:T(8,128)(2,1)S(1)}, u32[]{:S(2)}, u32[]{:S(2)}) collective-permute-start(bf16[384,768]{1,0:T(8,128)(2,1)S(1)} %pad_maximum_fusion.2), channel_id=1, source_target_pairs={{0,2},{1,3},{6,4},{7,5},{8,10},{9,11},{14,12},{15,13},{16,18},{17,... | collective-permute-start | bytes 1769480 | tf_op jit(solution)/shard_map/ppermute | solution.py:215
  164.1 10.4 %shard_map.233 = (f32[256,768]{1,0:T(8,128)}, bf16[256,768]{1,0:T(8,128)(2,1)}, bf16[1,10752]{1,0:T(2,128)(2,1)}) custom-call(bf16[256,2304]{1,0:T(8,128)(2,1)} %get-tuple-element.180.refs_0_, bf16[256,768]{1,0:T(8,128)(2,1)} %refs_1_.7, f32[1,4608]{1,0:T(1,128)} %fusion.9.refs_1_.refs_2_, f32[256,768]{1,0:T(8,128)} %get-tuple-element.181.refs_3_, ...), custom_call_target="tpu_custom_call" | custom-call | flops 99999997952 | bytes 15805440 | tf_op jit(solution)/shard_map/pallas_call | solution.py:642
  174.5 2.4 collective-permute-done.39
  182.1 2.1 add_convert_fusion.16
  185.6 7.7 %collective-permute-done.44 = bf16[96,3072]{1,0:T(8,128)(2,1)S(1)} collective-permute-done((bf16[96,3072]{1,0:T(8,128)(2,1)S(1)}, bf16[96,3072]{1,0:T(8,128)(2,1)S(1)}, u32[]{:S(2)}, u32[]{:S(2)}) %collective-permute-start.44) | collective-permute-done | bytes 589856 | tf_op jit(solution)/shard_map/ppermute | solution.py:215
  199.1 8.6 %collective-permute-start.55 = (bf16[96,1536]{1,0:T(8,128)(2,1)S(1)}, bf16[96,1536]{1,0:T(8,128)(2,1)S(1)}, u32[]{:S(2)}, u32[]{:S(2)}) collective-permute-start(bf16[96,1536]{1,0:T(8,128)(2,1)S(1)} %get-tuple-element.233), channel_id=1, source_target_pairs={{0,2},{1,3},{6,4},{7,5},{8,10},{9,11},{14,12},{15,13},{16,18},{17,... | collective-permute-start | bytes 884744 | tf_op jit(solution)/shard_map/ppermute | solution.py:215
  207.7 2.1 collective-permute-start.54
  215.9 1.9 collective-permute-done.54
  219.6 12.8 %collective-permute-done.51 = bf16[96,3072]{1,0:T(8,128)(2,1)S(1)} collective-permute-done((bf16[96,3072]{1,0:T(8,128)(2,1)S(1)}, bf16[96,3072]{1,0:T(8,128)(2,1)S(1)}, u32[]{:S(2)}, u32[]{:S(2)}) %collective-permute-start.51) | collective-permute-done | bytes 589856 | tf_op jit(solution)/shard_map/ppermute | solution.py:215
  232.5 2.9 %shard_map.234 = (f32[1,768]{1,0:T(1,128)}, f32[1,768]{1,0:T(1,128)}, f32[1,768]{1,0:T(1,128)}, f32[1,768]{1,0:T(1,128)}, bf16[1,8,4864]{2,1,0:T(8,128)(2,1)}) custom-call(bf16[1,10752]{1,0:T(2,128)(2,1)} %get-tuple-element.197.refs_0_, bf16[1,10752]{1,0:T(2,128)(2,1)} %copy-done.28, bf16[1,10752]{1,0:T(2,128)(2,1)} %copy-done.27, ...), custom_call_target="tpu_custom_call" | custom-call | flops 100000000 | bytes 1947136 | tf_op jit(solution)/shard_map/pallas_call | solution.py:642
  245.2 4.7 %collective-permute-done.64 = bf16[96,1536]{1,0:T(8,128)(2,1)S(1)} collective-permute-done((bf16[96,1536]{1,0:T(8,128)(2,1)S(1)}, bf16[96,1536]{1,0:T(8,128)(2,1)S(1)}, u32[]{:S(2)}, u32[]{:S(2)}) %collective-permute-start.64) | collective-permute-done | bytes 294944 | tf_op jit(solution)/shard_map/ppermute | solution.py:215
  249.9 6.3 %collective-permute-done.63 = bf16[96,1536]{1,0:T(8,128)(2,1)S(1)} collective-permute-done((bf16[96,1536]{1,0:T(8,128)(2,1)S(1)}, bf16[96,1536]{1,0:T(8,128)(2,1)S(1)}, u32[]{:S(2)}, u32[]{:S(2)}) %collective-permute-start.63) | collective-permute-done | bytes 294944 | tf_op jit(solution)/shard_map/ppermute | solution.py:215
  256.8 2.6 collective-permute-done.61
  265.5 3.5 %shard_map.235 = (f32[192,4608]{1,0:T(8,128)}, f32[1,1152]{1,0:T(1,128)}, f32[1,384]{1,0:T(1,128)}, f32[1,192]{1,0:T(1,128)}, f32[1,768]{1,0:T(1,128)}, /*index=5*/f32[1,192]{1,0:T(1,128)}) custom-call(bf16[8,8,4864]{2,1,0:T(8,128)(2,1)} %pad_maximum_fusion.refs_0_), custom_call_target="tpu_custom_call" | custom-call | flops 100000000 | bytes 4172288 | tf_op jit(solution)/shard_map/pallas_call | solution.py:642
  (302 shorter events, 96.9 us)
Async XLA Ops:
  2.8 18.2 %collective-permute-start.4 = (bf16[96,3072]{1,0:T(8,128)(2,1)S(1)}, bf16[96,3072]{1,0:T(8,128)(2,1)}, u32[]{:S(2)}, u32[]{:S(2)}) collective-permute-start(bf16[96,3072]{1,0:T(8,128)(2,1)S(1)} %pad_maximum_fusion.1), channel_id=1, source_target_pairs={{0,16},{8,24},{16,0},{24,8},{1,17},{9,25},{17,1},{25,9},{2,18},{10... | collective-permute-start | bytes 1769480 | tf_op jit(solution)/shard_map/ppermute | solution.py:42
  5.8 15.2 %collective-permute-start.3 = (bf16[96,3072]{1,0:T(8,128)(2,1)S(1)}, bf16[96,3072]{1,0:T(8,128)(2,1)S(1)}, u32[]{:S(2)}, u32[]{:S(2)}) collective-permute-start(bf16[96,3072]{1,0:T(8,128)(2,1)S(1)} %pad_maximum_fusion.1), channel_id=1, source_target_pairs={{0,8},{8,0},{16,24},{24,16},{1,9},{9,1},{17,25},{25,17},{2,10},{10... | collective-permute-start | bytes 1769480 | tf_op jit(solution)/shard_map/ppermute | solution.py:42
  37.9 15.4 %collective-permute-start.11 = (bf16[96,3072]{1,0:T(8,128)(2,1)S(1)}, bf16[96,3072]{1,0:T(8,128)(2,1)S(1)}, u32[]{:S(2)}, u32[]{:S(2)}) collective-permute-start(bf16[96,3072]{1,0:T(8,128)(2,1)S(1)} %constant_dynamic-slice_fusion.3), channel_id=1, source_target_pairs={{0,16},{8,24},{16,0},{24,8},{1,17},{9,25},{17,1},{25,9},{2,18},{10... | collective-permute-start | bytes 1769480 | tf_op jit(solution)/shard_map/ppermute | solution.py:42
  41.3 15.0 %collective-permute-start.10 = (bf16[96,3072]{1,0:T(8,128)(2,1)S(1)}, bf16[96,3072]{1,0:T(8,128)(2,1)S(1)}, u32[]{:S(2)}, u32[]{:S(2)}) collective-permute-start(bf16[96,3072]{1,0:T(8,128)(2,1)S(1)} %constant_dynamic-slice_fusion.3), channel_id=1, source_target_pairs={{0,8},{8,0},{16,24},{24,16},{1,9},{9,1},{17,25},{25,17},{2,10},{10... | collective-permute-start | bytes 1769480 | tf_op jit(solution)/shard_map/ppermute | solution.py:42
  65.5 15.7 %collective-permute-start.19 = (bf16[384,768]{1,0:T(8,128)(2,1)S(1)}, bf16[384,768]{1,0:T(8,128)(2,1)S(1)}, u32[]{:S(2)}, u32[]{:S(2)}) collective-permute-start(bf16[384,768]{1,0:T(8,128)(2,1)S(1)} %constant_dynamic-slice_fusion.4), channel_id=1, source_target_pairs={{0,16},{8,24},{16,0},{24,8},{1,17},{9,25},{17,1},{25,9},{2,18},{10... | collective-permute-start | bytes 1769480 | tf_op jit(solution)/shard_map/ppermute | solution.py:42
  66.9 15.5 %collective-permute-start.18 = (bf16[384,768]{1,0:T(8,128)(2,1)S(1)}, bf16[384,768]{1,0:T(8,128)(2,1)S(1)}, u32[]{:S(2)}, u32[]{:S(2)}) collective-permute-start(bf16[384,768]{1,0:T(8,128)(2,1)S(1)} %constant_dynamic-slice_fusion.4), channel_id=1, source_target_pairs={{0,8},{8,0},{16,24},{24,16},{1,9},{9,1},{17,25},{25,17},{2,10},{10... | collective-permute-start | bytes 1769480 | tf_op jit(solution)/shard_map/ppermute | solution.py:42
  91.3 13.0 %collective-permute-start.24 = (bf16[4,384,768]{2,1,0:T(8,128)(2,1)}, bf16[4,384,768]{2,1,0:T(8,128)(2,1)S(1)}, u32[]{:S(2)}, u32[]{:S(2)}) collective-permute-start(bf16[4,384,768]{2,1,0:T(8,128)(2,1)} %get-tuple-element.146), channel_id=1, source_target_pairs={{0,1},{1,0},{2,3},{3,2},{4,5},{5,4},{6,7},{7,6},{8,9},{9,8},{10,11... | collective-permute-start | bytes 7077896 | tf_op jit(solution)/shard_map/ppermute | solution.py:42
  106.5 15.7 %collective-permute-start.31 = (bf16[2,384,384]{2,1,0:T(8,128)(2,1)}, bf16[2,384,384]{2,1,0:T(8,128)(2,1)S(1)}, u32[]{:S(2)}, u32[]{:S(2)}) collective-permute-start(bf16[2,384,384]{2,1,0:T(8,128)(2,1)} %bitcast.2), channel_id=1, source_target_pairs={{0,8},{8,0},{16,24},{24,16},{1,9},{9,1},{17,25},{25,17},{2,10},{10... | collective-permute-start | bytes 1769480 | tf_op jit(solution)/shard_map/ppermute | solution.py:42
  108.3 15.3 %collective-permute-start.32 = (bf16[2,384,384]{2,1,0:T(8,128)(2,1)}, bf16[2,384,384]{2,1,0:T(8,128)(2,1)S(1)}, u32[]{:S(2)}, u32[]{:S(2)}) collective-permute-start(bf16[2,384,384]{2,1,0:T(8,128)(2,1)} %bitcast.4), channel_id=1, source_target_pairs={{0,16},{8,24},{16,0},{24,8},{1,17},{9,25},{17,1},{25,9},{2,18},{10... | collective-permute-start | bytes 1769480 | tf_op jit(solution)/shard_map/ppermute | solution.py:42
  109.0 14.6 %collective-permute-start.33 = (bf16[4,96,3072]{2,1,0:T(8,128)(2,1)}, bf16[4,96,3072]{2,1,0:T(8,128)(2,1)S(1)}, u32[]{:S(2)}, u32[]{:S(2)}) collective-permute-start(bf16[4,96,3072]{2,1,0:T(8,128)(2,1)} %get-tuple-element.154), channel_id=1, source_target_pairs={{0,1},{1,0},{2,3},{3,2},{4,5},{5,4},{6,7},{7,6},{8,9},{9,8},{10,11... | collective-permute-start | bytes 7077896 | tf_op jit(solution)/shard_map/ppermute | solution.py:42
  128.1 16.9 %collective-permute-start.34 = (bf16[1,384,384]{2,1,0:T(8,128)(2,1)}, bf16[1,384,384]{2,1,0:T(8,128)(2,1)S(1)}, u32[]{:S(2)}, u32[]{:S(2)}) collective-permute-start(bf16[1,384,384]{2,1,0:T(8,128)(2,1)} %bitcast.6), channel_id=1, source_target_pairs={{0,16},{8,24},{16,0},{24,8},{1,17},{9,25},{17,1},{25,9},{2,18},{10... | collective-permute-start | bytes 884744 | tf_op jit(solution)/shard_map/ppermute | solution.py:42
  128.7 16.3 %collective-permute-start.35 = (bf16[1,384,384]{2,1,0:T(8,128)(2,1)}, bf16[1,384,384]{2,1,0:T(8,128)(2,1)S(1)}, u32[]{:S(2)}, u32[]{:S(2)}) collective-permute-start(bf16[1,384,384]{2,1,0:T(8,128)(2,1)} %bitcast.8), channel_id=1, source_target_pairs={{0,8},{8,0},{16,24},{24,16},{1,9},{9,1},{17,25},{25,17},{2,10},{10... | collective-permute-start | bytes 884744 | tf_op jit(solution)/shard_map/ppermute | solution.py:42
  129.1 20.2 %collective-permute-start.36 = (bf16[2,96,1536]{2,1,0:T(8,128)(2,1)}, bf16[2,96,1536]{2,1,0:T(8,128)(2,1)S(1)}, u32[]{:S(2)}, u32[]{:S(2)}) collective-permute-start(bf16[2,96,1536]{2,1,0:T(8,128)(2,1)} %bitcast.12), channel_id=1, source_target_pairs={{0,8},{8,0},{16,24},{24,16},{1,9},{9,1},{17,25},{25,17},{2,10},{10... | collective-permute-start | bytes 1769480 | tf_op jit(solution)/shard_map/ppermute | solution.py:42
  130.8 18.4 %collective-permute-start.37 = (bf16[2,96,1536]{2,1,0:T(8,128)(2,1)}, bf16[2,96,1536]{2,1,0:T(8,128)(2,1)S(1)}, u32[]{:S(2)}, u32[]{:S(2)}) collective-permute-start(bf16[2,96,1536]{2,1,0:T(8,128)(2,1)} %bitcast.14), channel_id=1, source_target_pairs={{0,16},{8,24},{16,0},{24,8},{1,17},{9,25},{17,1},{25,9},{2,18},{10... | collective-permute-start | bytes 1769480 | tf_op jit(solution)/shard_map/ppermute | solution.py:42
  152.2 22.3 %collective-permute-start.41 = (bf16[1,96,1536]{2,1,0:T(8,128)(2,1)}, bf16[1,96,1536]{2,1,0:T(8,128)(2,1)S(1)}, u32[]{:S(2)}, u32[]{:S(2)}) collective-permute-start(bf16[1,96,1536]{2,1,0:T(8,128)(2,1)} %bitcast.24), channel_id=1, source_target_pairs={{0,16},{8,24},{16,0},{24,8},{1,17},{9,25},{17,1},{25,9},{2,18},{10... | collective-permute-start | bytes 884744 | tf_op jit(solution)/shard_map/ppermute | solution.py:42
  153.6 20.9 %collective-permute-start.42 = (bf16[1,96,1536]{2,1,0:T(8,128)(2,1)}, bf16[1,96,1536]{2,1,0:T(8,128)(2,1)S(1)}, u32[]{:S(2)}, u32[]{:S(2)}) collective-permute-start(bf16[1,96,1536]{2,1,0:T(8,128)(2,1)} %bitcast.26), channel_id=1, source_target_pairs={{0,8},{8,0},{16,24},{24,16},{1,9},{9,1},{17,25},{25,17},{2,10},{10... | collective-permute-start | bytes 884744 | tf_op jit(solution)/shard_map/ppermute | solution.py:42
  156.0 18.5 %collective-permute-start.43 = (bf16[384,768]{1,0:T(8,128)(2,1)S(1)}, bf16[384,768]{1,0:T(8,128)(2,1)S(1)}, u32[]{:S(2)}, u32[]{:S(2)}) collective-permute-start(bf16[384,768]{1,0:T(8,128)(2,1)S(1)} %pad_maximum_fusion.2), channel_id=1, source_target_pairs={{0,2},{1,3},{6,4},{7,5},{8,10},{9,11},{14,12},{15,13},{16,18},{17,... | collective-permute-start | bytes 1769480 | tf_op jit(solution)/shard_map/ppermute | solution.py:215
  162.0 14.9 %collective-permute-start.39 = (bf16[2,96,1536]{2,1,0:T(8,128)(2,1)S(1)}, bf16[2,96,1536]{2,1,0:T(8,128)(2,1)S(1)}, u32[]{:S(2)}, u32[]{:S(2)}) collective-permute-start(bf16[2,96,1536]{2,1,0:T(8,128)(2,1)S(1)} %bitcast.114), channel_id=1, source_target_pairs={{0,8},{8,0},{16,24},{24,16},{1,9},{9,1},{17,25},{25,17},{2,10},{10... | collective-permute-start | bytes 1769480 | tf_op jit(solution)/shard_map/ppermute | solution.py:42
  163.4 14.6 %collective-permute-start.40 = (bf16[2,96,1536]{2,1,0:T(8,128)(2,1)S(1)}, bf16[2,96,1536]{2,1,0:T(8,128)(2,1)S(1)}, u32[]{:S(2)}, u32[]{:S(2)}) collective-permute-start(bf16[2,96,1536]{2,1,0:T(8,128)(2,1)S(1)} %bitcast.113), channel_id=1, source_target_pairs={{0,16},{8,24},{16,0},{24,8},{1,17},{9,25},{17,1},{25,9},{2,18},{10... | collective-permute-start | bytes 1769480 | tf_op jit(solution)/shard_map/ppermute | solution.py:42
  179.8 13.5 %collective-permute-start.44 = (bf16[96,3072]{1,0:T(8,128)(2,1)S(1)}, bf16[96,3072]{1,0:T(8,128)(2,1)S(1)}, u32[]{:S(2)}, u32[]{:S(2)}) collective-permute-start(bf16[96,3072]{1,0:T(8,128)(2,1)S(1)} %pad_maximum_fusion.3), channel_id=1, source_target_pairs={{0,2},{1,3},{6,4},{7,5},{8,10},{9,11},{14,12},{15,13},{16,18},{17,... | collective-permute-start | bytes 1769480 | tf_op jit(solution)/shard_map/ppermute | solution.py:215
  193.7 17.0 %collective-permute-start.47 = (bf16[384,768]{1,0:T(8,128)(2,1)S(1)}, bf16[384,768]{1,0:T(8,128)(2,1)}, u32[]{:S(2)}, u32[]{:S(2)}) collective-permute-start(bf16[384,768]{1,0:T(8,128)(2,1)S(1)} %add_convert_fusion.1), channel_id=1, source_target_pairs={{2,0},{3,1},{4,6},{5,7},{10,8},{11,9},{12,14},{13,15},{18,16},{19,... | collective-permute-start | bytes 1769480 | tf_op jit(solution)/shard_map/ppermute | solution.py:215
  195.0 15.7 %collective-permute-start.46 = (bf16[96,3072]{1,0:T(8,128)(2,1)S(1)}, bf16[96,3072]{1,0:T(8,128)(2,1)}, u32[]{:S(2)}, u32[]{:S(2)}) collective-permute-start(bf16[96,3072]{1,0:T(8,128)(2,1)S(1)} %add_convert_fusion.2), channel_id=1, source_target_pairs={{2,4},{3,5},{4,2},{5,3},{10,12},{11,13},{12,10},{13,11},{18,20},{1... | collective-permute-start | bytes 1769480 | tf_op jit(solution)/shard_map/ppermute | solution.py:215
  196.5 22.1 %collective-permute-start.52 = (bf16[1,10752]{1,0:T(2,128)(2,1)}, bf16[1,10752]{1,0:T(2,128)(2,1)S(1)}, u32[]{:S(2)}, u32[]{:S(2)}) collective-permute-start(bf16[1,10752]{1,0:T(2,128)(2,1)} %get-tuple-element.197.refs_0_), channel_id=1, source_target_pairs={{0,16},{8,24},{16,0},{24,8},{1,17},{9,25},{17,1},{25,9},{2,18},{10... | collective-permute-start | bytes 64520 | tf_op jit(solution)/shard_map/ppermute | solution.py:42
  199.1 15.5 %collective-permute-start.55 = (bf16[96,1536]{1,0:T(8,128)(2,1)S(1)}, bf16[96,1536]{1,0:T(8,128)(2,1)S(1)}, u32[]{:S(2)}, u32[]{:S(2)}) collective-permute-start(bf16[96,1536]{1,0:T(8,128)(2,1)S(1)} %get-tuple-element.233), channel_id=1, source_target_pairs={{0,2},{1,3},{6,4},{7,5},{8,10},{9,11},{14,12},{15,13},{16,18},{17,... | collective-permute-start | bytes 884744 | tf_op jit(solution)/shard_map/ppermute | solution.py:215
  213.8 24.3 %collective-permute-start.69 = (bf16[384,768]{1,0:T(8,128)(2,1)S(1)}, bf16[384,768]{1,0:T(8,128)(2,1)S(1)}, u32[]{:S(2)}, u32[]{:S(2)}) collective-permute-start(bf16[384,768]{1,0:T(8,128)(2,1)S(1)} %broadcast_select_fusion.1), channel_id=1, source_target_pairs={{0,1},{1,0},{2,3},{3,2},{4,5},{5,4},{6,7},{7,6},{8,9},{9,8},{10,11... | collective-permute-start | bytes 1769480 | tf_op jit(solution)/shard_map/ppermute | solution.py:42
  214.6 17.8 %collective-permute-start.51 = (bf16[96,3072]{1,0:T(8,128)(2,1)S(1)}, bf16[96,3072]{1,0:T(8,128)(2,1)S(1)}, u32[]{:S(2)}, u32[]{:S(2)}) collective-permute-start(bf16[96,3072]{1,0:T(8,128)(2,1)S(1)} %add_convert_fusion), channel_id=1, source_target_pairs={{2,0},{3,1},{4,6},{5,7},{10,8},{11,9},{12,14},{13,15},{18,16},{19,... | collective-permute-start | bytes 1769480 | tf_op jit(solution)/shard_map/ppermute | solution.py:215
  217.9 19.5 %collective-permute-start.60 = (bf16[96,1536]{1,0:T(8,128)(2,1)S(1)}, bf16[96,1536]{1,0:T(8,128)(2,1)S(1)}, u32[]{:S(2)}, u32[]{:S(2)}) collective-permute-start(bf16[96,1536]{1,0:T(8,128)(2,1)S(1)} %add_convert_fusion.12), channel_id=1, source_target_pairs={{2,4},{3,5},{4,2},{5,3},{10,12},{11,13},{12,10},{13,11},{18,20},{1... | collective-permute-start | bytes 884744 | tf_op jit(solution)/shard_map/ppermute | solution.py:215
  218.6 19.2 %collective-permute-start.59 = (bf16[96,1536]{1,0:T(8,128)(2,1)S(1)}, bf16[96,1536]{1,0:T(8,128)(2,1)S(1)}, u32[]{:S(2)}, u32[]{:S(2)}) collective-permute-start(bf16[96,1536]{1,0:T(8,128)(2,1)S(1)} %add_convert_fusion.13), channel_id=1, source_target_pairs={{2,4},{3,5},{4,2},{5,3},{10,12},{11,13},{12,10},{13,11},{18,20},{1... | collective-permute-start | bytes 884744 | tf_op jit(solution)/shard_map/ppermute | solution.py:215
  237.9 25.1 %collective-permute-start.68 = (bf16[96,3072]{1,0:T(8,128)(2,1)S(1)}, bf16[96,3072]{1,0:T(8,128)(2,1)S(1)}, u32[]{:S(2)}, u32[]{:S(2)}) collective-permute-start(bf16[96,3072]{1,0:T(8,128)(2,1)S(1)} %broadcast_select_fusion), channel_id=1, source_target_pairs={{0,1},{1,0},{2,3},{3,2},{4,5},{5,4},{6,7},{7,6},{8,9},{9,8},{10,11... | collective-permute-start | bytes 1769480 | tf_op jit(solution)/shard_map/ppermute | solution.py:42
  241.0 15.2 %collective-permute-start.63 = (bf16[96,1536]{1,0:T(8,128)(2,1)S(1)}, bf16[96,1536]{1,0:T(8,128)(2,1)S(1)}, u32[]{:S(2)}, u32[]{:S(2)}) collective-permute-start(bf16[96,1536]{1,0:T(8,128)(2,1)S(1)} %add_convert_fusion.11), channel_id=1, source_target_pairs={{2,0},{3,1},{4,6},{5,7},{10,8},{11,9},{12,14},{13,15},{18,16},{19,... | collective-permute-start | bytes 884744 | tf_op jit(solution)/shard_map/ppermute | solution.py:215
  243.6 13.3 %collective-permute-start.62 = (f32[1,768]{1,0:T(1,128)S(1)}, f32[1,768]{1,0:T(1,128)S(1)}, u32[]{:S(2)}, u32[]{:S(2)}) collective-permute-start(f32[1,768]{1,0:T(1,128)S(1)} %add.245), channel_id=1, source_target_pairs={{0,8},{8,0},{16,24},{24,16},{1,9},{9,1},{17,25},{25,17},{2,10},{10... | collective-permute-start | bytes 9224 | tf_op jit(solution)/shard_map/ppermute | solution.py:42
  243.7 15.8 %collective-permute-start.61 = (bf16[2,8,4864]{2,1,0:T(8,128)(2,1)S(1)}, bf16[2,8,4864]{2,1,0:T(8,128)(2,1)S(1)}, u32[]{:S(2)}, u32[]{:S(2)}) collective-permute-start(bf16[2,8,4864]{2,1,0:T(8,128)(2,1)S(1)} %constant_dynamic-update-slice_fusion), channel_id=1, source_target_pairs={{0,2},{1,3},{2,0},{3,1},{4,6},{5,7},{6,4},{7,5},{8,10},{9,11},{10,... | collective-permute-start | bytes 466952 | tf_op jit(solution)/shard_map/ppermute | solution.py:42
  (91 other events, 654.4 us)

commit v2 on v1

--- a/solution.py
+++ b/solution.py
@@ -534,38 +534,41 @@
     wait_all(outs)
 
 
-def last_kernel(shards, *refs):
+def tokens_kernel(shards, *refs):
     refs = list(refs)
-    low_proj, tokens, mod, grad_middle, hidden, middle, cot, bias_fc2 = take(refs, 8)
-    sum_proj, sum_out, sum_pre, mods_b = take(refs, 4)
-    own_qkvo = take(refs, 2)
-    pieces_qkvo = take(refs, piece_total(shards))
-    own_fc2 = take(refs, 1)
-    pieces_fc2 = take(refs, piece_total(shards))
-    grad_tokens, mixed, news = take(refs, 3)
-    w_qkvo, w_fc2, sems_qkvo, sems_fc2 = refs
+    low_proj, tokens, mod, grad_middle = take(refs, 4)
+    own = take(refs, 2)
+    pieces = take(refs, piece_total(shards))
+    grad_tokens, grad_mods = take(refs, 2)
+    weight, sems = refs
     rows, width = tokens.shape
-    copies_qkvo = start_fetch(own_qkvo, pieces_qkvo, w_qkvo, sems_qkvo, shards)
-    copies_fc2 = start_fetch(own_fc2, pieces_fc2, w_fc2, sems_fc2, shards)
-    mod_val = mod[...]
+    copies = start_fetch(own, pieces, weight, sems, shards)
     norm_a, rstd_a = layer_norm(tokens[...].astype(F32))
-    wait_all(copies_qkvo)
-    grad_modul = dot_nt(low_proj[...], w_qkvo[:, : 3 * width])
-    sums = [
-        jnp.sum(grad_modul, 0, keepdims=True),
-        jnp.sum(grad_modul * norm_a, 0, keepdims=True),
-        mods_b[2:3, :],
-        mods_b[0:1, :],
-        mods_b[1:2, :],
-    ]
+    wait_all(copies)
+    grad_modul = dot_nt(low_proj[...], weight[:, : 3 * width])
+    grad_mods[0:1, :] = jnp.sum(grad_modul, 0, keepdims=True)
+    grad_mods[1:2, :] = jnp.sum(grad_modul * norm_a, 0, keepdims=True)
     grad_tokens[...] = grad_middle[...] + norm_back(
-        grad_modul * (1.0 + mod_piece(mod_val, 1, width)), norm_a, rstd_a
-    )
-    wait_all(copies_fc2)
-    branch_b = dot_nn(hidden[...], w_fc2[...]) + bias_fc2[...]
-    gate_b = mod_piece(mod_val, 5, width)
+        grad_modul * (1.0 + mod_piece(mod[...], 1, width)), norm_a, rstd_a
+    )
+
+
+def mixed_kernel(shards, *refs):
+    refs = list(refs)
+    hidden, mod, middle, cot, bias_fc2 = take(refs, 5)
+    mods_a, mods_b, sum_proj, sum_out, sum_pre = take(refs, 5)
+    own = take(refs, 1)
+    pieces = take(refs, piece_total(shards))
+    mixed, news = take(refs, 2)
+    weight, sems = refs
+    rows, width = middle.shape
+    copies = start_fetch(own, pieces, weight, sems, shards)
+    gate_b = mod_piece(mod[...], 5, width)
     grad_out = cot[...].astype(F32)
+    wait_all(copies)
+    branch_b = dot_nn(hidden[...], weight[...]) + bias_fc2[...]
     mixed[...] = (middle[...] + gate_b * branch_b).astype(BF16)
+    sums = [mods_a[0:1, :], mods_a[1:2, :], mods_b[2:3, :], mods_b[0:1, :], mods_b[1:2, :]]
     sums.append(jnp.sum(grad_out * branch_b, 0, keepdims=True))
     sums += [sum_proj[:, :width], sum_proj[:, 2 * width :], sum_out[...], sum_pre[...]]
     sums.append(jnp.sum(grad_out * gate_b, 0, keepdims=True))
@@ -613,20 +616,20 @@
     place = lax.axis_index("shard")
 
     def own(target, values):
-        size = target.shape[1]
+        size = target.shape[0]
         found = jnp.zeros((1, size), F32)
         for at in range(shards):
             found = jnp.where(place == at, values[:, at * size : (at + 1) * size], found)
-        target[...] = found
+        target[...] = found[0]
 
     own(own_mod, jnp.sum(jnp.where(row < shards, total[:, :span], 0.0), 0, keepdims=True))
-    part = shards * (own_qv.shape[1] + own_out.shape[1] + own_fc1.shape[1] + own_fc2.shape[1]) // 2
+    part = shards * (own_qv.shape[0] + own_out.shape[0] + own_fc1.shape[0] + own_fc2.shape[0]) // 2
     biases = jnp.concatenate(
         [total[shards : shards + 1, :part], total[shards + 1 : shards + 2, :part]], 1
     )
     low = 0
     for target in (own_qv, own_out, own_fc1, own_fc2):
-        high = low + shards * target.shape[1]
+        high = low + shards * target.shape[0]
         own(target, biases[:, low:high])
         low = high
     whole = share[...].reshape(groups * count, share.shape[2])
@@ -707,12 +710,12 @@
         return got
 
     came = [hop(partial[number : number + 1], "shard", shards, number) for number in range(1, shards)]
-    came, got = together(came, rest(all_qkvo, all_qkvo.operands(2)))
+    got = rest(all_qkvo, all_qkvo.operands(2))
     all_qkvo.hold(all_qkvo.depths, got)
     mod = partial[0:1]
     for row in came:
         mod = mod + row
-    bias_rows = xor_rows(gate([notes], mod)[0][:, width:].astype(F32), place)
+    bias_rows = xor_rows(gate([notes], partial)[0][:, width:].astype(F32), place)
     full_bias = []
     start = 0
     for piece in biases:
@@ -777,6 +780,10 @@
     pieces_fc2 = all_fc2.pieces()
     red_fc2 = Reduction(outs[0], outs[1], shards, replicas, 1)
     red_fc2.swap()
+    stages = len(red_fc2.bits)
+    steps = red_fc2.rounds()
+    slope = after(slope, *red_fc2.ready(0))
+    red_fc2.send(0)
     low_pre, sum_pre, *outs = call(
         pre_kernel,
         shards,
@@ -789,11 +796,15 @@
         + [pltpu.VMEM((width, rows), BF16), sems((pieces + 1,)), sems((2 * shards * chunks,))],
         10**11,
     )
-    [red_fc2.came], [low_pre, *outs] = together([red_fc2.came], [low_pre, *outs])
+    got, [low_pre, *outs] = together(red_fc2.flying, [low_pre, *outs])
+    red_fc2.land(got)
     red_fc1 = Reduction(outs[0], outs[1], shards, replicas, 1)
     red_fc1.swap()
-    low_pre = after(low_pre, *red_fc2.ready(0))
-    red_fc2.send(0)
+    for stage in range(1, stages - 1):
+        red_fc2.ready(stage)
+        red_fc2.land(red_fc2.send(stage))
+    low_pre = after(low_pre, *red_fc2.ready(stages - 1))
+    red_fc2.send(stages - 1)
     grad_middle, low_branch_a, sum_out, mods_b = call(
         middle_kernel,
         shards,
@@ -813,13 +824,9 @@
         red_fc2.flying, [red_fc1.came], [low_branch_a]
     )
     red_fc2.land(got)
-    stages = len(red_fc2.bits)
-    for stage in range(1, stages - 1):
-        red_fc2.ready(stage)
-        red_fc2.land(red_fc2.send(stage))
-    low_branch_a = after(low_branch_a, *red_fc2.ready(stages - 1), *red_fc1.ready(0))
-    red_fc2.send(stages - 1)
+    low_branch_a = after(low_branch_a, *red_fc1.ready(0), *red_fc2.own())
     red_fc1.send(0)
+    red_fc2.fold(0)
     low_proj, sum_proj, *outs = call(
         back_kernel,
         shards,
@@ -836,54 +843,74 @@
     got_2, got_1, [low_proj, *outs] = together(
         red_fc2.flying, red_fc1.flying, [low_proj, *outs]
     )
-    red_fc2.land(got_2)
+    red_fc2.folded(0, got_2)
     red_fc1.land(got_1)
     red_qkvo = Reduction(outs[0], outs[1], shards, replicas, part_count(shards))
     red_qkvo.swap()
     for stage in range(1, stages - 1):
         red_fc1.ready(stage)
         red_fc1.land(red_fc1.send(stage))
-    low_proj = after(low_proj, *red_qkvo.ready(0), *red_fc1.ready(stages - 1), *red_fc2.own())
+    low_proj = after(low_proj, *red_qkvo.ready(0), *red_fc1.ready(stages - 1), *red_fc2.values)
     red_qkvo.send(0)
     red_fc1.send(stages - 1)
-    red_fc2.fold(0)
-    grad_tokens, mixed, news = call(
-        last_kernel,
+    flying_2 = red_fc2.fold(1) if steps > 1 else []
+    grad_tokens, mods_a = call(
+        tokens_kernel,
         shards,
-        [low_proj, tokens, mod, grad_middle, hidden, middle, cot, bias_fc2]
-        + [sum_proj, sum_out, sum_pre, mods_b],
-        [w_qkv, w_out] + pieces_qkvo + [w_fc2] + pieces_fc2,
+        [low_proj, tokens, mod, grad_middle],
+        [w_qkv, w_out] + pieces_qkvo,
+        [shape((rows, width), F32), shape((2, width), F32)],
+        [],
+        qkvo_scratch + [sems((pieces + 2,))],
+        10**11,
+    )
+    got_q, got_1, got_2, [mods_a] = together(
+        red_qkvo.flying, red_fc1.flying, flying_2, [mods_a]
+    )
+    red_qkvo.land(got_q)
+    red_fc1.land(got_1)
+    if steps > 1:
+        red_fc2.folded(1, got_2)
+    for stage in range(1, stages - 1):
+        red_qkvo.ready(stage)
+        red_qkvo.land(red_qkvo.send(stage))
+    sent_q = red_qkvo.ready(stages - 1)
+    red_qkvo.send(stages - 1)
+    red_fc1.own()
+    red_fc1.fold(0)
+    flying_2 = red_fc2.fold(2) if steps > 2 else []
+    mods_a = after(mods_a, *sent_q, *red_fc1.values, *red_fc2.values)
+    mixed, news = call(
+        mixed_kernel,
+        shards,
+        [hidden, mod, middle, cot, bias_fc2, mods_a, mods_b, sum_proj, sum_out, sum_pre],
+        [w_fc2] + pieces_fc2,
         [
-            shape((rows, width), F32),
             shape((rows, width), BF16),
             shape((1, 6 * width + 3 * width + inner + width), BF16),
         ],
         [],
-        qkvo_scratch + fc2_scratch + [sems((pieces + 2,)), sems((pieces + 1,))],
+        fc2_scratch + [sems((pieces + 1,))],
         10**11,
     )
     got_q, got_1, got_2, [news] = together(
-        red_qkvo.flying, red_fc1.flying, red_fc2.flying, [news]
+        red_qkvo.flying, red_fc1.flying, flying_2, [news]
     )
     red_qkvo.land(got_q)
-    red_fc1.land(got_1)
-    red_fc2.folded(0, got_2)
-    for stage in range(1, stages - 1):
-        red_qkvo.ready(stage)
-        red_qkvo.land(red_qkvo.send(stage))
-    steps = red_fc2.rounds()
+    red_fc1.folded(0, got_1)
+    if steps > 2:
+        red_fc2.folded(2, got_2)
+
+    red_qkvo.own()
+
     count = -(-(shards + 2) // 8) * 8
     mod_span = 6 * width
     share_span = mod_span + 2 * 128 * -(-mod_rows // 256)
     share_steps = replicas.bit_length() - 1
 
     def mod_chain():
-        held = [news]
-        flip = 1
-        while flip < shards:
-            got = yield [(value, "shard", flip) for value in held]
-            held += got
-            flip *= 2
+        got = yield [(news, "shard", number) for number in range(1, shards)]
+        held = [news] + got
         *back, share = call(
             share_kernel,
             shards,
@@ -892,8 +919,9 @@
             [shape((1, width), F32)] * shards + [shape((1, count, share_span), BF16)],
             [],
             [pltpu.VMEM((count, share_span), F32)],
-            10**8,
+            10**11,
         )
+        share, *back = yield [(value, None, 0) for value in [share, *back]]
         rows = dict(enumerate(back))
         step = 0
         while step < share_steps:
@@ -916,60 +944,26 @@
 
     def send_on(moves):
         return [
-            hop(value, axis, shards if axis == "shard" else replicas, flip)
+            hop(value, axis, shards if axis == "shard" else replicas, flip) if axis else value
             for value, axis, flip in moves
         ]
 
-    at_1, at_2 = 1, min(2, steps)
-    sent_1 = red_fc1.own() + red_fc2.values
-    flying_1 = red_fc1.fold(0)
-    flying_2 = red_fc2.fold(1) if steps > 1 else []
-    red_qkvo.keep = after(red_qkvo.keep, *sent_1)
-    sent_q = red_qkvo.ready(stages - 1)
-    flying_q = red_qkvo.send(stages - 1)
-    [news], flying_1, flying_2, _ = together([news], flying_1, flying_2, sent_q)
-    red_fc1.folded(0, flying_1)
-    if steps > 1:
-        red_fc2.folded(1, flying_2)
     chain = mod_chain()
-    moves = next(chain)
-    at_q = -1
-    while True:
-        moves = list(moves)
-        values = [value for value, _, _ in moves]
-        lanes = [[], []]
-        if at_1 < steps:
-            lanes[0] = red_fc1.fold(at_1)
-        if at_2 < steps:
-            lanes[1] = red_fc2.fold(at_2)
-        flying_m = send_on(moves)
-        sent_b = values + red_fc1.values + red_fc2.values
-        if at_q < steps:
-            got = gate(flying_q, *sent_b)
-            if at_q < 0:
-                red_qkvo.land(got)
-                red_qkvo.own()
-            else:
-                red_qkvo.folded(at_q, got)
-            at_q += 1
-            if at_q < steps:
-                flying_q = red_qkvo.fold(at_q)
-        lanes[0], lanes[1], flying_m, _ = together(
-            lanes[0], lanes[1], flying_m, red_qkvo.values
-        )
-        if at_1 < steps:
-            red_fc1.folded(at_1, lanes[0])
-            at_1 += 1
-        if at_2 < steps:
-            red_fc2.folded(at_2, lanes[1])
-            at_2 += 1
-        try:
-            moves = chain.send(flying_m) if chain else []
-        except StopIteration:
-            chain = None
-            moves = []
-        if chain is None and at_1 >= steps and at_2 >= steps and at_q >= steps:
-            break
+    moves = list(next(chain))
+    lanes = {red_qkvo: 0, red_fc1: 1, red_fc2: min(3, steps)}
+    while chain or min(lanes.values()) < steps:
+        moving = [lane for lane in lanes if lanes[lane] < steps]
+        groups = [lane.fold(lanes[lane]) for lane in moving]
+        groups = together(*groups, send_on(moves))
+        for lane, got in zip(moving, groups):
+            lane.folded(lanes[lane], got)
+            lanes[lane] += 1
+        moves = []
+        if chain:
+            try:
+                moves = list(chain.send(groups[-1]))
+            except StopIteration:
+                chain = None
     share, grad_row = mod_chain.result
     _, silu_back = jax.vjp(jax.nn.silu, cond_f)
     grad_cond = silu_back(grad_row)[0]
@@ -978,14 +972,12 @@
         shards,
         [share],
         [],
-        [shape((mod_rows, mod_span), F32), shape((1, b_mod.shape[0]), F32)]
-        + [shape((1, piece.shape[0]), F32) for piece in biases],
+        [shape((mod_rows, mod_span), F32), shape(b_mod.shape, F32)]
+        + [shape(piece.shape, F32) for piece in biases],
         [],
         [],
         10**8,
     )
-    total_b_mod = total_b_mod.reshape(-1)
-    bias_totals = [piece.reshape(-1) for piece in bias_totals]
 
     total_fc2 = red_fc2.finish()
     total_fc1 = red_fc1.finish()

time: 274 us -> 264 us (0.964)
  waiting for transfers between devices: 89.7 us -> 73.7 us
  local copies, waits for them, and re-layouts: 12.9 us -> 17.2 us
  other arithmetic: 33 us -> 30.2 us
    ppermute x12, waiting for transfers between devices: 35 us -> 22.2 us  [fold(): lax.ppermute(value, 'replica', pairs)]
    ppermute x58, starting transfers between devices: 42.5 us -> 46.7 us  [hop(): return lax.ppermute(value, axis, [(at, at ^ flip) for at in range(size)])]
    pallas_call x3 -> x0, other arithmetic: 3.87 us -> none  [call(): pl.pallas_call(functools.partial(kernel, shards), out_shape=outs + outsid...]
    ppermute x58, waiting for transfers between devices: 54.7 us -> 51.5 us  [hop(): return lax.ppermute(value, axis, [(at, at ^ flip) for at in range(size)])]
    ppermute x12, starting transfers between devices: 24.8 us -> 21.7 us  [fold(): lax.ppermute(value, 'replica', pairs)]
    pallas_call x8 -> x9, Pallas kernels: 68 us -> 70.4 us  [call(): pl.pallas_call(functools.partial(kernel, shards), out_shape=outs + outsid...]
    unnamed x111 -> x96, local copies, waits for them, and re-layouts: 4.88 us -> 6.35 us
  transfers between devices with their start and end apart: 70 -> 70, of which waited for: 28 -> 28; matrix products, arithmetic and copies ran while one was open for 9% -> 11% of each run, Pallas kernels for 24% -> 25%
where the time goes in v2:
time: 264 us; the launch traced here: 263 us
  waiting for transfers between devices  73.7 us (28%)
  Pallas kernels  70.4 us (27%)
  starting transfers between devices  68.4 us (26%)
  other arithmetic  30.2 us (11%)
  local copies, waits for them, and re-layouts  17.2 us (7%)
    pallas_call x9, Pallas kernels, call(): pl.pallas_call(functools.partial(kernel, shards), out_shape=outs + outsid...  70.4 us
    ppermute x58, waiting for transfers between devices, hop(): return lax.ppermute(value, axis, [(at, at ^ flip) for at in range(size)])  51.5 us
    ppermute x58, starting transfers between devices, hop(): return lax.ppermute(value, axis, [(at, at ^ flip) for at in range(size)])  46.7 us
    ppermute x12, waiting for transfers between devices, fold(): lax.ppermute(value, 'replica', pairs)  22.2 us
    ppermute x12, starting transfers between devices, fold(): lax.ppermute(value, 'replica', pairs)  21.7 us
    convert_element_type x9, other arithmetic, ready(): self.sent = [self.total(at, stage).astype(BF16) for at in range(self.parts)]  11.8 us
    unnamed x96, local copies, waits for them, and re-layouts  6.35 us
  transfers between devices with their start and end apart: 70, of which 28 were waited for; matrix products, arithmetic and copies ran while one was open for 11% of the time, Pallas kernels for 25%

profile of v2, /device:TPU:0, one launch (start us, length us, event | category | flops | bytes accessed | tf_op | source)
XLA Modules:
  0.0 262.5 jit_solution(1878046563788218187)
XLA Ops:
  2.8 3.0 %collective-permute-start.1 = (bf16[96,3072]{1,0:T(8,128)(2,1)S(1)}, bf16[96,3072]{1,0:T(8,128)(2,1)S(1)}, u32[]{:S(2)}, u32[]{:S(2)}) collective-permute-start(bf16[96,3072]{1,0:T(8,128)(2,1)S(1)} %pad_maximum_fusion.1), channel_id=1, source_target_pairs={{0,16},{8,24},{16,0},{24,8},{1,17},{9,25},{17,1},{25,9},{2,18},{10... | collective-permute-start | bytes 1769480 | tf_op jit(solution)/shard_map/ppermute | solution.py:42
  8.2 1.9 collective-permute-start.3
  14.7 6.1 %collective-permute-done.4 = bf16[1,2304]{1,0:T(2,128)(2,1)} collective-permute-done((bf16[1,2304]{1,0:T(2,128)(2,1)S(1)}, bf16[1,2304]{1,0:T(2,128)(2,1)}, u32[]{:S(2)}, u32[]{:S(2)}) %collective-permute-start.4) | collective-permute-done | bytes 4640 | tf_op jit(solution)/shard_map/ppermute | solution.py:42
  39.7 9.9 %shard_map.228 = (bf16[256,768]{1,0:T(8,128)(2,1)}, bf16[256,2304]{1,0:T(8,128)(2,1)}, bf16[256,768]{1,0:T(8,128)(2,1)}, f32[256,128]{1,0:T(8,128)}, f32[256,768...) custom-call(bf16[256,768]{1,0:T(8,128)(2,1)} %refs_1_.7, f32[1,4608]{1,0:T(1,128)} %fusion.9.refs_1_.refs_2_, ...), custom_call_target="tpu_custom_call" | custom-call | flops 99999997952 | bytes 9202688 | tf_op jit(solution)/shard_map/pallas_call | solution.py:645
  57.9 4.4 %collective-permute-done.17.refs_8_.refs_9_ = bf16[96,1536]{1,0:T(8,128)(2,1)S(1)} collective-permute-done((bf16[96,1536]{1,0:T(8,128)(2,1)S(1)}, bf16[96,1536]{1,0:T(8,128)(2,1)S(1)}, u32[]{:S(2)}, u32[]{:S(2)}) %collective-permute-start.17) | collective-permute-done | bytes 294944 | tf_op jit(solution)/shard_map/ppermute | solution.py:42
  62.3 1.9 collective-permute-done.16.refs_7_.refs_8_
  68.4 11.3 %shard_map.229 = (bf16[256,3072]{1,0:T(8,128)(2,1)}, f32[256,3072]{1,0:T(8,128)}, bf16[4,384,768]{2,1,0:T(8,128)(2,1)}, bf16[4,384,768]{2,1,0:T(8,128)(2,1)}) custom-call(bf16[256,768]{1,0:T(8,128)(2,1)} %get-tuple-element.136.refs_0_, bf16[256,768]{1,0:T(8,128)(2,1)} %refs_3_.1, f32[1,4608]{1,0:T(1,128)} %fusion.9.refs_1_.refs_2_, f32[1,3072]{1,0:T(1,128)} %bitcast.117, ...), custom_call_target="tpu_custom_call" | custom-call | flops 99999997952 | bytes 14972928 | tf_op jit(solution)/shard_map/pallas_call | solution.py:645
  84.7 6.3 %collective-permute-done.27.refs_7_.refs_13_ = bf16[384,384]{1,0:T(8,128)(2,1)S(1)} collective-permute-done((bf16[384,384]{1,0:T(8,128)(2,1)S(1)}, bf16[384,384]{1,0:T(8,128)(2,1)S(1)}, u32[]{:S(2)}, u32[]{:S(2)}) %collective-permute-start.27) | collective-permute-done | bytes 294944 | tf_op jit(solution)/shard_map/ppermute | solution.py:42
  98.2 9.8 %shard_map.230 = (bf16[256,3072]{1,0:T(8,128)(2,1)}, f32[1,3072]{1,0:T(1,128)}, bf16[4,96,3072]{2,1,0:T(8,128)(2,1)}, bf16[4,96,3072]{2,1,0:T(8,128)(2,1)}) custom-call(bf16[256,768]{1,0:T(8,128)(2,1)} %get-tuple-element.136.refs_0_, bf16[256,768]{1,0:T(8,128)(2,1)} %refs_3_.1, f32[1,4608]{1,0:T(1,128)} %fusion.9.refs_1_.refs_2_, ...), custom_call_target="tpu_custom_call" | custom-call | flops 99999997952 | bytes 14972928 | tf_op jit(solution)/shard_map/pallas_call | solution.py:645
  108.0 2.0 collective-permute-done.25
  114.5 7.6 %shard_map.231 = (f32[256,768]{1,0:T(8,128)}, bf16[256,768]{1,0:T(8,128)(2,1)}, f32[1,768]{1,0:T(1,128)}, f32[3,768]{1,0:T(4,128)}) custom-call(bf16[256,3072]{1,0:T(8,128)(2,1)} %get-tuple-element.155.refs_0_, bf16[256,768]{1,0:T(8,128)(2,1)} %refs_3_.1, f32[1,4608]{1,0:T(1,128)} %fusion.9.refs_1_.refs_2_, f32[256,768]{1,0:T(8,128)} %get-tuple-element.138.refs_3_.refs_2_, ...), custom_call_target="tpu_custom_call" | custom-call | flops 99999997952 | bytes 9467904 | tf_op jit(solution)/shard_map/pallas_call | solution.py:645
  126.0 4.3 %collective-permute-start.36 = (bf16[384,768]{1,0:T(8,128)(2,1)S(1)}, bf16[384,768]{1,0:T(8,128)(2,1)}, u32[]{:S(2)}, u32[]{:S(2)}) collective-permute-start(bf16[384,768]{1,0:T(8,128)(2,1)S(1)} %pad_maximum_fusion.2), channel_id=1, source_target_pairs={{0,2},{1,3},{6,4},{7,5},{8,10},{9,11},{14,12},{15,13},{16,18},{17,... | collective-permute-start | bytes 1769480 | tf_op jit(solution)/shard_map/ppermute | solution.py:215
  131.8 12.8 %shard_map.232 = (bf16[256,2304]{1,0:T(8,128)(2,1)}, f32[1,2304]{1,0:T(1,128)}, bf16[4,96,3072]{2,1,0:T(8,128)(2,1)}, bf16[4,96,3072]{2,1,0:T(8,128)(2,1)}) custom-call(bf16[256,768]{1,0:T(8,128)(2,1)} %get-tuple-element.163.refs_0_, bf16[256,768]{1,0:T(8,128)(2,1)} %get-tuple-element.164.refs_1_, bf16[256,2304]{1,0:T(8,128)(2,1)} %get-tuple-element.165.refs_2_, ...), custom_call_target="tpu_custom_call" | custom-call | flops 99999997952 | bytes 13116416 | tf_op jit(solution)/shard_map/pallas_call | solution.py:645
  147.0 2.3 add_convert_fusion.20
  155.0 2.0 add_convert_fusion.5
  158.6 6.2 %shard_map.233 = (f32[256,768]{1,0:T(8,128)}, f32[2,768]{1,0:T(2,128)}) custom-call(bf16[256,2304]{1,0:T(8,128)(2,1)} %get-tuple-element.177.refs_0_, bf16[256,768]{1,0:T(8,128)(2,1)} %refs_1_.7, f32[1,4608]{1,0:T(1,128)} %fusion.9.refs_1_.refs_2_, f32[256,768]{1,0:T(8,128)} %get-tuple-element.178.refs_3_, bf16[192,2304]{1,0:T(8,128)(2,1)} %refs_4_.8, ...), custom_call_target="tpu_custom_call" | custom-call | flops 99999997952 | bytes 7888896 | tf_op jit(solution)/shard_map/pallas_call | solution.py:645
  164.8 7.6 %collective-permute-done.40 = bf16[2,96,1536]{2,1,0:T(8,128)(2,1)S(1)} collective-permute-done((bf16[2,96,1536]{2,1,0:T(8,128)(2,1)}, bf16[2,96,1536]{2,1,0:T(8,128)(2,1)S(1)}, u32[]{:S(2)}, u32[]{:S(2)}) %collective-permute-start.40) | collective-permute-done | bytes 589856 | tf_op jit(solution)/shard_map/ppermute | solution.py:42
  174.3 3.4 %collective-permute-start.47 = (bf16[96,3072]{1,0:T(8,128)(2,1)S(1)}, bf16[96,3072]{1,0:T(8,128)(2,1)S(1)}, u32[]{:S(2)}, u32[]{:S(2)}) collective-permute-start(bf16[96,3072]{1,0:T(8,128)(2,1)S(1)} %pad_maximum_fusion.3), channel_id=1, source_target_pairs={{0,2},{1,3},{6,4},{7,5},{8,10},{9,11},{14,12},{15,13},{16,18},{17,... | collective-permute-start | bytes 1769480 | tf_op jit(solution)/shard_map/ppermute | solution.py:215
  182.8 6.4 %shard_map.234 = (bf16[256,768]{1,0:T(8,128)(2,1)}, bf16[1,10752]{1,0:T(2,128)(2,1)}) custom-call(bf16[256,3072]{1,0:T(8,128)(2,1)} %get-tuple-element.137.refs_0_, f32[1,4608]{1,0:T(1,128)} %fusion.9.refs_1_.refs_2_, f32[256,768]{1,0:T(8,128)} %get-tuple-element.138.refs_3_.refs_2_, bf16[256,768]{1,0:T(8,128)(2,1)} %refs_3_.1, f32[1,768]{1,0:T(1,128)} %reshape.202.refs_4_, ...), custom_call_target="tpu_custom_call" | custom-call | flops 99999997952 | bytes 7947264 | tf_op jit(solution)/shard_map/pallas_call | solution.py:645
  189.2 4.0 %collective-permute-done.48 = bf16[384,768]{1,0:T(8,128)(2,1)S(1)} collective-permute-done((bf16[384,768]{1,0:T(8,128)(2,1)S(1)}, bf16[384,768]{1,0:T(8,128)(2,1)S(1)}, u32[]{:S(2)}, u32[]{:S(2)}) %collective-permute-start.48) | collective-permute-done | bytes 589856 | tf_op jit(solution)/shard_map/ppermute | solution.py:215
  195.4 3.8 %collective-permute-start.50 = (bf16[96,1536]{1,0:T(8,128)(2,1)S(1)}, bf16[96,1536]{1,0:T(8,128)(2,1)}, u32[]{:S(2)}, u32[]{:S(2)}) collective-permute-start(bf16[96,1536]{1,0:T(8,128)(2,1)S(1)} %get-tuple-element.233), channel_id=1, source_target_pairs={{0,2},{1,3},{6,4},{7,5},{8,10},{9,11},{14,12},{15,13},{16,18},{17,... | collective-permute-start | bytes 884744 | tf_op jit(solution)/shard_map/ppermute | solution.py:215
  199.2 2.0 collective-permute-start.49
  201.2 1.9 collective-permute-start.54
  204.1 2.6 collective-permute-done.54.refs_3_
  208.8 2.7 %collective-permute-done.52.refs_1_ = bf16[1,10752]{1,0:T(2,128)(2,1)S(1)} collective-permute-done((bf16[1,10752]{1,0:T(2,128)(2,1)}, bf16[1,10752]{1,0:T(2,128)(2,1)S(1)}, u32[]{:S(2)}, u32[]{:S(2)}) %collective-permute-start.52) | collective-permute-done | bytes 21536 | tf_op jit(solution)/shard_map/ppermute | solution.py:42
  216.8 2.9 %shard_map.235 = (f32[1,768]{1,0:T(1,128)}, f32[1,768]{1,0:T(1,128)}, f32[1,768]{1,0:T(1,128)}, f32[1,768]{1,0:T(1,128)}, bf16[1,8,4864]{2,1,0:T(8,128)(2,1)}) custom-call(bf16[1,10752]{1,0:T(2,128)(2,1)} %get-tuple-element.197.refs_0_, bf16[1,10752]{1,0:T(2,128)(2,1)} %copy-done.43, bf16[1,10752]{1,0:T(2,128)(2,1)} %copy-done.42, ...), custom_call_target="tpu_custom_call" | custom-call | flops 99999997952 | bytes 1947136 | tf_op jit(solution)/shard_map/pallas_call | solution.py:645
  221.3 8.8 %collective-permute-done.57 = bf16[96,3072]{1,0:T(8,128)(2,1)S(1)} collective-permute-done((bf16[96,3072]{1,0:T(8,128)(2,1)S(1)}, bf16[96,3072]{1,0:T(8,128)(2,1)S(1)}, u32[]{:S(2)}, u32[]{:S(2)}) %collective-permute-start.57) | collective-permute-done | bytes 589856 | tf_op jit(solution)/shard_map/ppermute | solution.py:215
  235.8 2.4 collective-permute-done.60
  238.2 4.6 %collective-permute-done.58 = bf16[96,1536]{1,0:T(8,128)(2,1)S(1)} collective-permute-done((bf16[96,1536]{1,0:T(8,128)(2,1)S(1)}, bf16[96,1536]{1,0:T(8,128)(2,1)S(1)}, u32[]{:S(2)}, u32[]{:S(2)}) %collective-permute-start.58) | collective-permute-done | bytes 294944 | tf_op jit(solution)/shard_map/ppermute | solution.py:215
  242.7 4.8 %collective-permute-done.59 = bf16[96,1536]{1,0:T(8,128)(2,1)S(1)} collective-permute-done((bf16[96,1536]{1,0:T(8,128)(2,1)S(1)}, bf16[96,1536]{1,0:T(8,128)(2,1)S(1)}, u32[]{:S(2)}, u32[]{:S(2)}) %collective-permute-start.59) | collective-permute-done | bytes 294944 | tf_op jit(solution)/shard_map/ppermute | solution.py:215
  248.4 2.9 %collective-permute-done.64 = f32[1,768]{1,0:T(1,128)S(1)} collective-permute-done((f32[1,768]{1,0:T(1,128)S(1)}, f32[1,768]{1,0:T(1,128)S(1)}, u32[]{:S(2)}, u32[]{:S(2)}) %collective-permute-start.64) | collective-permute-done | bytes 3104 | tf_op jit(solution)/shard_map/ppermute | solution.py:42
  259.0 3.5 %shard_map.236 = (f32[192,4608]{1,0:T(8,128)}, f32[1152]{0:T(1024)}, f32[384]{0:T(512)}, f32[192]{0:T(256)}, f32[768]{0:T(1024)}, /*index=5*/f32[192]{0:T(256)}) custom-call(bf16[8,8,4864]{2,1,0:T(8,128)(2,1)} %pad_maximum_fusion.refs_0_), custom_call_target="tpu_custom_call" | custom-call | flops 100000000 | bytes 4172288 | tf_op jit(solution)/shard_map/pallas_call | solution.py:645
  (285 shorter events, 104.6 us)
Async XLA Ops:
  2.8 18.3 %collective-permute-start.1 = (bf16[96,3072]{1,0:T(8,128)(2,1)S(1)}, bf16[96,3072]{1,0:T(8,128)(2,1)S(1)}, u32[]{:S(2)}, u32[]{:S(2)}) collective-permute-start(bf16[96,3072]{1,0:T(8,128)(2,1)S(1)} %pad_maximum_fusion.1), channel_id=1, source_target_pairs={{0,16},{8,24},{16,0},{24,8},{1,17},{9,25},{17,1},{25,9},{2,18},{10... | collective-permute-start | bytes 1769480 | tf_op jit(solution)/shard_map/ppermute | solution.py:42
  5.8 15.3 %collective-permute-start = (bf16[96,3072]{1,0:T(8,128)(2,1)S(1)}, bf16[96,3072]{1,0:T(8,128)(2,1)}, u32[]{:S(2)}, u32[]{:S(2)}) collective-permute-start(bf16[96,3072]{1,0:T(8,128)(2,1)S(1)} %pad_maximum_fusion.1), channel_id=1, source_target_pairs={{0,8},{8,0},{16,24},{24,16},{1,9},{9,1},{17,25},{25,17},{2,10},{10... | collective-permute-start | bytes 1769480 | tf_op jit(solution)/shard_map/ppermute | solution.py:42
  8.0 12.8 %collective-permute-start.4 = (bf16[1,2304]{1,0:T(2,128)(2,1)S(1)}, bf16[1,2304]{1,0:T(2,128)(2,1)}, u32[]{:S(2)}, u32[]{:S(2)}) collective-permute-start(bf16[1,2304]{1,0:T(2,128)(2,1)S(1)} %broadcast_in_dim.2), channel_id=1, source_target_pairs={{0,24},{8,16},{16,8},{24,0},{1,25},{9,17},{17,9},{25,1},{2,26},{10... | collective-permute-start | bytes 13832 | tf_op jit(solution)/shard_map/ppermute | solution.py:42
  8.2 12.7 %collective-permute-start.3 = (bf16[1,2304]{1,0:T(2,128)(2,1)S(1)}, bf16[1,2304]{1,0:T(2,128)(2,1)}, u32[]{:S(2)}, u32[]{:S(2)}) collective-permute-start(bf16[1,2304]{1,0:T(2,128)(2,1)S(1)} %broadcast_in_dim.2), channel_id=1, source_target_pairs={{0,16},{8,24},{16,0},{24,8},{1,17},{9,25},{17,1},{25,9},{2,18},{10... | collective-permute-start | bytes 13832 | tf_op jit(solution)/shard_map/ppermute | solution.py:42
  10.1 11.0 %collective-permute-start.2 = (bf16[1,2304]{1,0:T(2,128)(2,1)S(1)}, bf16[1,2304]{1,0:T(2,128)(2,1)}, u32[]{:S(2)}, u32[]{:S(2)}) collective-permute-start(bf16[1,2304]{1,0:T(2,128)(2,1)S(1)} %broadcast_in_dim.2), channel_id=1, source_target_pairs={{0,8},{8,0},{16,24},{24,16},{1,9},{9,1},{17,25},{25,17},{2,10},{10... | collective-permute-start | bytes 13832 | tf_op jit(solution)/shard_map/ppermute | solution.py:42
  35.6 15.8 %collective-permute-start.8 = (bf16[96,3072]{1,0:T(8,128)(2,1)S(1)}, bf16[96,3072]{1,0:T(8,128)(2,1)}, u32[]{:S(2)}, u32[]{:S(2)}) collective-permute-start(bf16[96,3072]{1,0:T(8,128)(2,1)S(1)} %constant_dynamic-slice_fusion.4), channel_id=1, source_target_pairs={{0,16},{8,24},{16,0},{24,8},{1,17},{9,25},{17,1},{25,9},{2,18},{10... | collective-permute-start | bytes 1769480 | tf_op jit(solution)/shard_map/ppermute | solution.py:42
  37.1 15.7 %collective-permute-start.7 = (bf16[96,3072]{1,0:T(8,128)(2,1)S(1)}, bf16[96,3072]{1,0:T(8,128)(2,1)}, u32[]{:S(2)}, u32[]{:S(2)}) collective-permute-start(bf16[96,3072]{1,0:T(8,128)(2,1)S(1)} %constant_dynamic-slice_fusion.4), channel_id=1, source_target_pairs={{0,8},{8,0},{16,24},{24,16},{1,9},{9,1},{17,25},{25,17},{2,10},{10... | collective-permute-start | bytes 1769480 | tf_op jit(solution)/shard_map/ppermute | solution.py:42
  57.4 10.1 %collective-permute-start.18 = (bf16[96,3072]{1,0:T(8,128)(2,1)}, bf16[96,3072]{1,0:T(8,128)(2,1)}, u32[]{:S(2)}, u32[]{:S(2)}) collective-permute-start(bf16[96,3072]{1,0:T(8,128)(2,1)} %collective-permute-done.7.refs_5_.refs_6_), channel_id=1, source_target_pairs={{0,1},{1,0},{2,3},{3,2},{4,5},{5,4},{6,7},{7,6},{8,9},{9,8},{10,11... | collective-permute-start | bytes 1769480 | tf_op jit(solution)/shard_map/ppermute | solution.py:42
  64.9 15.7 %collective-permute-start.23 = (bf16[384,768]{1,0:T(8,128)(2,1)S(1)}, bf16[384,768]{1,0:T(8,128)(2,1)S(1)}, u32[]{:S(2)}, u32[]{:S(2)}) collective-permute-start(bf16[384,768]{1,0:T(8,128)(2,1)S(1)} %constant_dynamic-slice_fusion), channel_id=1, source_target_pairs={{0,16},{8,24},{16,0},{24,8},{1,17},{9,25},{17,1},{25,9},{2,18},{10... | collective-permute-start | bytes 1769480 | tf_op jit(solution)/shard_map/ppermute | solution.py:42
  66.0 15.5 %collective-permute-start.22 = (bf16[384,768]{1,0:T(8,128)(2,1)S(1)}, bf16[384,768]{1,0:T(8,128)(2,1)S(1)}, u32[]{:S(2)}, u32[]{:S(2)}) collective-permute-start(bf16[384,768]{1,0:T(8,128)(2,1)S(1)} %constant_dynamic-slice_fusion), channel_id=1, source_target_pairs={{0,8},{8,0},{16,24},{24,16},{1,9},{9,1},{17,25},{25,17},{2,10},{10... | collective-permute-start | bytes 1769480 | tf_op jit(solution)/shard_map/ppermute | solution.py:42
  81.5 10.9 %collective-permute-start.24 = (bf16[4,384,768]{2,1,0:T(8,128)(2,1)}, bf16[4,384,768]{2,1,0:T(8,128)(2,1)S(1)}, u32[]{:S(2)}, u32[]{:S(2)}) collective-permute-start(bf16[4,384,768]{2,1,0:T(8,128)(2,1)} %get-tuple-element.143), channel_id=1, source_target_pairs={{0,1},{1,0},{2,3},{3,2},{4,5},{5,4},{6,7},{7,6},{8,9},{9,8},{10,11... | collective-permute-start | bytes 7077896 | tf_op jit(solution)/shard_map/ppermute | solution.py:42
  84.2 12.4 %collective-permute-start.29 = (bf16[384,768]{1,0:T(8,128)(2,1)S(1)}, bf16[384,768]{1,0:T(8,128)(2,1)S(1)}, u32[]{:S(2)}, u32[]{:S(2)}) collective-permute-start(bf16[384,768]{1,0:T(8,128)(2,1)S(1)} %collective-permute-done.22.refs_5_.refs_11_), channel_id=1, source_target_pairs={{0,1},{1,0},{2,3},{3,2},{4,5},{5,4},{6,7},{7,6},{8,9},{9,8},{10,11... | collective-permute-start | bytes 1769480 | tf_op jit(solution)/shard_map/ppermute | solution.py:42
  84.2 14.0 %collective-permute-start.30 = (bf16[384,768]{1,0:T(8,128)(2,1)S(1)}, bf16[384,768]{1,0:T(8,128)(2,1)}, u32[]{:S(2)}, u32[]{:S(2)}) collective-permute-start(bf16[384,768]{1,0:T(8,128)(2,1)S(1)} %collective-permute-done.23.refs_6_.refs_12_), channel_id=1, source_target_pairs={{0,1},{1,0},{2,3},{3,2},{4,5},{5,4},{6,7},{7,6},{8,9},{9,8},{10,11... | collective-permute-start | bytes 1769480 | tf_op jit(solution)/shard_map/ppermute | solution.py:42
  94.2 15.7 %collective-permute-start.25 = (bf16[2,384,384]{2,1,0:T(8,128)(2,1)S(1)}, bf16[2,384,384]{2,1,0:T(8,128)(2,1)S(1)}, u32[]{:S(2)}, u32[]{:S(2)}) collective-permute-start(bf16[2,384,384]{2,1,0:T(8,128)(2,1)S(1)} %bitcast.110), channel_id=1, source_target_pairs={{0,8},{8,0},{16,24},{24,16},{1,9},{9,1},{17,25},{25,17},{2,10},{10... | collective-permute-start | bytes 1769480 | tf_op jit(solution)/shard_map/ppermute | solution.py:42
  95.6 15.3 %collective-permute-start.26 = (bf16[2,384,384]{2,1,0:T(8,128)(2,1)S(1)}, bf16[2,384,384]{2,1,0:T(8,128)(2,1)S(1)}, u32[]{:S(2)}, u32[]{:S(2)}) collective-permute-start(bf16[2,384,384]{2,1,0:T(8,128)(2,1)S(1)} %bitcast.109), channel_id=1, source_target_pairs={{0,16},{8,24},{16,0},{24,8},{1,17},{9,25},{17,1},{25,9},{2,18},{10... | collective-permute-start | bytes 1769480 | tf_op jit(solution)/shard_map/ppermute | solution.py:42
  126.0 20.3 %collective-permute-start.36 = (bf16[384,768]{1,0:T(8,128)(2,1)S(1)}, bf16[384,768]{1,0:T(8,128)(2,1)}, u32[]{:S(2)}, u32[]{:S(2)}) collective-permute-start(bf16[384,768]{1,0:T(8,128)(2,1)S(1)} %pad_maximum_fusion.2), channel_id=1, source_target_pairs={{0,2},{1,3},{6,4},{7,5},{8,10},{9,11},{14,12},{15,13},{16,18},{17,... | collective-permute-start | bytes 1769480 | tf_op jit(solution)/shard_map/ppermute | solution.py:215
  130.3 15.7 %collective-permute-start.37 = (bf16[2,96,1536]{2,1,0:T(8,128)(2,1)}, bf16[2,96,1536]{2,1,0:T(8,128)(2,1)S(1)}, u32[]{:S(2)}, u32[]{:S(2)}) collective-permute-start(bf16[2,96,1536]{2,1,0:T(8,128)(2,1)} %bitcast.14), channel_id=1, source_target_pairs={{0,8},{8,0},{16,24},{24,16},{1,9},{9,1},{17,25},{25,17},{2,10},{10... | collective-permute-start | bytes 1769480 | tf_op jit(solution)/shard_map/ppermute | solution.py:42
  130.8 15.5 %collective-permute-start.38 = (bf16[2,96,1536]{2,1,0:T(8,128)(2,1)}, bf16[2,96,1536]{2,1,0:T(8,128)(2,1)}, u32[]{:S(2)}, u32[]{:S(2)}) collective-permute-start(bf16[2,96,1536]{2,1,0:T(8,128)(2,1)} %bitcast.16), channel_id=1, source_target_pairs={{0,16},{8,24},{16,0},{24,8},{1,17},{9,25},{17,1},{25,9},{2,18},{10... | collective-permute-start | bytes 1769480 | tf_op jit(solution)/shard_map/ppermute | solution.py:42
  149.3 15.5 %collective-permute-start.42 = (bf16[1,96,1536]{2,1,0:T(8,128)(2,1)}, bf16[1,96,1536]{2,1,0:T(8,128)(2,1)}, u32[]{:S(2)}, u32[]{:S(2)}) collective-permute-start(bf16[1,96,1536]{2,1,0:T(8,128)(2,1)} %bitcast.24), channel_id=1, source_target_pairs={{0,16},{8,24},{16,0},{24,8},{1,17},{9,25},{17,1},{25,9},{2,18},{10... | collective-permute-start | bytes 884744 | tf_op jit(solution)/shard_map/ppermute | solution.py:42
  150.3 14.5 %collective-permute-start.43 = (bf16[1,96,1536]{2,1,0:T(8,128)(2,1)}, bf16[1,96,1536]{2,1,0:T(8,128)(2,1)}, u32[]{:S(2)}, u32[]{:S(2)}) collective-permute-start(bf16[1,96,1536]{2,1,0:T(8,128)(2,1)} %bitcast.26), channel_id=1, source_target_pairs={{0,8},{8,0},{16,24},{24,16},{1,9},{9,1},{17,25},{25,17},{2,10},{10... | collective-permute-start | bytes 884744 | tf_op jit(solution)/shard_map/ppermute | solution.py:42
  153.0 11.8 %collective-permute-start.44 = (bf16[384,768]{1,0:T(8,128)(2,1)S(1)}, bf16[384,768]{1,0:T(8,128)(2,1)S(1)}, u32[]{:S(2)}, u32[]{:S(2)}) collective-permute-start(bf16[384,768]{1,0:T(8,128)(2,1)S(1)} %add_convert_fusion.3), channel_id=1, source_target_pairs={{2,4},{3,5},{4,2},{5,3},{10,12},{11,13},{12,10},{13,11},{18,20},{1... | collective-permute-start | bytes 1769480 | tf_op jit(solution)/shard_map/ppermute | solution.py:215
  157.0 15.4 %collective-permute-start.40 = (bf16[2,96,1536]{2,1,0:T(8,128)(2,1)}, bf16[2,96,1536]{2,1,0:T(8,128)(2,1)S(1)}, u32[]{:S(2)}, u32[]{:S(2)}) collective-permute-start(bf16[2,96,1536]{2,1,0:T(8,128)(2,1)} %bitcast.20), channel_id=1, source_target_pairs={{0,8},{8,0},{16,24},{24,16},{1,9},{9,1},{17,25},{25,17},{2,10},{10... | collective-permute-start | bytes 1769480 | tf_op jit(solution)/shard_map/ppermute | solution.py:42
  157.5 14.9 %collective-permute-start.41 = (bf16[2,96,1536]{2,1,0:T(8,128)(2,1)S(1)}, bf16[2,96,1536]{2,1,0:T(8,128)(2,1)S(1)}, u32[]{:S(2)}, u32[]{:S(2)}) collective-permute-start(bf16[2,96,1536]{2,1,0:T(8,128)(2,1)S(1)} %bitcast.108), channel_id=1, source_target_pairs={{0,16},{8,24},{16,0},{24,8},{1,17},{9,25},{17,1},{25,9},{2,18},{10... | collective-permute-start | bytes 1769480 | tf_op jit(solution)/shard_map/ppermute | solution.py:42
  174.3 14.9 %collective-permute-start.47 = (bf16[96,3072]{1,0:T(8,128)(2,1)S(1)}, bf16[96,3072]{1,0:T(8,128)(2,1)S(1)}, u32[]{:S(2)}, u32[]{:S(2)}) collective-permute-start(bf16[96,3072]{1,0:T(8,128)(2,1)S(1)} %pad_maximum_fusion.3), channel_id=1, source_target_pairs={{0,2},{1,3},{6,4},{7,5},{8,10},{9,11},{14,12},{15,13},{16,18},{17,... | collective-permute-start | bytes 1769480 | tf_op jit(solution)/shard_map/ppermute | solution.py:215
  177.7 15.5 %collective-permute-start.48 = (bf16[384,768]{1,0:T(8,128)(2,1)S(1)}, bf16[384,768]{1,0:T(8,128)(2,1)S(1)}, u32[]{:S(2)}, u32[]{:S(2)}) collective-permute-start(bf16[384,768]{1,0:T(8,128)(2,1)S(1)} %add_convert_fusion.2), channel_id=1, source_target_pairs={{2,0},{3,1},{4,6},{5,7},{10,8},{11,9},{12,14},{13,15},{18,16},{19,... | collective-permute-start | bytes 1769480 | tf_op jit(solution)/shard_map/ppermute | solution.py:215
  193.3 18.3 %collective-permute-start.51 = (bf16[96,3072]{1,0:T(8,128)(2,1)S(1)}, bf16[96,3072]{1,0:T(8,128)(2,1)S(1)}, u32[]{:S(2)}, u32[]{:S(2)}) collective-permute-start(bf16[96,3072]{1,0:T(8,128)(2,1)S(1)} %add_convert_fusion.1), channel_id=1, source_target_pairs={{2,4},{3,5},{4,2},{5,3},{10,12},{11,13},{12,10},{13,11},{18,20},{1... | collective-permute-start | bytes 1769480 | tf_op jit(solution)/shard_map/ppermute | solution.py:215
  195.4 16.2 %collective-permute-start.50 = (bf16[96,1536]{1,0:T(8,128)(2,1)S(1)}, bf16[96,1536]{1,0:T(8,128)(2,1)}, u32[]{:S(2)}, u32[]{:S(2)}) collective-permute-start(bf16[96,1536]{1,0:T(8,128)(2,1)S(1)} %get-tuple-element.233), channel_id=1, source_target_pairs={{0,2},{1,3},{6,4},{7,5},{8,10},{9,11},{14,12},{15,13},{16,18},{17,... | collective-permute-start | bytes 884744 | tf_op jit(solution)/shard_map/ppermute | solution.py:215
  199.2 12.4 %collective-permute-start.49 = (bf16[96,1536]{1,0:T(8,128)(2,1)S(1)}, bf16[96,1536]{1,0:T(8,128)(2,1)}, u32[]{:S(2)}, u32[]{:S(2)}) collective-permute-start(bf16[96,1536]{1,0:T(8,128)(2,1)S(1)} %get-tuple-element.234), channel_id=1, source_target_pairs={{0,2},{1,3},{6,4},{7,5},{8,10},{9,11},{14,12},{15,13},{16,18},{17,... | collective-permute-start | bytes 884744 | tf_op jit(solution)/shard_map/ppermute | solution.py:215
  208.8 10.9 %collective-permute-start.69 = (bf16[384,768]{1,0:T(8,128)(2,1)S(1)}, bf16[384,768]{1,0:T(8,128)(2,1)S(1)}, u32[]{:S(2)}, u32[]{:S(2)}) collective-permute-start(bf16[384,768]{1,0:T(8,128)(2,1)S(1)} %broadcast_select_fusion), channel_id=1, source_target_pairs={{0,1},{1,0},{2,3},{3,2},{4,5},{5,4},{6,7},{7,6},{8,9},{9,8},{10,11... | collective-permute-start | bytes 1769480 | tf_op jit(solution)/shard_map/ppermute | solution.py:42
  215.2 14.9 %collective-permute-start.57 = (bf16[96,3072]{1,0:T(8,128)(2,1)S(1)}, bf16[96,3072]{1,0:T(8,128)(2,1)S(1)}, u32[]{:S(2)}, u32[]{:S(2)}) collective-permute-start(bf16[96,3072]{1,0:T(8,128)(2,1)S(1)} %add_convert_fusion), channel_id=1, source_target_pairs={{2,0},{3,1},{4,6},{5,7},{10,8},{11,9},{12,14},{13,15},{18,16},{19,... | collective-permute-start | bytes 1769480 | tf_op jit(solution)/shard_map/ppermute | solution.py:215
  234.3 13.3 %collective-permute-start.59 = (bf16[96,1536]{1,0:T(8,128)(2,1)S(1)}, bf16[96,1536]{1,0:T(8,128)(2,1)S(1)}, u32[]{:S(2)}, u32[]{:S(2)}) collective-permute-start(bf16[96,1536]{1,0:T(8,128)(2,1)S(1)} %add_convert_fusion.10), channel_id=1, source_target_pairs={{2,0},{3,1},{4,6},{5,7},{10,8},{11,9},{12,14},{13,15},{18,16},{19,... | collective-permute-start | bytes 884744 | tf_op jit(solution)/shard_map/ppermute | solution.py:215
  235.7 20.8 %collective-permute-start.68 = (bf16[96,3072]{1,0:T(8,128)(2,1)S(1)}, bf16[96,3072]{1,0:T(8,128)(2,1)S(1)}, u32[]{:S(2)}, u32[]{:S(2)}) collective-permute-start(bf16[96,3072]{1,0:T(8,128)(2,1)S(1)} %broadcast_select_fusion.1), channel_id=1, source_target_pairs={{0,1},{1,0},{2,3},{3,2},{4,5},{5,4},{6,7},{7,6},{8,9},{9,8},{10,11... | collective-permute-start | bytes 1769480 | tf_op jit(solution)/shard_map/ppermute | solution.py:42
  (84 other events, 558.6 us)

commit v3 on v2

--- a/solution.py
+++ b/solution.py
@@ -926,7 +926,7 @@
         step = 0
         while step < share_steps:
             moving = [(share, "replica", replicas >> (step + 1))]
-            half = shards >> (step + 1)
+            half = shards >> step if step else 0
             if half:
                 moving += [(rows[half + at], "shard", half) for at in range(half)]
             got = yield moving
@@ -934,8 +934,8 @@
             for at in range(half):
                 rows[at] = rows[at] + got[1 + at]
             step += 1
-        while shards >> (step + 1):
-            half = shards >> (step + 1)
+        while shards >> step:
+            half = shards >> step
             got = yield [(rows[half + at], "shard", half) for at in range(half)]
             for at in range(half):
                 rows[at] = rows[at] + got[at]
@@ -951,13 +951,17 @@
     chain = mod_chain()
     moves = list(next(chain))
     lanes = {red_qkvo: 0, red_fc1: 1, red_fc2: min(3, steps)}
+    totals = []
     while chain or min(lanes.values()) < steps:
         moving = [lane for lane in lanes if lanes[lane] < steps]
         groups = [lane.fold(lanes[lane]) for lane in moving]
-        groups = together(*groups, send_on(moves))
+        *groups, totals = together(*groups, send_on(moves), totals)
         for lane, got in zip(moving, groups):
             lane.folded(lanes[lane], got)
             lanes[lane] += 1
+        if moving and min(lanes.values()) == steps:
+            whole = red_qkvo.finish()
+            totals = [whole[:, : 3 * width], whole[:, 3 * width :]]
         moves = []
         if chain:
             try:
@@ -981,16 +985,15 @@
 
     total_fc2 = red_fc2.finish()
     total_fc1 = red_fc1.finish()
-    total_qkvo = red_qkvo.finish()
     return (
         mixed,
         grad_tokens,
         grad_cond,
         total_mod,
         total_b_mod,
-        total_qkvo[:, : 3 * width],
+        totals[0],
         bias_totals[0],
-        total_qkvo[:, 3 * width :],
+        totals[1],
         bias_totals[1],
         total_fc1,
         bias_totals[2],

time: 264 us -> 262 us (level)
  waiting for transfers between devices: 73.7 us -> 70.3 us
  transfers between devices with their start and end apart: 70 -> 70, of which waited for: 28 -> 29; matrix products, arithmetic and copies ran while one was open for 11% -> 11% of each run, Pallas kernels for 25% -> 26%
where the time goes in v3:
time: 262 us; the launch traced here: 261 us
  starting transfers between devices  70.4 us (27%)
  Pallas kernels  70.4 us (27%)
  waiting for transfers between devices  70.3 us (27%)
  other arithmetic  30.2 us (12%)
  local copies, waits for them, and re-layouts  17.1 us (7%)
    pallas_call x9, Pallas kernels, call(): pl.pallas_call(functools.partial(kernel, shards), out_shape=outs + outsid...  70.4 us
    ppermute x58, waiting for transfers between devices, hop(): return lax.ppermute(value, axis, [(at, at ^ flip) for at in range(size)])  49.8 us
    ppermute x58, starting transfers between devices, hop(): return lax.ppermute(value, axis, [(at, at ^ flip) for at in range(size)])  48.6 us
    ppermute x12, starting transfers between devices, fold(): lax.ppermute(value, 'replica', pairs)  21.7 us
    ppermute x12, waiting for transfers between devices, fold(): lax.ppermute(value, 'replica', pairs)  20.4 us
    convert_element_type x9, other arithmetic, ready(): self.sent = [self.total(at, stage).astype(BF16) for at in range(self.parts)]  11.8 us
    unnamed x96, local copies, waits for them, and re-layouts  6.34 us
  transfers between devices with their start and end apart: 70, of which 29 were waited for; matrix products, arithmetic and copies ran while one was open for 11% of the time, Pallas kernels for 26%

profile of v3, /device:TPU:0, one launch (start us, length us, event | category | flops | bytes accessed | tf_op | source)
XLA Modules:
  0.0 261.0 jit_solution(5697589264371150297)
XLA Ops:
  2.8 3.0 %collective-permute-start.1 = (bf16[96,3072]{1,0:T(8,128)(2,1)S(1)}, bf16[96,3072]{1,0:T(8,128)(2,1)S(1)}, u32[]{:S(2)}, u32[]{:S(2)}) collective-permute-start(bf16[96,3072]{1,0:T(8,128)(2,1)S(1)} %pad_maximum_fusion.1), channel_id=1, source_target_pairs={{0,16},{8,24},{16,0},{24,8},{1,17},{9,25},{17,1},{25,9},{2,18},{10... | collective-permute-start | bytes 1769480 | tf_op jit(solution)/shard_map/ppermute | solution.py:42
  8.2 1.9 collective-permute-start.3
  14.7 6.1 %collective-permute-done.4 = bf16[1,2304]{1,0:T(2,128)(2,1)} collective-permute-done((bf16[1,2304]{1,0:T(2,128)(2,1)S(1)}, bf16[1,2304]{1,0:T(2,128)(2,1)}, u32[]{:S(2)}, u32[]{:S(2)}) %collective-permute-start.4) | collective-permute-done | bytes 4640 | tf_op jit(solution)/shard_map/ppermute | solution.py:42
  39.7 9.9 %shard_map.228 = (bf16[256,768]{1,0:T(8,128)(2,1)}, bf16[256,2304]{1,0:T(8,128)(2,1)}, bf16[256,768]{1,0:T(8,128)(2,1)}, f32[256,128]{1,0:T(8,128)}, f32[256,768...) custom-call(bf16[256,768]{1,0:T(8,128)(2,1)} %refs_1_.7, f32[1,4608]{1,0:T(1,128)} %fusion.9.refs_1_.refs_2_, ...), custom_call_target="tpu_custom_call" | custom-call | flops 99999997952 | bytes 9202688 | tf_op jit(solution)/shard_map/pallas_call | solution.py:645
  57.9 4.4 %collective-permute-done.17.refs_8_.refs_9_ = bf16[96,1536]{1,0:T(8,128)(2,1)S(1)} collective-permute-done((bf16[96,1536]{1,0:T(8,128)(2,1)S(1)}, bf16[96,1536]{1,0:T(8,128)(2,1)S(1)}, u32[]{:S(2)}, u32[]{:S(2)}) %collective-permute-start.17) | collective-permute-done | bytes 294944 | tf_op jit(solution)/shard_map/ppermute | solution.py:42
  62.3 1.9 collective-permute-done.16.refs_7_.refs_8_
  68.4 11.3 %shard_map.229 = (bf16[256,3072]{1,0:T(8,128)(2,1)}, f32[256,3072]{1,0:T(8,128)}, bf16[4,384,768]{2,1,0:T(8,128)(2,1)}, bf16[4,384,768]{2,1,0:T(8,128)(2,1)}) custom-call(bf16[256,768]{1,0:T(8,128)(2,1)} %get-tuple-element.141.refs_0_, bf16[256,768]{1,0:T(8,128)(2,1)} %refs_3_.1, f32[1,4608]{1,0:T(1,128)} %fusion.9.refs_1_.refs_2_, f32[1,3072]{1,0:T(1,128)} %bitcast.117, ...), custom_call_target="tpu_custom_call" | custom-call | flops 99999997952 | bytes 14972928 | tf_op jit(solution)/shard_map/pallas_call | solution.py:645
  84.7 6.3 %collective-permute-done.27.refs_7_.refs_13_ = bf16[384,384]{1,0:T(8,128)(2,1)S(1)} collective-permute-done((bf16[384,384]{1,0:T(8,128)(2,1)S(1)}, bf16[384,384]{1,0:T(8,128)(2,1)S(1)}, u32[]{:S(2)}, u32[]{:S(2)}) %collective-permute-start.27) | collective-permute-done | bytes 294944 | tf_op jit(solution)/shard_map/ppermute | solution.py:42
  98.2 9.8 %shard_map.230 = (bf16[256,3072]{1,0:T(8,128)(2,1)}, f32[1,3072]{1,0:T(1,128)}, bf16[4,96,3072]{2,1,0:T(8,128)(2,1)}, bf16[4,96,3072]{2,1,0:T(8,128)(2,1)}) custom-call(bf16[256,768]{1,0:T(8,128)(2,1)} %get-tuple-element.141.refs_0_, bf16[256,768]{1,0:T(8,128)(2,1)} %refs_3_.1, f32[1,4608]{1,0:T(1,128)} %fusion.9.refs_1_.refs_2_, ...), custom_call_target="tpu_custom_call" | custom-call | flops 99999997952 | bytes 14972928 | tf_op jit(solution)/shard_map/pallas_call | solution.py:645
  108.0 2.0 collective-permute-done.25
  114.5 7.6 %shard_map.231 = (f32[256,768]{1,0:T(8,128)}, bf16[256,768]{1,0:T(8,128)(2,1)}, f32[1,768]{1,0:T(1,128)}, f32[3,768]{1,0:T(4,128)}) custom-call(bf16[256,3072]{1,0:T(8,128)(2,1)} %get-tuple-element.160.refs_0_, bf16[256,768]{1,0:T(8,128)(2,1)} %refs_3_.1, f32[1,4608]{1,0:T(1,128)} %fusion.9.refs_1_.refs_2_, f32[256,768]{1,0:T(8,128)} %get-tuple-element.143.refs_3_.refs_2_, ...), custom_call_target="tpu_custom_call" | custom-call | flops 99999997952 | bytes 9467904 | tf_op jit(solution)/shard_map/pallas_call | solution.py:645
  126.0 4.3 %collective-permute-start.36 = (bf16[384,768]{1,0:T(8,128)(2,1)S(1)}, bf16[384,768]{1,0:T(8,128)(2,1)}, u32[]{:S(2)}, u32[]{:S(2)}) collective-permute-start(bf16[384,768]{1,0:T(8,128)(2,1)S(1)} %pad_maximum_fusion.2), channel_id=1, source_target_pairs={{0,2},{1,3},{6,4},{7,5},{8,10},{9,11},{14,12},{15,13},{16,18},{17,... | collective-permute-start | bytes 1769480 | tf_op jit(solution)/shard_map/ppermute | solution.py:215
  131.8 12.8 %shard_map.232 = (bf16[256,2304]{1,0:T(8,128)(2,1)}, f32[1,2304]{1,0:T(1,128)}, bf16[4,96,3072]{2,1,0:T(8,128)(2,1)}, bf16[4,96,3072]{2,1,0:T(8,128)(2,1)}) custom-call(bf16[256,768]{1,0:T(8,128)(2,1)} %get-tuple-element.168.refs_0_, bf16[256,768]{1,0:T(8,128)(2,1)} %get-tuple-element.169.refs_1_, bf16[256,2304]{1,0:T(8,128)(2,1)} %get-tuple-element.170.refs_2_, ...), custom_call_target="tpu_custom_call" | custom-call | flops 99999997952 | bytes 13116416 | tf_op jit(solution)/shard_map/pallas_call | solution.py:645
  147.0 2.3 add_convert_fusion.20
  155.0 2.0 add_convert_fusion.5
  158.6 6.2 %shard_map.233 = (f32[256,768]{1,0:T(8,128)}, f32[2,768]{1,0:T(2,128)}) custom-call(bf16[256,2304]{1,0:T(8,128)(2,1)} %get-tuple-element.182.refs_0_, bf16[256,768]{1,0:T(8,128)(2,1)} %refs_1_.7, f32[1,4608]{1,0:T(1,128)} %fusion.9.refs_1_.refs_2_, f32[256,768]{1,0:T(8,128)} %get-tuple-element.183.refs_3_, bf16[192,2304]{1,0:T(8,128)(2,1)} %refs_4_.8, ...), custom_call_target="tpu_custom_call" | custom-call | flops 99999997952 | bytes 7888896 | tf_op jit(solution)/shard_map/pallas_call | solution.py:645
  164.8 7.6 %collective-permute-done.40 = bf16[2,96,1536]{2,1,0:T(8,128)(2,1)S(1)} collective-permute-done((bf16[2,96,1536]{2,1,0:T(8,128)(2,1)}, bf16[2,96,1536]{2,1,0:T(8,128)(2,1)S(1)}, u32[]{:S(2)}, u32[]{:S(2)}) %collective-permute-start.40) | collective-permute-done | bytes 589856 | tf_op jit(solution)/shard_map/ppermute | solution.py:42
  174.3 3.4 %collective-permute-start.47 = (bf16[96,3072]{1,0:T(8,128)(2,1)S(1)}, bf16[96,3072]{1,0:T(8,128)(2,1)S(1)}, u32[]{:S(2)}, u32[]{:S(2)}) collective-permute-start(bf16[96,3072]{1,0:T(8,128)(2,1)S(1)} %pad_maximum_fusion.3), channel_id=1, source_target_pairs={{0,2},{1,3},{6,4},{7,5},{8,10},{9,11},{14,12},{15,13},{16,18},{17,... | collective-permute-start | bytes 1769480 | tf_op jit(solution)/shard_map/ppermute | solution.py:215
  182.8 6.4 %shard_map.234 = (bf16[256,768]{1,0:T(8,128)(2,1)}, bf16[1,10752]{1,0:T(2,128)(2,1)}) custom-call(bf16[256,3072]{1,0:T(8,128)(2,1)} %get-tuple-element.142.refs_0_, f32[1,4608]{1,0:T(1,128)} %fusion.9.refs_1_.refs_2_, f32[256,768]{1,0:T(8,128)} %get-tuple-element.143.refs_3_.refs_2_, bf16[256,768]{1,0:T(8,128)(2,1)} %refs_3_.1, f32[1,768]{1,0:T(1,128)} %reshape.202.refs_4_, ...), custom_call_target="tpu_custom_call" | custom-call | flops 99999997952 | bytes 7947264 | tf_op jit(solution)/shard_map/pallas_call | solution.py:645
  189.2 4.0 %collective-permute-done.48 = bf16[384,768]{1,0:T(8,128)(2,1)S(1)} collective-permute-done((bf16[384,768]{1,0:T(8,128)(2,1)S(1)}, bf16[384,768]{1,0:T(8,128)(2,1)S(1)}, u32[]{:S(2)}, u32[]{:S(2)}) %collective-permute-start.48) | collective-permute-done | bytes 589856 | tf_op jit(solution)/shard_map/ppermute | solution.py:215
  195.4 3.8 %collective-permute-start.50 = (bf16[96,1536]{1,0:T(8,128)(2,1)S(1)}, bf16[96,1536]{1,0:T(8,128)(2,1)}, u32[]{:S(2)}, u32[]{:S(2)}) collective-permute-start(bf16[96,1536]{1,0:T(8,128)(2,1)S(1)} %get-tuple-element.243), channel_id=1, source_target_pairs={{0,2},{1,3},{6,4},{7,5},{8,10},{9,11},{14,12},{15,13},{16,18},{17,... | collective-permute-start | bytes 884744 | tf_op jit(solution)/shard_map/ppermute | solution.py:215
  199.2 2.0 collective-permute-start.49
  201.2 1.9 collective-permute-start.54
  204.1 2.6 %collective-permute-done.54.refs_3_ = bf16[1,10752]{1,0:T(2,128)(2,1)S(1)} collective-permute-done((bf16[1,10752]{1,0:T(2,128)(2,1)}, bf16[1,10752]{1,0:T(2,128)(2,1)S(1)}, u32[]{:S(2)}, u32[]{:S(2)}) %collective-permute-start.54) | collective-permute-done | bytes 21536 | tf_op jit(solution)/shard_map/ppermute | solution.py:42
  208.8 2.7 %collective-permute-done.52.refs_1_ = bf16[1,10752]{1,0:T(2,128)(2,1)S(1)} collective-permute-done((bf16[1,10752]{1,0:T(2,128)(2,1)}, bf16[1,10752]{1,0:T(2,128)(2,1)S(1)}, u32[]{:S(2)}, u32[]{:S(2)}) %collective-permute-start.52) | collective-permute-done | bytes 21536 | tf_op jit(solution)/shard_map/ppermute | solution.py:42
  216.8 2.9 %shard_map.235 = (f32[1,768]{1,0:T(1,128)}, f32[1,768]{1,0:T(1,128)}, f32[1,768]{1,0:T(1,128)}, f32[1,768]{1,0:T(1,128)}, bf16[1,8,4864]{2,1,0:T(8,128)(2,1)}) custom-call(bf16[1,10752]{1,0:T(2,128)(2,1)} %get-tuple-element.202.refs_0_, bf16[1,10752]{1,0:T(2,128)(2,1)} %copy-done.43, bf16[1,10752]{1,0:T(2,128)(2,1)} %copy-done.42, ...), custom_call_target="tpu_custom_call" | custom-call | flops 99999997952 | bytes 1947136 | tf_op jit(solution)/shard_map/pallas_call | solution.py:645
  221.3 8.9 %collective-permute-done.57 = bf16[96,3072]{1,0:T(8,128)(2,1)S(1)} collective-permute-done((bf16[96,3072]{1,0:T(8,128)(2,1)S(1)}, bf16[96,3072]{1,0:T(8,128)(2,1)S(1)}, u32[]{:S(2)}, u32[]{:S(2)}) %collective-permute-start.57) | collective-permute-done | bytes 589856 | tf_op jit(solution)/shard_map/ppermute | solution.py:215
  230.4 1.8 collective-permute-start.60
  237.0 4.3 %collective-permute-done.58 = bf16[96,1536]{1,0:T(8,128)(2,1)S(1)} collective-permute-done((bf16[96,1536]{1,0:T(8,128)(2,1)S(1)}, bf16[96,1536]{1,0:T(8,128)(2,1)S(1)}, u32[]{:S(2)}, u32[]{:S(2)}) %collective-permute-start.58) | collective-permute-done | bytes 294944 | tf_op jit(solution)/shard_map/ppermute | solution.py:215
  241.3 3.2 %collective-permute-done.59 = bf16[96,1536]{1,0:T(8,128)(2,1)S(1)} collective-permute-done((bf16[96,1536]{1,0:T(8,128)(2,1)S(1)}, bf16[96,1536]{1,0:T(8,128)(2,1)S(1)}, u32[]{:S(2)}, u32[]{:S(2)}) %collective-permute-start.59) | collective-permute-done | bytes 294944 | tf_op jit(solution)/shard_map/ppermute | solution.py:215
  249.2 3.1 %collective-permute-done.61 = bf16[2,8,4864]{2,1,0:T(8,128)(2,1)S(1)} collective-permute-done((bf16[2,8,4864]{2,1,0:T(8,128)(2,1)S(1)}, bf16[2,8,4864]{2,1,0:T(8,128)(2,1)S(1)}, u32[]{:S(2)}, u32[]{:S(2)}) %collective-permute-start.61) | collective-permute-done | bytes 155680 | tf_op jit(solution)/shard_map/ppermute | solution.py:42
  256.8 3.5 %shard_map.236 = (f32[192,4608]{1,0:T(8,128)}, f32[1152]{0:T(1024)}, f32[384]{0:T(512)}, f32[192]{0:T(256)}, f32[768]{0:T(1024)}, /*index=5*/f32[192]{0:T(256)}) custom-call(bf16[8,8,4864]{2,1,0:T(8,128)(2,1)} %pad_maximum_fusion.refs_0_), custom_call_target="tpu_custom_call" | custom-call | flops 100000000 | bytes 4172288 | tf_op jit(solution)/shard_map/pallas_call | solution.py:645
  (285 shorter events, 105.3 us)
Async XLA Ops:
  2.8 18.3 %collective-permute-start.1 = (bf16[96,3072]{1,0:T(8,128)(2,1)S(1)}, bf16[96,3072]{1,0:T(8,128)(2,1)S(1)}, u32[]{:S(2)}, u32[]{:S(2)}) collective-permute-start(bf16[96,3072]{1,0:T(8,128)(2,1)S(1)} %pad_maximum_fusion.1), channel_id=1, source_target_pairs={{0,16},{8,24},{16,0},{24,8},{1,17},{9,25},{17,1},{25,9},{2,18},{10... | collective-permute-start | bytes 1769480 | tf_op jit(solution)/shard_map/ppermute | solution.py:42
  5.8 15.3 %collective-permute-start = (bf16[96,3072]{1,0:T(8,128)(2,1)S(1)}, bf16[96,3072]{1,0:T(8,128)(2,1)}, u32[]{:S(2)}, u32[]{:S(2)}) collective-permute-start(bf16[96,3072]{1,0:T(8,128)(2,1)S(1)} %pad_maximum_fusion.1), channel_id=1, source_target_pairs={{0,8},{8,0},{16,24},{24,16},{1,9},{9,1},{17,25},{25,17},{2,10},{10... | collective-permute-start | bytes 1769480 | tf_op jit(solution)/shard_map/ppermute | solution.py:42
  8.0 12.8 %collective-permute-start.4 = (bf16[1,2304]{1,0:T(2,128)(2,1)S(1)}, bf16[1,2304]{1,0:T(2,128)(2,1)}, u32[]{:S(2)}, u32[]{:S(2)}) collective-permute-start(bf16[1,2304]{1,0:T(2,128)(2,1)S(1)} %broadcast_in_dim.2), channel_id=1, source_target_pairs={{0,24},{8,16},{16,8},{24,0},{1,25},{9,17},{17,9},{25,1},{2,26},{10... | collective-permute-start | bytes 13832 | tf_op jit(solution)/shard_map/ppermute | solution.py:42
  8.2 12.7 %collective-permute-start.3 = (bf16[1,2304]{1,0:T(2,128)(2,1)S(1)}, bf16[1,2304]{1,0:T(2,128)(2,1)}, u32[]{:S(2)}, u32[]{:S(2)}) collective-permute-start(bf16[1,2304]{1,0:T(2,128)(2,1)S(1)} %broadcast_in_dim.2), channel_id=1, source_target_pairs={{0,16},{8,24},{16,0},{24,8},{1,17},{9,25},{17,1},{25,9},{2,18},{10... | collective-permute-start | bytes 13832 | tf_op jit(solution)/shard_map/ppermute | solution.py:42
  10.1 11.0 %collective-permute-start.2 = (bf16[1,2304]{1,0:T(2,128)(2,1)S(1)}, bf16[1,2304]{1,0:T(2,128)(2,1)}, u32[]{:S(2)}, u32[]{:S(2)}) collective-permute-start(bf16[1,2304]{1,0:T(2,128)(2,1)S(1)} %broadcast_in_dim.2), channel_id=1, source_target_pairs={{0,8},{8,0},{16,24},{24,16},{1,9},{9,1},{17,25},{25,17},{2,10},{10... | collective-permute-start | bytes 13832 | tf_op jit(solution)/shard_map/ppermute | solution.py:42
  35.6 15.8 %collective-permute-start.8 = (bf16[96,3072]{1,0:T(8,128)(2,1)S(1)}, bf16[96,3072]{1,0:T(8,128)(2,1)}, u32[]{:S(2)}, u32[]{:S(2)}) collective-permute-start(bf16[96,3072]{1,0:T(8,128)(2,1)S(1)} %constant_dynamic-slice_fusion.4), channel_id=1, source_target_pairs={{0,16},{8,24},{16,0},{24,8},{1,17},{9,25},{17,1},{25,9},{2,18},{10... | collective-permute-start | bytes 1769480 | tf_op jit(solution)/shard_map/ppermute | solution.py:42
  37.1 15.7 %collective-permute-start.7 = (bf16[96,3072]{1,0:T(8,128)(2,1)S(1)}, bf16[96,3072]{1,0:T(8,128)(2,1)}, u32[]{:S(2)}, u32[]{:S(2)}) collective-permute-start(bf16[96,3072]{1,0:T(8,128)(2,1)S(1)} %constant_dynamic-slice_fusion.4), channel_id=1, source_target_pairs={{0,8},{8,0},{16,24},{24,16},{1,9},{9,1},{17,25},{25,17},{2,10},{10... | collective-permute-start | bytes 1769480 | tf_op jit(solution)/shard_map/ppermute | solution.py:42
  64.9 15.7 %collective-permute-start.23 = (bf16[384,768]{1,0:T(8,128)(2,1)S(1)}, bf16[384,768]{1,0:T(8,128)(2,1)S(1)}, u32[]{:S(2)}, u32[]{:S(2)}) collective-permute-start(bf16[384,768]{1,0:T(8,128)(2,1)S(1)} %constant_dynamic-slice_fusion), channel_id=1, source_target_pairs={{0,16},{8,24},{16,0},{24,8},{1,17},{9,25},{17,1},{25,9},{2,18},{10... | collective-permute-start | bytes 1769480 | tf_op jit(solution)/shard_map/ppermute | solution.py:42
  66.0 15.5 %collective-permute-start.22 = (bf16[384,768]{1,0:T(8,128)(2,1)S(1)}, bf16[384,768]{1,0:T(8,128)(2,1)S(1)}, u32[]{:S(2)}, u32[]{:S(2)}) collective-permute-start(bf16[384,768]{1,0:T(8,128)(2,1)S(1)} %constant_dynamic-slice_fusion), channel_id=1, source_target_pairs={{0,8},{8,0},{16,24},{24,16},{1,9},{9,1},{17,25},{25,17},{2,10},{10... | collective-permute-start | bytes 1769480 | tf_op jit(solution)/shard_map/ppermute | solution.py:42
  84.2 12.4 %collective-permute-start.29 = (bf16[384,768]{1,0:T(8,128)(2,1)S(1)}, bf16[384,768]{1,0:T(8,128)(2,1)S(1)}, u32[]{:S(2)}, u32[]{:S(2)}) collective-permute-start(bf16[384,768]{1,0:T(8,128)(2,1)S(1)} %collective-permute-done.22.refs_5_.refs_11_), channel_id=1, source_target_pairs={{0,1},{1,0},{2,3},{3,2},{4,5},{5,4},{6,7},{7,6},{8,9},{9,8},{10,11... | collective-permute-start | bytes 1769480 | tf_op jit(solution)/shard_map/ppermute | solution.py:42
  84.2 14.0 %collective-permute-start.30 = (bf16[384,768]{1,0:T(8,128)(2,1)S(1)}, bf16[384,768]{1,0:T(8,128)(2,1)}, u32[]{:S(2)}, u32[]{:S(2)}) collective-permute-start(bf16[384,768]{1,0:T(8,128)(2,1)S(1)} %collective-permute-done.23.refs_6_.refs_12_), channel_id=1, source_target_pairs={{0,1},{1,0},{2,3},{3,2},{4,5},{5,4},{6,7},{7,6},{8,9},{9,8},{10,11... | collective-permute-start | bytes 1769480 | tf_op jit(solution)/shard_map/ppermute | solution.py:42
  94.2 15.7 %collective-permute-start.25 = (bf16[2,384,384]{2,1,0:T(8,128)(2,1)S(1)}, bf16[2,384,384]{2,1,0:T(8,128)(2,1)S(1)}, u32[]{:S(2)}, u32[]{:S(2)}) collective-permute-start(bf16[2,384,384]{2,1,0:T(8,128)(2,1)S(1)} %bitcast.110), channel_id=1, source_target_pairs={{0,8},{8,0},{16,24},{24,16},{1,9},{9,1},{17,25},{25,17},{2,10},{10... | collective-permute-start | bytes 1769480 | tf_op jit(solution)/shard_map/ppermute | solution.py:42
  95.6 15.3 %collective-permute-start.26 = (bf16[2,384,384]{2,1,0:T(8,128)(2,1)S(1)}, bf16[2,384,384]{2,1,0:T(8,128)(2,1)S(1)}, u32[]{:S(2)}, u32[]{:S(2)}) collective-permute-start(bf16[2,384,384]{2,1,0:T(8,128)(2,1)S(1)} %bitcast.109), channel_id=1, source_target_pairs={{0,16},{8,24},{16,0},{24,8},{1,17},{9,25},{17,1},{25,9},{2,18},{10... | collective-permute-start | bytes 1769480 | tf_op jit(solution)/shard_map/ppermute | solution.py:42
  126.0 20.3 %collective-permute-start.36 = (bf16[384,768]{1,0:T(8,128)(2,1)S(1)}, bf16[384,768]{1,0:T(8,128)(2,1)}, u32[]{:S(2)}, u32[]{:S(2)}) collective-permute-start(bf16[384,768]{1,0:T(8,128)(2,1)S(1)} %pad_maximum_fusion.2), channel_id=1, source_target_pairs={{0,2},{1,3},{6,4},{7,5},{8,10},{9,11},{14,12},{15,13},{16,18},{17,... | collective-permute-start | bytes 1769480 | tf_op jit(solution)/shard_map/ppermute | solution.py:215
  130.3 15.7 %collective-permute-start.37 = (bf16[2,96,1536]{2,1,0:T(8,128)(2,1)}, bf16[2,96,1536]{2,1,0:T(8,128)(2,1)S(1)}, u32[]{:S(2)}, u32[]{:S(2)}) collective-permute-start(bf16[2,96,1536]{2,1,0:T(8,128)(2,1)} %bitcast.14), channel_id=1, source_target_pairs={{0,8},{8,0},{16,24},{24,16},{1,9},{9,1},{17,25},{25,17},{2,10},{10... | collective-permute-start | bytes 1769480 | tf_op jit(solution)/shard_map/ppermute | solution.py:42
  130.8 15.5 %collective-permute-start.38 = (bf16[2,96,1536]{2,1,0:T(8,128)(2,1)}, bf16[2,96,1536]{2,1,0:T(8,128)(2,1)}, u32[]{:S(2)}, u32[]{:S(2)}) collective-permute-start(bf16[2,96,1536]{2,1,0:T(8,128)(2,1)} %bitcast.16), channel_id=1, source_target_pairs={{0,16},{8,24},{16,0},{24,8},{1,17},{9,25},{17,1},{25,9},{2,18},{10... | collective-permute-start | bytes 1769480 | tf_op jit(solution)/shard_map/ppermute | solution.py:42
  149.3 15.5 %collective-permute-start.42 = (bf16[1,96,1536]{2,1,0:T(8,128)(2,1)}, bf16[1,96,1536]{2,1,0:T(8,128)(2,1)}, u32[]{:S(2)}, u32[]{:S(2)}) collective-permute-start(bf16[1,96,1536]{2,1,0:T(8,128)(2,1)} %bitcast.24), channel_id=1, source_target_pairs={{0,16},{8,24},{16,0},{24,8},{1,17},{9,25},{17,1},{25,9},{2,18},{10... | collective-permute-start | bytes 884744 | tf_op jit(solution)/shard_map/ppermute | solution.py:42
  150.3 14.5 %collective-permute-start.43 = (bf16[1,96,1536]{2,1,0:T(8,128)(2,1)}, bf16[1,96,1536]{2,1,0:T(8,128)(2,1)}, u32[]{:S(2)}, u32[]{:S(2)}) collective-permute-start(bf16[1,96,1536]{2,1,0:T(8,128)(2,1)} %bitcast.26), channel_id=1, source_target_pairs={{0,8},{8,0},{16,24},{24,16},{1,9},{9,1},{17,25},{25,17},{2,10},{10... | collective-permute-start | bytes 884744 | tf_op jit(solution)/shard_map/ppermute | solution.py:42
  153.0 11.8 %collective-permute-start.44 = (bf16[384,768]{1,0:T(8,128)(2,1)S(1)}, bf16[384,768]{1,0:T(8,128)(2,1)S(1)}, u32[]{:S(2)}, u32[]{:S(2)}) collective-permute-start(bf16[384,768]{1,0:T(8,128)(2,1)S(1)} %add_convert_fusion.3), channel_id=1, source_target_pairs={{2,4},{3,5},{4,2},{5,3},{10,12},{11,13},{12,10},{13,11},{18,20},{1... | collective-permute-start | bytes 1769480 | tf_op jit(solution)/shard_map/ppermute | solution.py:215
  157.0 15.4 %collective-permute-start.40 = (bf16[2,96,1536]{2,1,0:T(8,128)(2,1)}, bf16[2,96,1536]{2,1,0:T(8,128)(2,1)S(1)}, u32[]{:S(2)}, u32[]{:S(2)}) collective-permute-start(bf16[2,96,1536]{2,1,0:T(8,128)(2,1)} %bitcast.20), channel_id=1, source_target_pairs={{0,8},{8,0},{16,24},{24,16},{1,9},{9,1},{17,25},{25,17},{2,10},{10... | collective-permute-start | bytes 1769480 | tf_op jit(solution)/shard_map/ppermute | solution.py:42
  157.5 14.9 %collective-permute-start.41 = (bf16[2,96,1536]{2,1,0:T(8,128)(2,1)S(1)}, bf16[2,96,1536]{2,1,0:T(8,128)(2,1)S(1)}, u32[]{:S(2)}, u32[]{:S(2)}) collective-permute-start(bf16[2,96,1536]{2,1,0:T(8,128)(2,1)S(1)} %bitcast.108), channel_id=1, source_target_pairs={{0,16},{8,24},{16,0},{24,8},{1,17},{9,25},{17,1},{25,9},{2,18},{10... | collective-permute-start | bytes 1769480 | tf_op jit(solution)/shard_map/ppermute | solution.py:42
  174.3 14.9 %collective-permute-start.47 = (bf16[96,3072]{1,0:T(8,128)(2,1)S(1)}, bf16[96,3072]{1,0:T(8,128)(2,1)S(1)}, u32[]{:S(2)}, u32[]{:S(2)}) collective-permute-start(bf16[96,3072]{1,0:T(8,128)(2,1)S(1)} %pad_maximum_fusion.3), channel_id=1, source_target_pairs={{0,2},{1,3},{6,4},{7,5},{8,10},{9,11},{14,12},{15,13},{16,18},{17,... | collective-permute-start | bytes 1769480 | tf_op jit(solution)/shard_map/ppermute | solution.py:215
  177.7 15.5 %collective-permute-start.48 = (bf16[384,768]{1,0:T(8,128)(2,1)S(1)}, bf16[384,768]{1,0:T(8,128)(2,1)S(1)}, u32[]{:S(2)}, u32[]{:S(2)}) collective-permute-start(bf16[384,768]{1,0:T(8,128)(2,1)S(1)} %add_convert_fusion.2), channel_id=1, source_target_pairs={{2,0},{3,1},{4,6},{5,7},{10,8},{11,9},{12,14},{13,15},{18,16},{19,... | collective-permute-start | bytes 1769480 | tf_op jit(solution)/shard_map/ppermute | solution.py:215
  193.3 18.3 %collective-permute-start.51 = (bf16[96,3072]{1,0:T(8,128)(2,1)S(1)}, bf16[96,3072]{1,0:T(8,128)(2,1)S(1)}, u32[]{:S(2)}, u32[]{:S(2)}) collective-permute-start(bf16[96,3072]{1,0:T(8,128)(2,1)S(1)} %add_convert_fusion.1), channel_id=1, source_target_pairs={{2,4},{3,5},{4,2},{5,3},{10,12},{11,13},{12,10},{13,11},{18,20},{1... | collective-permute-start | bytes 1769480 | tf_op jit(solution)/shard_map/ppermute | solution.py:215
  195.4 16.2 %collective-permute-start.50 = (bf16[96,1536]{1,0:T(8,128)(2,1)S(1)}, bf16[96,1536]{1,0:T(8,128)(2,1)}, u32[]{:S(2)}, u32[]{:S(2)}) collective-permute-start(bf16[96,1536]{1,0:T(8,128)(2,1)S(1)} %get-tuple-element.243), channel_id=1, source_target_pairs={{0,2},{1,3},{6,4},{7,5},{8,10},{9,11},{14,12},{15,13},{16,18},{17,... | collective-permute-start | bytes 884744 | tf_op jit(solution)/shard_map/ppermute | solution.py:215
  199.2 12.4 %collective-permute-start.49 = (bf16[96,1536]{1,0:T(8,128)(2,1)S(1)}, bf16[96,1536]{1,0:T(8,128)(2,1)}, u32[]{:S(2)}, u32[]{:S(2)}) collective-permute-start(bf16[96,1536]{1,0:T(8,128)(2,1)S(1)} %get-tuple-element.244), channel_id=1, source_target_pairs={{0,2},{1,3},{6,4},{7,5},{8,10},{9,11},{14,12},{15,13},{16,18},{17,... | collective-permute-start | bytes 884744 | tf_op jit(solution)/shard_map/ppermute | solution.py:215
  208.8 10.9 %collective-permute-start.69 = (bf16[384,768]{1,0:T(8,128)(2,1)S(1)}, bf16[384,768]{1,0:T(8,128)(2,1)S(1)}, u32[]{:S(2)}, u32[]{:S(2)}) collective-permute-start(bf16[384,768]{1,0:T(8,128)(2,1)S(1)} %broadcast_select_fusion), channel_id=1, source_target_pairs={{0,1},{1,0},{2,3},{3,2},{4,5},{5,4},{6,7},{7,6},{8,9},{9,8},{10,11... | collective-permute-start | bytes 1769480 | tf_op jit(solution)/shard_map/ppermute | solution.py:42
  215.2 15.0 %collective-permute-start.57 = (bf16[96,3072]{1,0:T(8,128)(2,1)S(1)}, bf16[96,3072]{1,0:T(8,128)(2,1)S(1)}, u32[]{:S(2)}, u32[]{:S(2)}) collective-permute-start(bf16[96,3072]{1,0:T(8,128)(2,1)S(1)} %add_convert_fusion), channel_id=1, source_target_pairs={{2,0},{3,1},{4,6},{5,7},{10,8},{11,9},{12,14},{13,15},{18,16},{19,... | collective-permute-start | bytes 1769480 | tf_op jit(solution)/shard_map/ppermute | solution.py:215
  233.5 11.0 %collective-permute-start.59 = (bf16[96,1536]{1,0:T(8,128)(2,1)S(1)}, bf16[96,1536]{1,0:T(8,128)(2,1)S(1)}, u32[]{:S(2)}, u32[]{:S(2)}) collective-permute-start(bf16[96,1536]{1,0:T(8,128)(2,1)S(1)} %add_convert_fusion.10), channel_id=1, source_target_pairs={{2,0},{3,1},{4,6},{5,7},{10,8},{11,9},{12,14},{13,15},{18,16},{19,... | collective-permute-start | bytes 884744 | tf_op jit(solution)/shard_map/ppermute | solution.py:215
  234.9 14.3 %collective-permute-start.62 = (f32[1,768]{1,0:T(1,128)S(1)}, f32[1,768]{1,0:T(1,128)S(1)}, u32[]{:S(2)}, u32[]{:S(2)}) collective-permute-start(f32[1,768]{1,0:T(1,128)S(1)} %copy-done.45), channel_id=1, source_target_pairs={{0,16},{8,24},{16,0},{24,8},{1,17},{9,25},{17,1},{25,9},{2,18},{10... | collective-permute-start | bytes 9224 | tf_op jit(solution)/shard_map/ppermute | solution.py:42
  235.9 13.2 %collective-permute-start.63 = (f32[1,768]{1,0:T(1,128)S(1)}, f32[1,768]{1,0:T(1,128)S(1)}, u32[]{:S(2)}, u32[]{:S(2)}) collective-permute-start(f32[1,768]{1,0:T(1,128)S(1)} %copy-done.44), channel_id=1, source_target_pairs={{0,16},{8,24},{16,0},{24,8},{1,17},{9,25},{17,1},{25,9},{2,18},{10... | collective-permute-start | bytes 9224 | tf_op jit(solution)/shard_map/ppermute | solution.py:42
  237.0 16.3 %collective-permute-start.68 = (bf16[96,3072]{1,0:T(8,128)(2,1)S(1)}, bf16[96,3072]{1,0:T(8,128)(2,1)S(1)}, u32[]{:S(2)}, u32[]{:S(2)}) collective-permute-start(bf16[96,3072]{1,0:T(8,128)(2,1)S(1)} %broadcast_select_fusion.1), channel_id=1, source_target_pairs={{0,1},{1,0},{2,3},{3,2},{4,5},{5,4},{6,7},{7,6},{8,9},{9,8},{10,11... | collective-permute-start | bytes 1769480 | tf_op jit(solution)/shard_map/ppermute | solution.py:42
  (84 other events, 500.1 us)
